TPU v7x, 256 devices: a whole 4x4x8 slice. The times are simulated.
256 devices in a mesh: ref: 64 (over z, x, core), voc: 4 (over y).
Axes of the slice: x: 4, y: 4, z: 8, core: 2. Of those that a mesh axis runs over, the one named last changes fastest.
Arguments:
- private_logits: bfloat16 [768, 4, 128256], P('ref', None, 'voc'), may hold values from -16 to 16
- public_logits: bfloat16 [4, 4, 128256], P(None, None, ('voc', 'ref')), may hold values from -250 to 250
- noise: bfloat16 [4, 4, 128256], P(None, None, ('voc', 'ref')), may hold values from -6 to 6
- owner: int32 [768], P('ref'), may hold values from 0 to 3, as said below
- counts: int32 [4], replicated, may hold values from 1 to 192, as said below
- tokens: int32 [4, 4], replicated, may hold values from 0 to 128255
Outputs:
- logprobs: float32 [4, 4, 128256], P(None, None, ('voc', 'ref'))
- target: float32 [4, 4], replicated
Inputs may be any that keep to these rules, and one draw needn't show every extreme that they name: `owner`: each of the 4 texts owns exactly 192 rows. `counts`: the count of a text is at least half of the rows that it owns, rounded up, and at most all of them; some text keeps all of its rows.
All inputs are finite; a program needn't handle non-finite values.
Results may differ from a plain program's by a relative error of at most 0.0003.
Values may be sent and summed in bfloat16 or wider, within the bound.
No kernel may reach another device: no remote copies, remote signals or barrier semaphores. Data moves between devices by JAX's collectives and lax.ppermute only.
A program may use at most 64 MiB of HBM per device.

v0:
```python
import jax
import jax.numpy as jnp
from jax import lax
from jax.sharding import Mesh
from jax.sharding import PartitionSpec as P

REF_VOC = ("ref_0", "ref_1", "ref_2", "voc")
REF = ("ref_0", "ref_1", "ref_2")
VOC_REF = ("voc", "ref_0", "ref_1", "ref_2")


clip_bound = 2.0


def all_in_one(x, axis):
    leaves = jax.tree.leaves(x)
    sequence = sorted(range(len(leaves)), key=lambda k: -leaves[k].size)
    width = (1, *leaves[sequence[0]].shape)[-1]
    lines = [
        jnp.pad(leaves[k].reshape(-1), (0, -leaves[k].size % width)).reshape(-1, width)
        for k in sequence
    ]
    both, at, found = (lax.all_gather(jnp.concatenate(lines), axis), 0, {})
    for k, line in zip(sequence, lines):
        section = both[:, at : at + len(line)].reshape(len(both), -1)
        found[k] = section[:, : leaves[k].size].reshape(-1, *leaves[k].shape)
        at += len(line)
    numbers = iter(range(len(leaves)))
    return jax.tree.map(lambda _: found[next(numbers)], x)


def joined_all(x, axes, combine):
    for axis in axes:
        pieces = all_in_one(x, axis)
        x = jax.tree.map(lambda part: part[0], pieces)
        for k in range(1, lax.axis_size(axis)):
            x = combine(x, jax.tree.map(lambda part: part[k], pieces))
    return x


def from_everyone(x, axis):
    copies = jnp.broadcast_to(x, (lax.axis_size(axis), *x.shape))
    return lax.all_to_all(copies, axis, split_axis=0, concat_axis=0, tiled=True)


def joined_by_halves(pieces, combine):
    while len(jax.tree.leaves(pieces)[0]) > 1:
        pieces = jax.vmap(combine)(*(pieces[side::2] for side in (0, 1)))
    return pieces[0]


def entering(x, axis, combine, identity):
    peers, index = (lax.axis_size(axis), lax.axis_index(axis))
    passed = jnp.arange(peers) < index

    def kept(part, zero, own):
        part = jnp.where(
            passed.reshape(-1, *(1 for _ in own.shape)), part, jnp.asarray(zero, own.dtype)
        )
        return part

    pieces = from_everyone(x, axis)
    return joined_by_halves(kept(pieces, identity, x), combine)


def joined_along(tiles, dim):
    dims = list(tiles.shape[1:])
    dims[dim] *= tiles.shape[0]
    return jnp.moveaxis(tiles, 0, dim).reshape(dims)


def gather_directly(x, axis, dim):
    tiles = from_everyone(x, axis)
    return joined_along(tiles, dim)


def split_up(x, dim, peers):
    before, after = (x.shape[:dim], x.shape[dim + 1 :])
    return jnp.moveaxis(x.reshape(*before, peers, -1, *after), dim, 0)


def sent_and_summed(x, axis, dim):
    peers = lax.axis_size(axis)
    tiles = lax.all_to_all(split_up(x, dim, peers), axis, 0, 0, tiled=True)
    return jnp.sum(tiles, axis=0)


def add_counts(earlier, later):
    return earlier + later


def join_stats(left_stats, right_stats):
    row_peak = jnp.maximum(left_stats[0], right_stats[0])
    row_total = left_stats[1] * jnp.exp(left_stats[0] - row_peak) + right_stats[1] * jnp.exp(
        right_stats[0] - row_peak
    )
    return (row_peak, row_total, left_stats[2] + right_stats[2])


def local_terms(combined, picked_local):
    row_peak = jnp.max(combined, axis=2)
    row_total = jnp.sum(jnp.exp(combined - row_peak[:, :, None]), axis=2)
    return (row_peak, row_total, picked_local)


def wide_stats(combined, picked_local):
    return joined_all(local_terms(combined, picked_local), REF_VOC, join_stats)


def pick_tokens(combined, first_column, tokens):
    column = first_column + jnp.arange(combined.shape[2], dtype=jnp.int32)
    return jnp.sum(jnp.where(column[None, None, :] == tokens[:, :, None], combined, 0.0), axis=2)


def body(private_logits, public_logits, noise, owner, counts, tokens):
    text_count = counts.shape[0]
    labels = jnp.arange(text_count, dtype=jnp.int32)
    chosen = (owner[:, None] == labels[None, :]).astype(jnp.int32)
    offset = entering(jnp.sum(chosen, 0), REF, add_counts, jnp.zeros((text_count,), jnp.int32))
    before = jnp.cumsum(chosen, 0) - chosen
    row_rank = jnp.sum((before + offset[None, :]) * chosen, 1)
    row_limit = jnp.sum(chosen * counts[None, :], 1)
    select = chosen.astype(jnp.float32)
    weight = select * (row_rank < row_limit).astype(jnp.float32)[:, None]
    text_scale = 1.0 / (clip_bound * jnp.sqrt(counts.astype(jnp.float32)))
    matched = jnp.einsum(
        "rt,tpv->rpv",
        select,
        gather_directly(public_logits, REF, 2).astype(jnp.float32),
        precision=lax.Precision.HIGHEST,
    )
    clipped = jnp.clip(private_logits.astype(jnp.float32) - matched, -clip_bound, clip_bound)
    partial_sums = jnp.einsum("rt,rpv->tpv", weight, clipped, precision=lax.Precision.HIGHEST)
    summed = sent_and_summed(partial_sums, REF, 2)
    combined = (
        public_logits.astype(jnp.float32)
        + summed * text_scale[:, None, None]
        + noise.astype(jnp.float32)
    )
    block_width = combined.shape[2]
    first_column = (lax.axis_index("voc") * lax.axis_size(REF) + lax.axis_index(REF)) * block_width
    row_peak, row_total, picked = wide_stats(combined, pick_tokens(combined, first_column, tokens))
    lse = row_peak + jnp.log(row_total)
    logprobs = combined - lse[:, :, None]
    target = picked - lse
    return (logprobs, target)


def solution(mesh):
    finer = Mesh(
        mesh.devices.reshape(8, 4, 2, mesh.shape["voc"]), ("ref_0", "ref_1", "ref_2", "voc")
    )
    placed = (P(REF, None, "voc"), P(None, None, VOC_REF), P(None, None, VOC_REF), P(REF), P(), P())
    return jax.shard_map(
        body, mesh=finer, in_specs=placed, out_specs=(P(None, None, VOC_REF), P()), check_vma=False
    )
```

profile of v0, /device:TPU:1, one launch (start us, length us, event | category | flops | bytes accessed | tf_op | source)
XLA Modules:
  0.0 191.6 jit_solution(4459227304451496546)
XLA Ops:
  0.6 1.0 select_reduce_fusion.1
  1.7 22.2 %all_to_all.19 = s32[64,1,4]{2,1,0:T(1,128)S(1)} all-to-all(s32[64,1,4]{2,1,0:T(1,128)S(1)} %broadcast_in_dim.32), channel_id=1, replica_groups=mesh['ref_0'=8,'ref_1'=4,'ref_2'=2,'voc'=4] {'ref_0','ref_1','ref_2'}, dimensions={0} | all-to-all | bytes 2048 | tf_op jit(solution)/shard_map/all_to_all | solution.py:43
  23.9 2.3 %broadcast_in_dim.34 = bf16[64,4,4,501]{3,2,1,0:T(4,128)(2,1)} broadcast(bf16[4,4,501]{2,1,0:T(4,128)(2,1)} %param.7), dimensions={1,2,3} | broadcast | bytes 1042080 | tf_op jit(solution)/shard_map/broadcast_in_dim | solution.py:42
  26.1 5.6 %all-to-all-start.1 = ((bf16[64,4,4,501]{3,2,1,0:T(4,128)(2,1)}), bf16[64,4,4,501]{3,2,1,0:T(4,128)(2,1)}, u32[]{:S(2)}, u32[]{:S(2)}) async-start(bf16[64,4,4,501]{3,2,1,0:T(4,128)(2,1)} %broadcast_in_dim.34), calls=%async_computation.1 | async-start | bytes 2097152 | tf_op jit(solution)/shard_map/all_to_all | solution.py:43
  31.7 0.7 fusion.74
  32.4 0.2 reduce_window_sum.11
  32.9 0.7 fusion.9
  33.6 26.3 %all-to-all-done.1 = bf16[64,4,4,501]{3,2,1,0:T(4,128)(2,1)} async-done(((bf16[64,4,4,501]{3,2,1,0:T(4,128)(2,1)}), bf16[64,4,4,501]{3,2,1,0:T(4,128)(2,1)}, u32[]{:S(2)}, u32[]{:S(2)}) %all-to-all-start.1) | async-done | bytes 1026080 | tf_op jit(solution)/shard_map/all_to_all | solution.py:43
  59.9 2.8 %copy.228 = bf16[4,4,64,501]{3,2,0,1:T(8,128)(2,1)} copy(bf16[4,4,64,501]{3,1,0,2:T(4,128)(2,1)} %bitcast.4) | data formatting | bytes 2052096 | tf_op jit(solution)/shard_map/reshape | solution.py:69
  62.7 4.0 %reshape.162 = bf16[4,4,32064]{2,0,1:T(4,128)(2,1)} reshape(bf16[4,4,64,501]{3,2,0,1:T(8,128)(2,1)} %copy.228) | data formatting | bytes 2052096 | tf_op jit(solution)/shard_map/reshape | solution.py:69
  66.8 5.8 %fusion = f32[12,4,32064]{2,0,1:T(8,128)S(1)} fusion(bf16[4,4,32064]{2,0,1:T(4,128)(2,1)} %reshape.162, bf16[12,4,32064]{2,1,0:T(4,128)(2,1)S(1)} %copy-done, s32[12]{0:T(128)} %param.9), kind=kOutput, calls=%fused_computation.1 | convolution fusion | flops 78492816 | bytes 10260528 | tf_op jit(solution)/shard_map/rt,tpv->rpv/dot_general | solution.py:126
  72.6 5.2 %fusion.4 = f32[4,4,32064]{2,0,1:T(4,128)} fusion(f32[12,4,32064]{2,0,1:T(8,128)S(1)} %fusion, f32[12]{0:T(128)S(1)} %compare_convert_fusion, s32[12]{0:T(128)S(1)} %copy-done.3), kind=kOutput, calls=%fused_computation.14 | convolution fusion | flops 73875648 | bytes 8208480 | tf_op jit(solution)/shard_map/rt,rpv->tpv/dot_general | solution.py:133
  77.8 3.8 %reshape.140 = f32[4,4,64,501]{3,2,0,1:T(8,128)S(1)} reshape(f32[4,4,32064]{2,0,1:T(4,128)} %fusion.4) | data formatting | bytes 4104192 | tf_op jit(solution)/shard_map/reshape | solution.py:79
  81.6 2.7 %copy.243 = f32[4,4,64,501]{3,0,1,2:T(4,128)} copy(f32[4,4,64,501]{3,2,0,1:T(8,128)S(1)} %reshape.140) | data formatting | bytes 4104192 | tf_op jit(solution)/shard_map/reshape | solution.py:79
  84.3 6.3 %all-to-all-start.2 = ((f32[64,4,4,501]{3,1,2,0:T(4,128)}), f32[64,4,4,501]{3,1,2,0:T(4,128)S(1)}, u32[]{:S(2)}, u32[]{:S(2)}) async-start(f32[64,4,4,501]{3,1,2,0:T(4,128)} %bitcast.410), calls=%async_computation.2 | async-start | bytes 4194304 | tf_op jit(solution)/shard_map/all_to_all | solution.py:84
  90.8 49.6 %all-to-all-done.2 = f32[64,4,4,501]{3,1,2,0:T(4,128)S(1)} async-done(((f32[64,4,4,501]{3,1,2,0:T(4,128)}), f32[64,4,4,501]{3,1,2,0:T(4,128)S(1)}, u32[]{:S(2)}, u32[]{:S(2)}) %all-to-all-start.2) | async-done | bytes 2052128 | tf_op jit(solution)/shard_map/all_to_all | solution.py:84
  140.3 0.4 reduce_sum.57
  140.9 0.2 exponential_reduce_fusion
  141.1 16.9 %all-gather.4 = f32[8,12,4]{1,2,0:T(4,128)S(1)} all-gather(f32[1,12,4]{1,2,0:T(4,128)S(1)} %maximum_bitcast_fusion), channel_id=2, replica_groups=mesh['ref_0'=8,'ref_1'=4,'ref_2'=2,'voc'=4] {'ref_0'}, dimensions={0}, use_global_device_ids=true | all-gather | bytes 1728 | tf_op jit(solution)/shard_map/all_gather | solution.py:23
  160.0 8.1 %all-gather.5 = f32[4,12,4]{1,2,0:T(4,128)S(1)} all-gather(f32[1,12,4]{1,2,0:T(4,128)S(1)} %maximum_bitcast_fusion.1), channel_id=3, replica_groups=mesh['ref_0'=8,'ref_1'=4,'ref_2'=2,'voc'=4] {'ref_1'}, dimensions={0}, use_global_device_ids=true | all-gather | bytes 960 | tf_op jit(solution)/shard_map/all_gather | solution.py:23
  169.2 10.6 %all-gather.6 = f32[2,12,4]{1,2,0:T(4,128)S(1)} all-gather(f32[1,12,4]{1,2,0:T(4,128)S(1)} %maximum_bitcast_fusion.2), channel_id=4, replica_groups=mesh['ref_0'=8,'ref_1'=4,'ref_2'=2,'voc'=4] {'ref_2'}, dimensions={0}, use_global_device_ids=true | all-gather | bytes 576 | tf_op jit(solution)/shard_map/all_gather | solution.py:23
  180.6 8.7 %all-gather.7 = f32[4,12,4]{1,2,0:T(4,128)S(1)} all-gather(f32[1,12,4]{1,2,0:T(4,128)S(1)} %maximum_bitcast_fusion.3), channel_id=5, replica_groups=mesh['ref_0'=8,'ref_1'=4,'ref_2'=2,'voc'=4] {'voc'}, dimensions={0}, use_global_device_ids=true | all-gather | bytes 960 | tf_op jit(solution)/shard_map/all_gather | solution.py:23
  190.2 0.6 bitcast_subtract_fusion
  190.9 0.6 copy.227
  (93 shorter events, 5.5 us)
Async XLA Ops:
  0.6 66.2 %copy-start = (bf16[12,4,32064]{2,1,0:T(4,128)(2,1)S(1)}, bf16[12,4,32064]{2,1,0:T(4,128)(2,1)}, u32[]{:S(2)}) copy-start(bf16[12,4,32064]{2,1,0:T(4,128)(2,1)} %param.6) | copy-start | bytes 9234436
  26.1 33.8 %all-to-all-start.1 = ((bf16[64,4,4,501]{3,2,1,0:T(4,128)(2,1)}), bf16[64,4,4,501]{3,2,1,0:T(4,128)(2,1)}, u32[]{:S(2)}, u32[]{:S(2)}) async-start(bf16[64,4,4,501]{3,2,1,0:T(4,128)(2,1)} %broadcast_in_dim.34), calls=%async_computation.1 | async-start | bytes 2097152 | tf_op jit(solution)/shard_map/all_to_all | solution.py:43
  62.7 9.8 %copy-start.3 = (s32[12]{0:T(128)S(1)}, s32[12]{0:T(128)}, u32[]{:S(2)}) copy-start(s32[12]{0:T(128)} %param.9) | copy-start | bytes 148
  77.8 12.9 %copy-start.4 = (s32[4,4]{1,0:T(4,128)S(1)}, s32[4,4]{1,0:T(4,128)}, u32[]{:S(2)}) copy-start(s32[4,4]{1,0:T(4,128)} %param.11) | copy-start | bytes 196
  77.8 13.0 %copy-start.5 = (s32[4]{0:T(128)S(1)}, s32[4]{0:T(128)}, u32[]{:S(2)}) copy-start(s32[4]{0:T(128)} %param.10) | copy-start | bytes 52
  77.8 62.9 %copy-start.1 = (bf16[4,4,501]{2,1,0:T(4,128)(2,1)S(1)}, bf16[4,4,501]{2,1,0:T(4,128)(2,1)}, u32[]{:S(2)}) copy-start(bf16[4,4,501]{2,1,0:T(4,128)(2,1)} %param.7) | copy-start | bytes 48100
  77.8 62.9 %copy-start.2 = (bf16[4,4,501]{2,1,0:T(4,128)(2,1)S(1)}, bf16[4,4,501]{2,1,0:T(4,128)(2,1)}, u32[]{:S(2)}) copy-start(bf16[4,4,501]{2,1,0:T(4,128)(2,1)} %param.8) | copy-start | bytes 48100
  84.3 56.0 %all-to-all-start.2 = ((f32[64,4,4,501]{3,1,2,0:T(4,128)}), f32[64,4,4,501]{3,1,2,0:T(4,128)S(1)}, u32[]{:S(2)}, u32[]{:S(2)}) async-start(f32[64,4,4,501]{3,1,2,0:T(4,128)} %bitcast.410), calls=%async_computation.2 | async-start | bytes 4194304 | tf_op jit(solution)/shard_map/all_to_all | solution.py:84
where the time goes:
time: 193 us; the launch traced here: 192 us
  waiting for transfers between devices  75.9 us (39%)
  blocking collectives  66.5 us (34%)
  local copies, waits for them, and re-layouts  20.8 us (11%)
  starting transfers between devices  11.9 us (6%)
  matrix products  11 us (6%)
  other arithmetic  4.81 us (2%)
    all_to_all x1, waiting for transfers between devices, sent_and_summed(): tiles = lax.all_to_all(split_up(x, dim, peers), axis, 0, 0, tiled=True)  49.6 us
    all_gather x4, blocking collectives, all_in_one(): both, at, found = (lax.all_gather(jnp.concatenate(lines), axis), 0, {})  44.4 us
    all_to_all x1, waiting for transfers between devices, from_everyone(): return lax.all_to_all(copies, axis, split_axis=0, concat_axis=0, tiled=True)  26.3 us
    all_to_all x1, blocking collectives, from_everyone(): return lax.all_to_all(copies, axis, split_axis=0, concat_axis=0, tiled=True)  22.2 us
    reshape x2, local copies, waits for them, and re-layouts, joined_along(): return jnp.moveaxis(tiles, 0, dim).reshape(dims)  6.88 us
    reshape x2, local copies, waits for them, and re-layouts, split_up(): return jnp.moveaxis(x.reshape(*before, peers, -1, *after), dim, 0)  6.54 us
    all_to_all x1, starting transfers between devices, sent_and_summed(): tiles = lax.all_to_all(split_up(x, dim, peers), axis, 0, 0, tiled=True)  6.3 us
    dot_general x1, matrix products, body(): jnp.einsum('rt,tpv->rpv', select, gather_directly(public_logits, REF, 2)....  5.78 us
  transfers between devices with their start and end apart: 2, of which 2 were waited for; matrix products, arithmetic and copies ran while one was open for 1% of the time, Pallas kernels for 0%

commit v1 on v0

v1 whole, which is shorter than its diff:
```python
import jax
import jax.numpy as jnp
from jax import lax
from jax.experimental import pallas as pl
from jax.experimental.pallas import tpu as pltpu
from jax.sharding import Mesh
from jax.sharding import PartitionSpec as P

REF_VOC = ("ref_0", "ref_1", "ref_2", "voc")
REF = ("ref_0", "ref_1", "ref_2")
CHIP = ("ref_0", "ref_1")
CORE = "ref_2"
VOC_REF = ("voc", "ref_0", "ref_1", "ref_2")

clip_bound = 2.0

LANES = 128
WIDE = 512


def partial_sums_kernel(piece, scale):
    def kernel(owner, counts, ids, priv, own, other, keep, send, peak, pub, acc, left):
        rows, positions, columns = priv.shape
        texts = pub.shape[0]
        chips = own.shape[0]
        flat = texts * positions
        chip, core = ids[0], ids[1]
        lane = lax.broadcasted_iota(jnp.int32, (flat, LANES), 1)
        row = lax.broadcasted_iota(jnp.int32, (flat, LANES), 0)
        tail = piece // LANES * LANES
        used = piece - tail

        index = lax.broadcasted_iota(jnp.int32, (chips, flat, LANES), 0)
        near = own[:, :, tail:WIDE].astype(jnp.float32)
        far = other[:, :, tail:WIDE].astype(jnp.float32)
        earlier = jnp.sum(
            jnp.where(index < chip, near, 0.0) + jnp.where(index < chip + core, far, 0.0), axis=0
        )
        for t in range(texts):
            here = jnp.where((lane == used) & (row == t * positions), earlier, 0.0)
            left[t] = counts[t] - jnp.sum(here).astype(jnp.int32)

        def place(q, value):
            start = q * piece
            base = pl.multiple_of(start // LANES * LANES, LANES)
            shift = start - base
            turned = [
                pltpu.roll(value[:, k * LANES : (k + 1) * LANES], shift, 1)
                for k in range(WIDE // LANES)
            ]
            first = lane >= shift
            for t in range(texts):
                part = slice(t * positions, (t + 1) * positions)
                held = pub[t, :, pl.ds(base, LANES)]
                pub[t, :, pl.ds(base, LANES)] = jnp.where(first[part], turned[0][part], held)
            for k in range(1, WIDE // LANES + 1):
                if k < WIDE // LANES:
                    tile = jnp.where(first, turned[k], turned[k - 1])
                else:
                    tile = turned[k - 1]
                for t in range(texts):
                    part = slice(t * positions, (t + 1) * positions)
                    pub[t, :, pl.ds(base + k * LANES, LANES)] = tile[part]

        def join(j, top):
            a = own[j].astype(jnp.float32)
            b = other[j].astype(jnp.float32)
            place(2 * j, jnp.where(core == 0, a, b))
            place(2 * j + 1, jnp.where(core == 0, b, a))
            both = jnp.maximum(a, b)
            for k in range(WIDE // LANES):
                tile = both[:, k * LANES : (k + 1) * LANES]
                if k * LANES == tail:
                    tile = jnp.where(lane < used, tile, top)
                top = jnp.maximum(top, tile)
            return top

        lowest = jnp.full((flat, LANES), -jnp.inf, jnp.float32)
        top = lax.fori_loop(0, chips, join, lowest)
        peak[...] = jnp.broadcast_to(jnp.max(top, axis=1, keepdims=True), (flat, LANES))

        slots = []
        for r in range(rows):
            text = owner[r]
            still = left[text]
            left[text] = still - 1
            slots.append((text, jnp.where(still > 0, text, texts)))

        def accumulate(start, width):
            for t in range(texts):
                acc[t, :, pl.ds(start, width)] = jnp.zeros((positions, width), jnp.float32)
            for r, (text, slot) in enumerate(slots):
                value = priv[r, :, pl.ds(start, width)].astype(jnp.float32)
                value = value - pub[text, :, pl.ds(start, width)]
                value = jnp.clip(value, -clip_bound, clip_bound)
                acc[slot, :, pl.ds(start, width)] = acc[slot, :, pl.ds(start, width)] + value

        step = 2048
        acc[texts] = jnp.zeros(acc.shape[1:], jnp.float32)

        def chunk(i, carry):
            accumulate(pl.multiple_of(i * step, step), step)
            return carry

        lax.fori_loop(0, columns // step, chunk, 0)
        accumulate(columns // step * step, columns % step)

        def cut(q, out, j):
            start = q * piece
            base = pl.multiple_of(start // LANES * LANES, LANES)
            back = LANES - (start - base)
            turned = []
            for k in range(WIDE // LANES + 1):
                tile = jnp.concatenate(
                    [acc[t, :, pl.ds(base + k * LANES, LANES)] for t in range(texts)], axis=0
                )
                turned.append(pltpu.roll(tile, back, 1))
            for k in range(WIDE // LANES):
                tile = jnp.where(lane < back, turned[k], turned[k + 1])
                tile = jnp.round(tile * scale).astype(jnp.int32).astype(jnp.int16)
                out[j, :, k * LANES : (k + 1) * LANES] = tile

        def part_out(j, carry):
            cut(2 * j + core, keep, j)
            cut(2 * j + 1 - core, send, j)
            return carry

        lax.fori_loop(0, chips, part_out, 0)

    return kernel


def partial_sums(private_logits, own, other, owner, counts, ids, piece, scale):
    rows, positions, columns = private_logits.shape
    texts = counts.shape[0]
    chips, flat, wide = own.shape
    padded = -(-columns // LANES) * LANES
    smem = pl.BlockSpec(memory_space=pltpu.SMEM)
    vmem = pl.BlockSpec(memory_space=pltpu.VMEM)
    half = jax.ShapeDtypeStruct((chips, flat, wide), jnp.int16)
    return pl.pallas_call(
        partial_sums_kernel(piece, scale),
        out_shape=(half, half, jax.ShapeDtypeStruct((flat, LANES), jnp.float32)),
        in_specs=[smem, smem, smem, vmem, vmem, vmem],
        out_specs=(vmem, vmem, vmem),
        scratch_shapes=[
            pltpu.VMEM((texts, positions, padded), jnp.float32),
            pltpu.VMEM((texts + 1, positions, padded), jnp.float32),
            pltpu.SMEM((texts,), jnp.int32),
        ],
        name="partial_sums",
    )(owner, counts, ids, private_logits, own, other)


def body(private_logits, public_logits, noise, owner, counts, tokens):
    texts, positions, piece = public_logits.shape
    rows = owner.shape[0]
    flat = texts * positions
    chips = lax.axis_size(CHIP)
    chip, core = lax.axis_index(CHIP), lax.axis_index(CORE)
    swap = [(0, 1), (1, 0)]
    scale = float(32767 // (2 * rows * int(clip_bound)))

    labels = jnp.arange(texts, dtype=jnp.int32)
    held = jnp.sum((owner[:, None] == labels[None, :]).astype(jnp.int32), 0)
    public_rows = public_logits.reshape(flat, piece)
    count_column = jnp.repeat(held, positions).astype(jnp.bfloat16)[:, None]
    packed = jnp.concatenate([public_rows, count_column], axis=1)
    packed = jnp.pad(packed, ((0, 0), (0, WIDE - piece - 1)))
    own = lax.all_to_all(
        jnp.broadcast_to(packed, (chips, flat, WIDE)), CHIP, split_axis=0, concat_axis=0, tiled=True
    )
    other = lax.ppermute(own, CORE, swap)

    ids = jnp.stack([chip, core]).astype(jnp.int32)
    keep, send, peak = partial_sums(
        private_logits, own, other, owner, counts, ids, piece, scale
    )
    both = keep + lax.ppermute(send, CORE, swap)
    parts = lax.all_to_all(both, CHIP, split_axis=0, concat_axis=0, tiled=True)

    text_scale = 1.0 / (clip_bound * jnp.sqrt(counts.astype(jnp.float32)))
    summed = jnp.sum(parts.astype(jnp.float32), axis=0)
    row_scale = jnp.repeat(text_scale, positions)[:, None] * (1.0 / scale)
    noise_rows = jnp.pad(noise.reshape(flat, piece), ((0, 0), (0, WIDE - piece)))
    combined = packed.astype(jnp.float32) + summed * row_scale + noise_rows.astype(jnp.float32)
    at = jnp.arange(WIDE, dtype=jnp.int32)
    first_column = (lax.axis_index("voc") * lax.axis_size(REF) + lax.axis_index(REF)) * piece
    token_rows = tokens.reshape(flat)[:, None] - first_column
    level = peak[:, 0]
    inside = (at < piece)[None, :]
    terms = jnp.where(inside, jnp.exp(combined - level[:, None]), 0.0)
    row_total = jnp.sum(terms, axis=1)
    picked = jnp.sum(jnp.where((at[None, :] == token_rows) & inside, combined, 0.0), axis=1)

    stats = jnp.concatenate([row_total, picked, level])
    stats = jnp.pad(stats, (0, LANES - 3 * flat))
    devices = lax.axis_size(REF_VOC)
    everyone = lax.all_to_all(
        jnp.broadcast_to(stats, (devices, 1, LANES)), REF_VOC, split_axis=0, concat_axis=0, tiled=True
    ).reshape(devices, LANES)
    levels = everyone[:, 2 * flat : 3 * flat]
    row_peak = jnp.max(levels, axis=0)
    total = jnp.sum(everyone[:, :flat] * jnp.exp(levels - row_peak), axis=0)
    target = jnp.sum(everyone[:, flat : 2 * flat], axis=0)
    lse = row_peak + jnp.log(total)
    logprobs = (combined - lse[:, None])[:, :piece].reshape(texts, positions, piece)
    return (logprobs, (target - lse).reshape(texts, positions))


def solution(mesh):
    finer = Mesh(
        mesh.devices.reshape(8, 4, 2, mesh.shape["voc"]), ("ref_0", "ref_1", "ref_2", "voc")
    )
    placed = (P(REF, None, "voc"), P(None, None, VOC_REF), P(None, None, VOC_REF), P(REF), P(), P())
    return jax.shard_map(
        body, mesh=finer, in_specs=placed, out_specs=(P(None, None, VOC_REF), P()), check_vma=False
    )
```

time: 193 us -> 96.5 us (0.50)
  waiting for transfers between devices: 75.9 us -> 18.2 us
  local copies, waits for them, and re-layouts: 20.8 us -> 4.33 us
  blocking collectives: 66.5 us -> 50.1 us
  Pallas kernels: 0 us -> 11.3 us
  matrix products: 11 us -> 0 us
  starting transfers between devices: 11.9 us -> 7.17 us
    all_to_all x2 -> x1, waiting for transfers between devices: 75.9 us -> 15.5 us  [body(): parts = lax.all_to_all(both, CHIP, split_axis=0, concat_axis=0, tiled=True)]
    all_gather x4 -> x0, blocking collectives: 44.4 us -> none  [all_in_one(): both, at, found = (lax.all_gather(jnp.concatenate(lines), axis), 0, {})]
    all_to_all x1 -> x2, blocking collectives: 22.2 us -> 50.1 us  [the longest x1 27.9 us: body(): lax.all_to_all(jnp.broadcast_to(packed, (chips, flat, WIDE)), CHIP, split...]
    reshape x4 -> x3, local copies, waits for them, and re-layouts: 13.4 us -> 1.4 us  [the longest x1 0.74 us: body(): public_rows = public_logits.reshape(flat, piece)]
    pallas_call x0 -> x1, Pallas kernels: none -> 11.3 us  [partial_sums(): pl.pallas_call(partial_sums_kernel(piece, scale), out_shape=(half, half,...]
    dot_general x2 -> x0, matrix products: 11 us -> none  [the longest x1 5.78 us: body(): jnp.einsum('rt,tpv->rpv', select, gather_directly(public_logits, REF, 2)....]
    all_to_all x2 -> x1, starting transfers between devices: 11.9 us -> 4.3 us  [body(): parts = lax.all_to_all(both, CHIP, split_axis=0, concat_axis=0, tiled=True)]
    ppermute x0 -> x2, starting transfers between devices: none -> 2.88 us  [the longest x1 2.43 us: body(): other = lax.ppermute(own, CORE, swap)]
  transfers between devices with their start and end apart: 2 -> 3, of which waited for: 2 -> 3; matrix products, arithmetic and copies ran while one was open for 1% -> 2% of each run, Pallas kernels for 0% -> 0%
where the time goes in v1:
time: 96.5 us; the launch traced here: 96 us
  blocking collectives  50.1 us (52%)
  waiting for transfers between devices  18.2 us (19%)
  Pallas kernels  11.3 us (12%)
  starting transfers between devices  7.17 us (7%)
  other arithmetic  4.35 us (5%)
  local copies, waits for them, and re-layouts  4.33 us (4%)
    all_to_all x1, blocking collectives, body(): lax.all_to_all(jnp.broadcast_to(packed, (chips, flat, WIDE)), CHIP, split...  27.9 us
    all_to_all x1, blocking collectives, body(): lax.all_to_all(jnp.broadcast_to(stats, (devices, 1, LANES)), REF_VOC, spl...  22.1 us
    all_to_all x1, waiting for transfers between devices, body(): parts = lax.all_to_all(both, CHIP, split_axis=0, concat_axis=0, tiled=True)  15.5 us
    pallas_call x1, Pallas kernels, partial_sums(): pl.pallas_call(partial_sums_kernel(piece, scale), out_shape=(half, half,...  11.3 us
    all_to_all x1, starting transfers between devices, body(): parts = lax.all_to_all(both, CHIP, split_axis=0, concat_axis=0, tiled=True)  4.3 us
    ppermute x1, starting transfers between devices, body(): other = lax.ppermute(own, CORE, swap)  2.43 us
    add x1, other arithmetic, body(): both = keep + lax.ppermute(send, CORE, swap)  2.04 us
  transfers between devices with their start and end apart: 3, of which 3 were waited for; matrix products, arithmetic and copies ran while one was open for 2% of the time, Pallas kernels for 0%

profile of v1, /device:TPU:1, one launch (start us, length us, event | category | flops | bytes accessed | tf_op | source)
XLA Modules:
  0.0 96.0 jit_solution(9537896601050207683)
XLA Ops:
  0.6 0.7 reshape.65
  1.4 0.8 convert_reduce_fusion.1
  2.2 0.1 convert_element_type.42
  2.5 27.9 %all_to_all.15.own = bf16[32,16,512]{2,1,0:T(8,128)(2,1)S(1)} all-to-all(bf16[32,16,512]{2,1,0:T(8,128)(2,1)S(1)} %broadcast_in_dim.36), channel_id=1, replica_groups=mesh['ref_0'=8,'ref_1'=4,'ref_2'=2,'voc'=4] {'ref_0','ref_1'}, dimensions={0} | all-to-all | bytes 1048576 | tf_op jit(solution)/shard_map/all_to_all | solution.py:170
  30.4 2.4 %collective-permute-start = (bf16[32,16,512]{2,1,0:T(8,128)(2,1)S(1)}, bf16[32,16,512]{2,1,0:T(8,128)(2,1)S(1)}, u32[]{:S(2)}, u32[]{:S(2)}) collective-permute-start(bf16[32,16,512]{2,1,0:T(8,128)(2,1)S(1)} %all_to_all.15.own), channel_id=1, source_target_pairs={{0,4},{4,0},{1,5},{5,1},{2,6},{6,2},{3,7},{7,3},{8,12},{12,8},{9,1... | collective-permute-start | bytes 1572872 | tf_op jit(solution)/shard_map/ppermute | solution.py:173
  32.8 0.6 pad_add_fusion.ids
  33.4 0.9 collective-permute-done.other
  34.4 0.8 copy-done.1
  35.2 11.3 %partial_sums.1 = (s16[32,16,512]{2,1,0:T(8,128)(2,1)}, s16[32,16,512]{2,1,0:T(8,128)(2,1)}, f32[16,128]{1,0:T(8,128)}) custom-call(s32[12]{0:T(128)} %owner.1, s32[4]{0:T(128)} %counts.1, s32[2]{0:T(128)} %pad_add_fusion.ids, bf16[12,4,32064]{2,1,0:T(4,128)(2,1)} %priv.1, bf16[32,16,512]{2,1,0:T(8,128)(2,1)} %copy-done, bf16[32,16,512]{2,1,0:T(8,128)(2,1)} %copy-done.1), custom_call_target="tpu_custom_call" | custom-call | tf_op jit(solution)/shard_map/partial_sums/pallas_call | solution.py:141
  46.4 0.4 collective-permute-start.1
  46.9 1.7 %collective-permute-done.1 = s16[32,16,512]{2,1,0:T(8,128)(2,1)S(1)} collective-permute-done((s16[32,16,512]{2,1,0:T(8,128)(2,1)}, s16[32,16,512]{2,1,0:T(8,128)(2,1)S(1)}, u32[]{:S(2)}, u32[]{:S(2)}) %collective-permute-start.1) | collective-permute-done | bytes 524320 | tf_op jit(solution)/shard_map/ppermute | solution.py:179
  48.6 2.0 %add.37 = s16[32,16,512]{2,1,0:T(8,128)(2,1)} add(s16[32,16,512]{2,1,0:T(8,128)(2,1)} %get-tuple-element.5, s16[32,16,512]{2,1,0:T(8,128)(2,1)S(1)} %collective-permute-done.1) | non-fusion elementwise | flops 262144 | bytes 1572864 | tf_op jit(solution)/shard_map/add | solution.py:179
  50.7 4.3 %all-to-all-start.1 = ((s16[32,16,512]{2,1,0:T(8,128)(2,1)}), s16[32,16,512]{2,1,0:T(8,128)(2,1)S(1)}, u32[]{:S(2)}, u32[]{:S(2)}) async-start(s16[32,16,512]{2,1,0:T(8,128)(2,1)} %add.37), calls=%async_computation.1 | async-start | bytes 1048576 | tf_op jit(solution)/shard_map/all_to_all | solution.py:180
  55.2 0.1 mul.44
  55.3 0.8 slice_reduce_fusion.2
  56.1 15.5 %all-to-all-done.1 = s16[32,16,512]{2,1,0:T(8,128)(2,1)S(1)} async-done(((s16[32,16,512]{2,1,0:T(8,128)(2,1)}), s16[32,16,512]{2,1,0:T(8,128)(2,1)S(1)}, u32[]{:S(2)}, u32[]{:S(2)}) %all-to-all-start.1) | async-done | bytes 524320 | tf_op jit(solution)/shard_map/all_to_all | solution.py:180
  71.6 0.2 convert_reduce_fusion
  71.8 0.2 select_reduce_fusion.1
  72.1 22.1 %all_to_all.16 = f32[256,1,128]{2,1,0:T(1,128)S(1)} all-to-all(f32[256,1,128]{2,1,0:T(1,128)S(1)} %broadcast_in_dim.40), channel_id=1, replica_groups=mesh['ref_0'=8,'ref_1'=4,'ref_2'=2,'voc'=4] {'ref_0','ref_1','ref_2','voc'}, dimensions={0} | all-to-all | bytes 262144 | tf_op jit(solution)/shard_map/all_to_all | solution.py:199
  94.3 0.1 copy.16
  94.4 0.1 slice_reduce_fusion.1
  94.5 0.2 slice_reduce_fusion
  94.7 0.6 reshape.68
  95.4 0.7 sub.58
  (23 shorter events, 0.7 us)
Async XLA Ops:
  30.4 4.0 %copy-start = (bf16[32,16,512]{2,1,0:T(8,128)(2,1)}, bf16[32,16,512]{2,1,0:T(8,128)(2,1)S(1)}, u32[]{:S(2)}) copy-start(bf16[32,16,512]{2,1,0:T(8,128)(2,1)S(1)} %all_to_all.15.own) | copy-start | bytes 1572868
  30.4 4.0 %collective-permute-start = (bf16[32,16,512]{2,1,0:T(8,128)(2,1)S(1)}, bf16[32,16,512]{2,1,0:T(8,128)(2,1)S(1)}, u32[]{:S(2)}, u32[]{:S(2)}) collective-permute-start(bf16[32,16,512]{2,1,0:T(8,128)(2,1)S(1)} %all_to_all.15.own), channel_id=1, source_target_pairs={{0,4},{4,0},{1,5},{5,1},{2,6},{6,2},{3,7},{7,3},{8,12},{12,8},{9,1... | collective-permute-start | bytes 1572872 | tf_op jit(solution)/shard_map/ppermute | solution.py:173
  33.4 21.6 %copy-start.3 = (s32[4,4]{1,0:T(4,128)S(1)}, s32[4,4]{1,0:T(4,128)}, u32[]{:S(2)}) copy-start(s32[4,4]{1,0:T(4,128)} %param.11) | copy-start | bytes 196
  33.4 21.7 %copy-start.2 = (bf16[4,4,501]{2,1,0:T(4,128)(2,1)S(1)}, bf16[4,4,501]{2,1,0:T(4,128)(2,1)}, u32[]{:S(2)}) copy-start(bf16[4,4,501]{2,1,0:T(4,128)(2,1)} %param.8) | copy-start | bytes 48100
  33.4 21.7 %copy-start.4 = (s32[4]{0:T(128)S(1)}, s32[4]{0:T(128)}, u32[]{:S(2)}) copy-start(s32[4]{0:T(128)} %counts.1) | copy-start | bytes 52
  34.4 0.8 copy-start.1
  46.4 2.2 %collective-permute-start.1 = (s16[32,16,512]{2,1,0:T(8,128)(2,1)}, s16[32,16,512]{2,1,0:T(8,128)(2,1)S(1)}, u32[]{:S(2)}, u32[]{:S(2)}) collective-permute-start(s16[32,16,512]{2,1,0:T(8,128)(2,1)} %get-tuple-element.6), channel_id=1, source_target_pairs={{0,4},{4,0},{1,5},{5,1},{2,6},{6,2},{3,7},{7,3},{8,12},{12,8},{9,1... | collective-permute-start | bytes 1572872 | tf_op jit(solution)/shard_map/ppermute | solution.py:179
  50.7 20.9 %all-to-all-start.1 = ((s16[32,16,512]{2,1,0:T(8,128)(2,1)}), s16[32,16,512]{2,1,0:T(8,128)(2,1)S(1)}, u32[]{:S(2)}, u32[]{:S(2)}) async-start(s16[32,16,512]{2,1,0:T(8,128)(2,1)} %add.37), calls=%async_computation.1 | async-start | bytes 1048576 | tf_op jit(solution)/shard_map/all_to_all | solution.py:180

commit v2 on v1

v2 whole, which is shorter than its diff:
```python
import jax
import jax.numpy as jnp
from jax import lax
from jax.experimental import pallas as pl
from jax.experimental.pallas import tpu as pltpu
from jax.sharding import Mesh
from jax.sharding import PartitionSpec as P

REF_VOC = ("ref_0", "ref_1", "ref_2", "voc")
REF = ("ref_0", "ref_1", "ref_2")
CHIP = ("ref_0", "ref_1")
CORE = "ref_2"
VOC_REF = ("voc", "ref_0", "ref_1", "ref_2")

clip_bound = 2.0

LANES = 128
WIDE = 512
TILES = WIDE // LANES
WINDOW = WIDE + LANES
GROUP = 4

PARAMS = pltpu.CompilerParams(vmem_limit_bytes=16 << 20)
SMEM = pl.BlockSpec(memory_space=pltpu.SMEM)
VMEM = pl.BlockSpec(memory_space=pltpu.VMEM)


def tile_of(x, k):
    return x[:, k * LANES : (k + 1) * LANES]


def turned(tiles, shift, lane):
    spun = [pltpu.roll(tile, shift, 1) for tile in tiles]
    return [jnp.where(lane >= shift, spun[k], spun[k - 1]) for k in range(TILES)]


def turned_back(tiles, shift, lane):
    back = LANES - shift
    spun = [pltpu.roll(tile, back, 1) for tile in tiles]
    return [jnp.where(lane < back, spun[k], spun[(k + 1) % TILES]) for k in range(TILES)]


def lanes_of(shape):
    return lax.broadcasted_iota(jnp.int32, shape, len(shape) - 1)


def pack_kernel(public, near, far, ids, out, flat_rows):
    texts, positions, piece = public.shape
    flat = texts * positions
    for t in range(texts):
        flat_rows[t * positions : (t + 1) * positions, :piece] = public[t].astype(jnp.float32)
    row = lax.broadcasted_iota(jnp.int32, (flat, LANES), 0)
    lane = lanes_of((flat, LANES))
    number = jnp.zeros((flat, LANES), jnp.float32)
    for t in range(texts):
        held = jnp.int32(0)
        for r in range(near.shape[0]):
            held += jnp.where(near[r] == t, 1, 0) + jnp.where(far[r] == t, 1, 0)
        inside = (row >= t * positions) & (row < (t + 1) * positions)
        number = jnp.where(inside, held.astype(jnp.float32), number)
    values = flat_rows[...]
    tiles = [
        jnp.where(lane + k * LANES < piece, tile_of(values, k), number) for k in range(TILES)
    ]
    tiles = [tile.astype(out.dtype) for tile in turned(tiles, ids[2], lane)]
    for j in range(out.shape[0]):
        for k in range(TILES):
            out[j, :, k * LANES : (k + 1) * LANES] = tiles[k]


def sums_kernel(piece, scale):
    def kernel(owner, partner, counts, ids, priv, swapped, own, out, pub, acc, left):
        rows, positions, columns = priv.shape
        texts = counts.shape[0]
        chips, flat, _ = own.shape
        chip, core = ids[0], ids[1]
        lane = lanes_of((flat, LANES))
        row = lax.broadcasted_iota(jnp.int32, (flat, LANES), 0)
        last = columns // LANES * LANES

        def begins(j):
            start = (2 * j + core) * piece
            base = start // LANES * LANES
            return pl.multiple_of(base, LANES), start - base

        def widen(j, earlier):
            value = own[j].astype(jnp.float32)
            for t in range(texts):
                part = value[t * positions : (t + 1) * positions]
                pub[t, :, pl.ds(pl.multiple_of(j * WINDOW, LANES), WIDE)] = part
                pub[t, :, pl.ds(pl.multiple_of(j * WINDOW + WIDE, LANES), LANES)] = part[:, :LANES]
            shift = begins(j)[1]
            free = jnp.where(shift == 0, LANES - 1, shift - 1)
            tile = jnp.where(shift == 0, tile_of(value, TILES - 1), tile_of(value, 0))
            free = jnp.where(j < chip, free, LANES)
            return earlier + jnp.where(lane == free, tile, 0.0)

        earlier = lax.fori_loop(0, chips, widen, jnp.zeros((flat, LANES), jnp.float32))
        for t in range(texts):
            here = jnp.where(row == t * positions, earlier, 0.0)
            left[t] = counts[t] - jnp.sum(here).astype(jnp.int32)

        slots = [[None] * rows, [None] * rows]
        for c in range(2):
            for r in range(rows):
                text = jnp.where(core == c, owner[r], partner[r])
                still = left[text]
                left[text] = still - 1
                slots[c][r] = jnp.where(still > 0, text, texts)
        acc[texts] = jnp.zeros(acc.shape[1:], jnp.float32)

        def accumulate(first, many, size):
            places = [first + g for g in range(many)]
            bases = [begins(j)[0] for j in places]
            for t in range(texts):
                for g in range(many):
                    acc[t, :, g * WINDOW : g * WINDOW + size[g]] = jnp.zeros(
                        (positions, size[g]), jnp.float32
                    )
            for r in range(rows):
                for held, text, c in ((priv, owner, core), (swapped, partner, 1 - core)):
                    slot = jnp.where(c == 0, slots[0][r], slots[1][r])
                    for g, j in enumerate(places):
                        at = pl.multiple_of(j * WINDOW, LANES)
                        value = held[r, :, pl.ds(bases[g], size[g])].astype(jnp.float32)
                        value = value - pub[text[r], :, pl.ds(at, size[g])]
                        value = jnp.clip(value, -clip_bound, clip_bound)
                        where = slice(g * WINDOW, g * WINDOW + size[g])
                        acc[slot, :, where] = acc[slot, :, where] + value
            for g, j in enumerate(places):
                shift = begins(j)[1]
                tiles = [
                    jnp.concatenate(
                        [
                            acc[t, :, g * WINDOW + k * LANES : g * WINDOW + (k + 1) * LANES]
                            for t in range(texts)
                        ],
                        axis=0,
                    )
                    for k in range(TILES + 1)
                ]
                tiles[0] = jnp.where(lane >= shift, tiles[0], tiles[TILES])
                for k in range(TILES):
                    fixed = jnp.round(tiles[k] * scale).astype(jnp.int32).astype(jnp.int16)
                    out[j, :, k * LANES : (k + 1) * LANES] = fixed

        def some(i, carry):
            accumulate(i * GROUP, GROUP, [WINDOW] * GROUP)
            return carry

        lax.fori_loop(0, chips // GROUP - 1, some, 0)
        accumulate(chips - GROUP, GROUP - 1, [WINDOW] * (GROUP - 1))
        for c in range(2):
            start = (2 * chips - 2 + c) * piece // LANES * LANES

            @pl.when(core == c)
            def _():
                accumulate(jnp.int32(chips - 1), 1, [min(WINDOW, columns - start)])

    return kernel


def chip_sums(private_logits, swapped, own, owner, partner, counts, ids, piece, scale):
    rows, positions, columns = private_logits.shape
    texts = counts.shape[0]
    chips, flat, wide = own.shape
    return pl.pallas_call(
        sums_kernel(piece, scale),
        out_shape=pltpu.VMEM((chips, flat, wide), jnp.int16),
        in_specs=[SMEM, SMEM, SMEM, SMEM, VMEM, VMEM, VMEM],
        out_specs=VMEM,
        scratch_shapes=[
            pltpu.VMEM((texts, positions, chips * WINDOW), jnp.float32),
            pltpu.VMEM((texts + 1, positions, GROUP * WINDOW), jnp.float32),
            pltpu.SMEM((texts,), jnp.int32),
        ],
        compiler_params=PARAMS,
        name="chip_sums",
    )(owner, partner, counts, ids, private_logits, swapped, own)


def finish_kernel(inverse):
    def kernel(counts, tokens, ids, parts, public, noise, combined, stats, base):
        texts, positions, piece = public.shape
        flat = texts * positions
        lane = lanes_of((flat, LANES))
        row = lax.broadcasted_iota(jnp.int32, (flat, LANES), 0)
        base[...] = jnp.full(base.shape, -jnp.inf, jnp.float32)
        for t in range(texts):
            part = slice(t * positions, (t + 1) * positions)
            base[0, part, :piece] = public[t].astype(jnp.float32)
            base[1, part, :piece] = noise[t].astype(jnp.float32)
        scale = jnp.zeros((flat, LANES), jnp.float32)
        token = jnp.zeros((flat, LANES), jnp.int32)
        for t in range(texts):
            inside = (row >= t * positions) & (row < (t + 1) * positions)
            number = jnp.where(inside, counts[t].astype(jnp.float32), 1.0)
            scale = jnp.where(inside, inverse / (clip_bound * jnp.sqrt(number)), scale)
            for p in range(positions):
                token = jnp.where(row == t * positions + p, tokens[t, p], token)
        token = token - ids[3]
        total = []
        for k in range(TILES):
            tile = parts[0, :, k * LANES : (k + 1) * LANES].astype(jnp.int32)
            for j in range(1, parts.shape[0]):
                tile = tile + parts[j, :, k * LANES : (k + 1) * LANES].astype(jnp.int32)
            total.append(tile.astype(jnp.float32))
        total = turned_back(total, ids[2], lane)
        public_tiles = [base[0, :, k * LANES : (k + 1) * LANES] for k in range(TILES)]
        level = public_tiles[0]
        for k in range(1, TILES):
            level = jnp.maximum(level, public_tiles[k])
        level = jnp.max(level, axis=1, keepdims=True)
        terms = jnp.zeros((flat, LANES), jnp.float32)
        picked = jnp.zeros((flat, LANES), jnp.float32)
        for k in range(TILES):
            tile = public_tiles[k] + total[k] * scale + base[1, :, k * LANES : (k + 1) * LANES]
            inside = lane + k * LANES < piece
            combined[:, k * LANES : (k + 1) * LANES] = tile
            terms = terms + jnp.where(inside, jnp.exp(tile - level), 0.0)
            picked = picked + jnp.where((lane + k * LANES == token) & inside, tile, 0.0)
        terms = jnp.sum(terms, axis=1, keepdims=True)
        picked = jnp.sum(picked, axis=1, keepdims=True)
        spread = jnp.where(lane == row, terms, 0.0)
        spread = spread + jnp.where(lane == row + flat, picked, 0.0)
        spread = spread + jnp.where(lane == row + 2 * flat, level, 0.0)
        stats[...] = jnp.sum(spread, axis=0, keepdims=True)

    return kernel


def body(private_logits, public_logits, noise, owner, counts, tokens):
    texts, positions, piece = public_logits.shape
    rows = owner.shape[0]
    flat = texts * positions
    chips = lax.axis_size(CHIP)
    chip, core = lax.axis_index(CHIP), lax.axis_index(CORE)
    swap = [(0, 1), (1, 0)]
    scale = float(32767 // (2 * rows * int(clip_bound)))
    place = lax.axis_index(REF)
    first_column = (lax.axis_index("voc") * lax.axis_size(REF) + place) * piece
    ids = jnp.stack([chip, core, place * piece % LANES, first_column]).astype(jnp.int32)

    partner = lax.ppermute(owner, CORE, swap)
    swapped = lax.ppermute(private_logits, CORE, swap)
    packed = pl.pallas_call(
        pack_kernel,
        out_shape=pltpu.VMEM((chips, flat, WIDE), jnp.bfloat16),
        in_specs=[VMEM, SMEM, SMEM, SMEM],
        out_specs=VMEM,
        scratch_shapes=[pltpu.VMEM((flat, WIDE), jnp.float32)],
        compiler_params=PARAMS,
        name="pack",
    )(public_logits, owner, partner, ids)
    own = lax.all_to_all(packed, CHIP, split_axis=0, concat_axis=0, tiled=True)
    private_logits, swapped, own = (
        pltpu.with_memory_space_constraint(x, pltpu.VMEM) for x in (private_logits, swapped, own)
    )
    sums = chip_sums(private_logits, swapped, own, owner, partner, counts, ids, piece, scale)
    parts = lax.all_to_all(sums, CHIP, split_axis=0, concat_axis=0, tiled=True)

    parts = pltpu.with_memory_space_constraint(parts, pltpu.VMEM)
    combined, stats = pl.pallas_call(
        finish_kernel(1.0 / scale),
        out_shape=(
            pltpu.VMEM((flat, WIDE), jnp.float32),
            pltpu.VMEM((1, LANES), jnp.float32),
        ),
        in_specs=[SMEM, SMEM, SMEM, VMEM, VMEM, VMEM],
        out_specs=(VMEM, VMEM),
        scratch_shapes=[pltpu.VMEM((2, flat, WIDE), jnp.float32)],
        compiler_params=PARAMS,
        name="finish",
    )(counts, tokens, ids, parts, public_logits, noise)

    devices = lax.axis_size(REF_VOC)
    everyone = lax.all_to_all(
        jnp.broadcast_to(stats, (devices, 1, LANES)), REF_VOC, split_axis=0, concat_axis=0, tiled=True
    ).reshape(devices, LANES)
    levels = everyone[:, 2 * flat : 3 * flat]
    row_peak = jnp.max(levels, axis=0)
    total = jnp.sum(everyone[:, :flat] * jnp.exp(levels - row_peak), axis=0)
    target = jnp.sum(everyone[:, flat : 2 * flat], axis=0)
    lse = row_peak + jnp.log(total)
    logprobs = (combined - lse[:, None])[:, :piece].reshape(texts, positions, piece)
    return (logprobs, (target - lse).reshape(texts, positions))


def solution(mesh):
    finer = Mesh(
        mesh.devices.reshape(8, 4, 2, mesh.shape["voc"]), ("ref_0", "ref_1", "ref_2", "voc")
    )
    placed = (P(REF, None, "voc"), P(None, None, VOC_REF), P(None, None, VOC_REF), P(REF), P(), P())
    return jax.shard_map(
        body, mesh=finer, in_specs=placed, out_specs=(P(None, None, VOC_REF), P()), check_vma=False
    )
```

time: 96.5 us -> 90.5 us (0.938)
  blocking collectives: 50.1 us -> 69.3 us
  waiting for transfers between devices: 18.2 us -> 5.23 us
  Pallas kernels: 11.3 us -> 5.08 us
  other arithmetic: 4.35 us -> 0.46 us
  starting transfers between devices: 7.17 us -> 3.39 us
  local copies, waits for them, and re-layouts: 4.33 us -> 6.03 us
    all_to_all x1 -> x2, blocking collectives: 27.9 us -> 46 us  [the longest x1 25.7 us: body(): own = lax.all_to_all(packed, CHIP, split_axis=0, concat_axis=0, tiled=True)]
    all_to_all x1 -> x0, waiting for transfers between devices: 15.5 us -> none  [body(): parts = lax.all_to_all(both, CHIP, split_axis=0, concat_axis=0, tiled=True)]
    pallas_call x1 -> x3, Pallas kernels: 11.3 us -> 5.08 us  [the longest x1 3.46 us: chip_sums(): pl.pallas_call(sums_kernel(piece, scale), out_shape=pltpu.VMEM((chips, fl...]
    all_to_all x1 -> x0, starting transfers between devices: 4.3 us -> none  [body(): parts = lax.all_to_all(both, CHIP, split_axis=0, concat_axis=0, tiled=True)]
    unnamed x10 -> x16, local copies, waits for them, and re-layouts: 0.83 us -> 4.56 us
    ppermute x2, waiting for transfers between devices: 2.69 us -> 5.23 us  [the longest x1 5.23 us: body(): partner = lax.ppermute(owner, CORE, swap)]
    add x1 -> x0, other arithmetic: 2.04 us -> none  [body(): both = keep + lax.ppermute(send, CORE, swap)]
    all_to_all x1, blocking collectives: 22.1 us -> 23.3 us  [body(): lax.all_to_all(jnp.broadcast_to(stats, (devices, 1, LANES)), REF_VOC, spl...]
  transfers between devices with their start and end apart: 3 -> 2, of which waited for: 3 -> 1; matrix products, arithmetic and copies ran while one was open for 2% -> 0% of each run, Pallas kernels for 0% -> 1%
where the time goes in v2:
time: 90.5 us; the launch traced here: 90.2 us
  blocking collectives  69.3 us (77%)
  local copies, waits for them, and re-layouts  6.03 us (7%)
  waiting for transfers between devices  5.23 us (6%)
  Pallas kernels  5.08 us (6%)
  starting transfers between devices  3.39 us (4%)
    all_to_all x1, blocking collectives, body(): own = lax.all_to_all(packed, CHIP, split_axis=0, concat_axis=0, tiled=True)  25.7 us
    all_to_all x1, blocking collectives, body(): lax.all_to_all(jnp.broadcast_to(stats, (devices, 1, LANES)), REF_VOC, spl...  23.3 us
    all_to_all x1, blocking collectives, body(): parts = lax.all_to_all(sums, CHIP, split_axis=0, concat_axis=0, tiled=True)  20.2 us
    ppermute x1, waiting for transfers between devices, body(): partner = lax.ppermute(owner, CORE, swap)  5.23 us
    unnamed x16, local copies, waits for them, and re-layouts  4.56 us
    pallas_call x1, Pallas kernels, chip_sums(): pl.pallas_call(sums_kernel(piece, scale), out_shape=pltpu.VMEM((chips, fl...  3.46 us
    ppermute x1, starting transfers between devices, body(): swapped = lax.ppermute(private_logits, CORE, swap)  3.29 us
  transfers between devices with their start and end apart: 2, of which 1 were waited for; matrix products, arithmetic and copies ran while one was open for 0% of the time, Pallas kernels for 1%

profile of v2, /device:TPU:1, one launch (start us, length us, event | category | flops | bytes accessed | tf_op | source)
XLA Modules:
  0.0 90.2 jit_solution(1450506932487076695)
XLA Ops:
  0.6 3.3 %collective-permute-start.1 = (bf16[12,4,32064]{2,1,0:T(4,128)(2,1)}, bf16[12,4,32064]{2,1,0:T(4,128)(2,1)S(1)}, u32[]{:S(2)}, u32[]{:S(2)}) collective-permute-start(bf16[12,4,32064]{2,1,0:T(4,128)(2,1)} %priv.1), channel_id=1, source_target_pairs={{0,4},{4,0},{1,5},{5,1},{2,6},{6,2},{3,7},{7,3},{8,12},{12,8},{9,1... | collective-permute-start | bytes 9234440 | tf_op jit(solution)/shard_map/ppermute | solution.py:245
  3.9 0.1 collective-permute-start
  4.0 0.1 pad_add_fusion.ids
  4.1 5.2 %collective-permute-done.far.partner = s32[12]{0:T(128)S(1)} collective-permute-done((s32[12]{0:T(128)}, s32[12]{0:T(128)S(1)}, u32[]{:S(2)}, u32[]{:S(2)}) %collective-permute-start) | collective-permute-done | bytes 80 | tf_op jit(solution)/shard_map/ppermute | solution.py:244
  9.3 0.7 copy-done.1
  10.0 0.7 copy-done.5
  10.7 0.8 pack.1
  11.5 25.7 %all_to_all.15.own = bf16[32,16,512]{2,1,0:T(8,128)(2,1)S(1)} all-to-all(bf16[32,16,512]{2,1,0:T(8,128)(2,1)S(1)} %pack.1), channel_id=1, replica_groups=mesh['ref_0'=8,'ref_1'=4,'ref_2'=2,'voc'=4] {'ref_0','ref_1'}, dimensions={0} | all-to-all | bytes 1048576 | tf_op jit(solution)/shard_map/all_to_all | solution.py:255
  37.2 0.0 collective-permute-done.1.swapped
  37.2 1.9 %copy-done = bf16[12,4,32064]{2,1,0:T(4,128)(2,1)S(1)} copy-done((bf16[12,4,32064]{2,1,0:T(4,128)(2,1)S(1)}, bf16[12,4,32064]{2,1,0:T(4,128)(2,1)}, u32[]{:S(2)}) %copy-start) | copy-done | bytes 3078168
  39.1 0.7 copy-done.6
  39.8 0.7 copy-done.7
  40.4 3.5 %chip_sums.1 = s16[32,16,512]{2,1,0:T(8,128)(2,1)S(1)} custom-call(s32[12]{0:T(128)S(1)} %copy-done.6, s32[12]{0:T(128)S(1)} %collective-permute-done.far.partner, s32[4]{0:T(128)S(1)} %copy-done.7, s32[4]{0:T(128)S(1)} %pad_add_fusion.ids, bf16[12,4,32064]{2,1,0:T(4,128)(2,1)S(1)} %copy-done, bf16[12,4,32064]{2,1,0:T(4,128)(2,1)S(1)} %collective-permute-done.1.swapped, ...), custom_call_target="tpu_custom_call" | custom-call | tf_op jit(solution)/shard_map/chip_sums/pallas_call | solution.py:167
  43.9 20.2 %all_to_all.16.parts = s16[32,16,512]{2,1,0:T(8,128)(2,1)S(1)} all-to-all(s16[32,16,512]{2,1,0:T(8,128)(2,1)S(1)} %chip_sums.1), channel_id=1, replica_groups=mesh['ref_0'=8,'ref_1'=4,'ref_2'=2,'voc'=4] {'ref_0','ref_1'}, dimensions={0} | all-to-all | bytes 1048576 | tf_op jit(solution)/shard_map/all_to_all | solution.py:260
  64.1 0.0 copy-done.2
  64.1 0.8 finish.1
  65.0 0.1 broadcast_in_dim.2
  65.1 23.3 %all_to_all.17 = f32[256,1,128]{2,1,0:T(1,128)S(1)} all-to-all(f32[256,1,128]{2,1,0:T(1,128)S(1)} %broadcast_in_dim.2), channel_id=1, replica_groups=mesh['ref_0'=8,'ref_1'=4,'ref_2'=2,'voc'=4] {'ref_0','ref_1','ref_2','voc'}, dimensions={0} | all-to-all | bytes 262144 | tf_op jit(solution)/shard_map/all_to_all | solution.py:277
  88.4 0.1 copy.11
  88.5 0.1 slice_reduce_fusion.1
  88.6 0.2 slice_reduce_fusion
  88.8 0.1 slice_subtract_fusion
  88.9 0.6 reshape.26
  89.5 0.7 sub.28
  (11 shorter events, 0.0 us)
Async XLA Ops:
  0.6 36.6 %collective-permute-start.1 = (bf16[12,4,32064]{2,1,0:T(4,128)(2,1)}, bf16[12,4,32064]{2,1,0:T(4,128)(2,1)S(1)}, u32[]{:S(2)}, u32[]{:S(2)}) collective-permute-start(bf16[12,4,32064]{2,1,0:T(4,128)(2,1)} %priv.1), channel_id=1, source_target_pairs={{0,4},{4,0},{1,5},{5,1},{2,6},{6,2},{3,7},{7,3},{8,12},{12,8},{9,1... | collective-permute-start | bytes 9234440 | tf_op jit(solution)/shard_map/ppermute | solution.py:245
  3.9 5.4 %collective-permute-start = (s32[12]{0:T(128)}, s32[12]{0:T(128)S(1)}, u32[]{:S(2)}, u32[]{:S(2)}) collective-permute-start(s32[12]{0:T(128)} %owner.1), channel_id=1, source_target_pairs={{0,4},{4,0},{1,5},{5,1},{2,6},{6,2},{3,7},{7,3},{8,12},{12,8},{9,1... | collective-permute-start | bytes 152 | tf_op jit(solution)/shard_map/ppermute | solution.py:244
  9.3 0.7 copy-start.1
  10.0 0.7 copy-start.5
  37.2 1.9 %copy-start = (bf16[12,4,32064]{2,1,0:T(4,128)(2,1)S(1)}, bf16[12,4,32064]{2,1,0:T(4,128)(2,1)}, u32[]{:S(2)}) copy-start(bf16[12,4,32064]{2,1,0:T(4,128)(2,1)} %priv.1) | copy-start | bytes 9234436
  39.1 0.7 copy-start.6
  39.8 0.7 copy-start.7
  40.4 23.7 %copy-start.2 = (bf16[4,4,501]{2,1,0:T(4,128)(2,1)S(1)}, bf16[4,4,501]{2,1,0:T(4,128)(2,1)}, u32[]{:S(2)}) copy-start(bf16[4,4,501]{2,1,0:T(4,128)(2,1)} %public.3) | copy-start | bytes 48100
  40.4 23.7 %copy-start.3 = (bf16[4,4,501]{2,1,0:T(4,128)(2,1)S(1)}, bf16[4,4,501]{2,1,0:T(4,128)(2,1)}, u32[]{:S(2)}) copy-start(bf16[4,4,501]{2,1,0:T(4,128)(2,1)} %noise.1) | copy-start | bytes 48100
  40.4 23.7 %copy-start.4 = (s32[4,4]{1,0:T(4,128)S(1)}, s32[4,4]{1,0:T(4,128)}, u32[]{:S(2)}) copy-start(s32[4,4]{1,0:T(4,128)} %tokens.1) | copy-start | bytes 196

commit v3 on v2

--- a/solution.py
+++ b/solution.py
@@ -19,10 +19,14 @@
 TILES = WIDE // LANES
 WINDOW = WIDE + LANES
 GROUP = 4
+LEAD = LANES
+
+CHIP_AT, CORE_AT, SHIFT, FIRST, COUNTS, TOKENS, OWNER = 0, 1, 2, 3, 4, 8, 24
 
 PARAMS = pltpu.CompilerParams(vmem_limit_bytes=16 << 20)
 SMEM = pl.BlockSpec(memory_space=pltpu.SMEM)
 VMEM = pl.BlockSpec(memory_space=pltpu.VMEM)
+HBM = pl.BlockSpec(memory_space=pltpu.HBM)
 
 
 def tile_of(x, k):
@@ -44,7 +48,7 @@
     return lax.broadcasted_iota(jnp.int32, shape, len(shape) - 1)
 
 
-def pack_kernel(public, near, far, ids, out, flat_rows):
+def pack_kernel(public, table, far, out, flat_rows):
     texts, positions, piece = public.shape
     flat = texts * positions
     for t in range(texts):
@@ -54,26 +58,46 @@
     number = jnp.zeros((flat, LANES), jnp.float32)
     for t in range(texts):
         held = jnp.int32(0)
-        for r in range(near.shape[0]):
-            held += jnp.where(near[r] == t, 1, 0) + jnp.where(far[r] == t, 1, 0)
+        for r in range(far.shape[0]):
+            held += jnp.where(table[OWNER + r] == t, 1, 0) + jnp.where(far[r] == t, 1, 0)
         inside = (row >= t * positions) & (row < (t + 1) * positions)
         number = jnp.where(inside, held.astype(jnp.float32), number)
     values = flat_rows[...]
     tiles = [
         jnp.where(lane + k * LANES < piece, tile_of(values, k), number) for k in range(TILES)
     ]
-    tiles = [tile.astype(out.dtype) for tile in turned(tiles, ids[2], lane)]
+    tiles = [tile.astype(out.dtype) for tile in turned(tiles, table[SHIFT], lane)]
     for j in range(out.shape[0]):
         for k in range(TILES):
             out[j, :, k * LANES : (k + 1) * LANES] = tiles[k]
 
 
 def sums_kernel(piece, scale):
-    def kernel(owner, partner, counts, ids, priv, swapped, own, out, pub, acc, left):
+    def kernel(table, partner, source, swapped, own, out, priv, pub, acc, left, arrived):
         rows, positions, columns = priv.shape
-        texts = counts.shape[0]
+        texts = pub.shape[0]
         chips, flat, _ = own.shape
-        chip, core = ids[0], ids[1]
+        groups = chips // GROUP
+        chip, core = table[CHIP_AT], table[CORE_AT]
+
+        stride = 2 * GROUP * piece
+        stride = -(-stride // LANES) * LANES
+
+        def copy_of(i, start, width):
+            return pltpu.make_async_copy(
+                source.at[:, :, pl.ds(start, width)],
+                priv.at[:, :, pl.ds(start, width)],
+                arrived.at[i],
+            )
+
+        first_chunk = (0, 0, stride + LEAD)
+        last_start = LEAD + (groups - 1) * stride
+        last_chunk = (groups - 1, last_start, columns - last_start)
+        copy_of(*first_chunk).start()
+        for i in range(1, groups - 1):
+            copy_of(i, LEAD + i * stride, stride).start()
+        copy_of(*last_chunk).start()
+
         lane = lanes_of((flat, LANES))
         row = lax.broadcasted_iota(jnp.int32, (flat, LANES), 0)
         last = columns // LANES * LANES
@@ -98,12 +122,12 @@
         earlier = lax.fori_loop(0, chips, widen, jnp.zeros((flat, LANES), jnp.float32))
         for t in range(texts):
             here = jnp.where(row == t * positions, earlier, 0.0)
-            left[t] = counts[t] - jnp.sum(here).astype(jnp.int32)
+            left[t] = table[COUNTS + t] - jnp.sum(here).astype(jnp.int32)
 
         slots = [[None] * rows, [None] * rows]
         for c in range(2):
             for r in range(rows):
-                text = jnp.where(core == c, owner[r], partner[r])
+                text = jnp.where(core == c, table[OWNER + r], partner[r])
                 still = left[text]
                 left[text] = still - 1
                 slots[c][r] = jnp.where(still > 0, text, texts)
@@ -118,12 +142,15 @@
                         (positions, size[g]), jnp.float32
                     )
             for r in range(rows):
-                for held, text, c in ((priv, owner, core), (swapped, partner, 1 - core)):
+                for held, text, c in (
+                    (priv, table[OWNER + r], core),
+                    (swapped, partner[r], 1 - core),
+                ):
                     slot = jnp.where(c == 0, slots[0][r], slots[1][r])
                     for g, j in enumerate(places):
                         at = pl.multiple_of(j * WINDOW, LANES)
                         value = held[r, :, pl.ds(bases[g], size[g])].astype(jnp.float32)
-                        value = value - pub[text[r], :, pl.ds(at, size[g])]
+                        value = value - pub[text, :, pl.ds(at, size[g])]
                         value = jnp.clip(value, -clip_bound, clip_bound)
                         where = slice(g * WINDOW, g * WINDOW + size[g])
                         acc[slot, :, where] = acc[slot, :, where] + value
@@ -145,10 +172,14 @@
                     out[j, :, k * LANES : (k + 1) * LANES] = fixed
 
         def some(i, carry):
+            copy_of(i, pl.multiple_of(LEAD + i * stride, LANES), stride).wait()
             accumulate(i * GROUP, GROUP, [WINDOW] * GROUP)
             return carry
 
-        lax.fori_loop(0, chips // GROUP - 1, some, 0)
+        copy_of(*first_chunk).wait()
+        accumulate(jnp.int32(0), GROUP, [WINDOW] * GROUP)
+        lax.fori_loop(1, groups - 1, some, 0)
+        copy_of(*last_chunk).wait()
         accumulate(chips - GROUP, GROUP - 1, [WINDOW] * (GROUP - 1))
         for c in range(2):
             start = (2 * chips - 2 + c) * piece // LANES * LANES
@@ -160,27 +191,28 @@
     return kernel
 
 
-def chip_sums(private_logits, swapped, own, owner, partner, counts, ids, piece, scale):
+def chip_sums(private_logits, swapped, own, table, partner, texts, piece, scale):
     rows, positions, columns = private_logits.shape
-    texts = counts.shape[0]
     chips, flat, wide = own.shape
     return pl.pallas_call(
         sums_kernel(piece, scale),
         out_shape=pltpu.VMEM((chips, flat, wide), jnp.int16),
-        in_specs=[SMEM, SMEM, SMEM, SMEM, VMEM, VMEM, VMEM],
+        in_specs=[SMEM, SMEM, HBM, VMEM, VMEM],
         out_specs=VMEM,
         scratch_shapes=[
+            pltpu.VMEM(private_logits.shape, private_logits.dtype),
             pltpu.VMEM((texts, positions, chips * WINDOW), jnp.float32),
             pltpu.VMEM((texts + 1, positions, GROUP * WINDOW), jnp.float32),
             pltpu.SMEM((texts,), jnp.int32),
+            pltpu.SemaphoreType.DMA((chips // GROUP,)),
         ],
         compiler_params=PARAMS,
         name="chip_sums",
-    )(owner, partner, counts, ids, private_logits, swapped, own)
+    )(table, partner, private_logits, swapped, own)
 
 
 def finish_kernel(inverse):
-    def kernel(counts, tokens, ids, parts, public, noise, combined, stats, base):
+    def kernel(table, parts, public, noise, combined, stats, base):
         texts, positions, piece = public.shape
         flat = texts * positions
         lane = lanes_of((flat, LANES))
@@ -194,18 +226,19 @@
         token = jnp.zeros((flat, LANES), jnp.int32)
         for t in range(texts):
             inside = (row >= t * positions) & (row < (t + 1) * positions)
-            number = jnp.where(inside, counts[t].astype(jnp.float32), 1.0)
+            number = jnp.where(inside, table[COUNTS + t].astype(jnp.float32), 1.0)
             scale = jnp.where(inside, inverse / (clip_bound * jnp.sqrt(number)), scale)
             for p in range(positions):
-                token = jnp.where(row == t * positions + p, tokens[t, p], token)
-        token = token - ids[3]
+                at = t * positions + p
+                token = jnp.where(row == at, table[TOKENS + at], token)
+        token = token - table[FIRST]
         total = []
         for k in range(TILES):
             tile = parts[0, :, k * LANES : (k + 1) * LANES].astype(jnp.int32)
             for j in range(1, parts.shape[0]):
                 tile = tile + parts[j, :, k * LANES : (k + 1) * LANES].astype(jnp.int32)
             total.append(tile.astype(jnp.float32))
-        total = turned_back(total, ids[2], lane)
+        total = turned_back(total, table[SHIFT], lane)
         public_tiles = [base[0, :, k * LANES : (k + 1) * LANES] for k in range(TILES)]
         level = public_tiles[0]
         for k in range(1, TILES):
@@ -229,6 +262,30 @@
     return kernel
 
 
+def last_kernel(everyone, combined, logprobs, target):
+    texts, positions, piece = logprobs.shape
+    flat = texts * positions
+    values = everyone[...]
+    lane = lanes_of((1, LANES))
+    level = jnp.max(values, axis=0, keepdims=True)
+    weight = pltpu.roll(jnp.exp(values - level), LANES - 2 * flat, 1)
+    total = jnp.sum(values * weight, axis=0, keepdims=True)
+    picked = pltpu.roll(jnp.sum(values, axis=0, keepdims=True), LANES - flat, 1)
+    level = pltpu.roll(level, LANES - 2 * flat, 1)
+    own = lane < flat
+    lse = jnp.where(own, level + jnp.log(jnp.where(own, total, 1.0)), 0.0)
+    picked = picked - lse
+    square = (flat, LANES)
+    mine = lanes_of(square) == lax.broadcasted_iota(jnp.int32, square, 0)
+    column = jnp.sum(jnp.where(mine, jnp.broadcast_to(lse, square), 0.0), axis=1, keepdims=True)
+    shifted = combined[:, :piece] - column
+    for t in range(texts):
+        logprobs[t] = shifted[t * positions : (t + 1) * positions]
+    for t in range(texts):
+        turn = picked if t == 0 else pltpu.roll(picked, LANES - t * positions, 1)
+        target[t : t + 1, :] = turn[:, :positions]
+
+
 def body(private_logits, public_logits, noise, owner, counts, tokens):
     texts, positions, piece = public_logits.shape
     rows = owner.shape[0]
@@ -239,24 +296,31 @@
     scale = float(32767 // (2 * rows * int(clip_bound)))
     place = lax.axis_index(REF)
     first_column = (lax.axis_index("voc") * lax.axis_size(REF) + place) * piece
-    ids = jnp.stack([chip, core, place * piece % LANES, first_column]).astype(jnp.int32)
+    table = jnp.concatenate(
+        [
+            jnp.stack([chip, core, place * piece % LANES, first_column]).astype(jnp.int32),
+            counts,
+            tokens.reshape(-1),
+            owner,
+        ]
+    )
 
     partner = lax.ppermute(owner, CORE, swap)
-    swapped = lax.ppermute(private_logits, CORE, swap)
+    partner, private_later = lax.optimization_barrier((partner, private_logits))
+    swapped = lax.ppermute(private_later, CORE, swap)
     packed = pl.pallas_call(
         pack_kernel,
         out_shape=pltpu.VMEM((chips, flat, WIDE), jnp.bfloat16),
-        in_specs=[VMEM, SMEM, SMEM, SMEM],
+        in_specs=[VMEM, SMEM, SMEM],
         out_specs=VMEM,
         scratch_shapes=[pltpu.VMEM((flat, WIDE), jnp.float32)],
         compiler_params=PARAMS,
         name="pack",
-    )(public_logits, owner, partner, ids)
+    )(pltpu.with_memory_space_constraint(public_logits, pltpu.HBM), table, partner)
     own = lax.all_to_all(packed, CHIP, split_axis=0, concat_axis=0, tiled=True)
-    private_logits, swapped, own = (
-        pltpu.with_memory_space_constraint(x, pltpu.VMEM) for x in (private_logits, swapped, own)
-    )
-    sums = chip_sums(private_logits, swapped, own, owner, partner, counts, ids, piece, scale)
+    swapped, own = (pltpu.with_memory_space_constraint(x, pltpu.VMEM) for x in (swapped, own))
+    source = pltpu.with_memory_space_constraint(private_logits, pltpu.HBM)
+    sums = chip_sums(source, swapped, own, table, partner, texts, piece, scale)
     parts = lax.all_to_all(sums, CHIP, split_axis=0, concat_axis=0, tiled=True)
 
     parts = pltpu.with_memory_space_constraint(parts, pltpu.VMEM)
@@ -266,24 +330,28 @@
             pltpu.VMEM((flat, WIDE), jnp.float32),
             pltpu.VMEM((1, LANES), jnp.float32),
         ),
-        in_specs=[SMEM, SMEM, SMEM, VMEM, VMEM, VMEM],
+        in_specs=[SMEM, VMEM, VMEM, VMEM],
         out_specs=(VMEM, VMEM),
         scratch_shapes=[pltpu.VMEM((2, flat, WIDE), jnp.float32)],
         compiler_params=PARAMS,
         name="finish",
-    )(counts, tokens, ids, parts, public_logits, noise)
+    )(table, parts, public_logits, noise)
 
     devices = lax.axis_size(REF_VOC)
     everyone = lax.all_to_all(
         jnp.broadcast_to(stats, (devices, 1, LANES)), REF_VOC, split_axis=0, concat_axis=0, tiled=True
     ).reshape(devices, LANES)
-    levels = everyone[:, 2 * flat : 3 * flat]
-    row_peak = jnp.max(levels, axis=0)
-    total = jnp.sum(everyone[:, :flat] * jnp.exp(levels - row_peak), axis=0)
-    target = jnp.sum(everyone[:, flat : 2 * flat], axis=0)
-    lse = row_peak + jnp.log(total)
-    logprobs = (combined - lse[:, None])[:, :piece].reshape(texts, positions, piece)
-    return (logprobs, (target - lse).reshape(texts, positions))
+    return pl.pallas_call(
+        last_kernel,
+        out_shape=(
+            jax.ShapeDtypeStruct(public_logits.shape, jnp.float32),
+            jax.ShapeDtypeStruct((texts, positions), jnp.float32),
+        ),
+        in_specs=[VMEM, VMEM],
+        out_specs=(VMEM, VMEM),
+        compiler_params=PARAMS,
+        name="last",
+    )(pltpu.with_memory_space_constraint(everyone, pltpu.VMEM), combined)
 
 
 def solution(mesh):

time: 90.5 us -> 83 us (0.917)
  local copies, waits for them, and re-layouts: 6.03 us -> 1.6 us
  waiting for transfers between devices: 5.23 us -> 0.96 us
  Pallas kernels: 5.08 us -> 6.42 us
    unnamed x16 -> x4, local copies, waits for them, and re-layouts: 4.56 us -> 0.01 us
    ppermute x1, waiting for transfers between devices: 5.23 us -> 0.95 us  [body(): partner = lax.ppermute(owner, CORE, swap)]
    ppermute x1, starting transfers between devices: 0.1 us -> 3.29 us  [body(): partner = lax.ppermute(owner, CORE, swap)]
    ppermute x1, starting transfers between devices: 3.29 us -> 0.34 us  [body(): swapped = lax.ppermute(private_later, CORE, swap)]
  transfers between devices with their start and end apart: 2 -> 2, of which waited for: 1 -> 1; matrix products, arithmetic and copies ran while one was open for 0% -> 2% of each run, Pallas kernels for 1% -> 1%
where the time goes in v3:
time: 83 us; the launch traced here: 82.7 us
  blocking collectives  69.5 us (84%)
  Pallas kernels  6.42 us (8%)
  starting transfers between devices  3.63 us (4%)
  local copies, waits for them, and re-layouts  1.6 us (2%)
  waiting for transfers between devices  0.96 us (1%)
    all_to_all x1, blocking collectives, body(): own = lax.all_to_all(packed, CHIP, split_axis=0, concat_axis=0, tiled=True)  25.8 us
    all_to_all x1, blocking collectives, body(): lax.all_to_all(jnp.broadcast_to(stats, (devices, 1, LANES)), REF_VOC, spl...  23.3 us
    all_to_all x1, blocking collectives, body(): parts = lax.all_to_all(sums, CHIP, split_axis=0, concat_axis=0, tiled=True)  20.4 us
    pallas_call x1, Pallas kernels, chip_sums(): pl.pallas_call(sums_kernel(piece, scale), out_shape=pltpu.VMEM((chips, fl...  3.8 us
    ppermute x1, starting transfers between devices, body(): partner = lax.ppermute(owner, CORE, swap)  3.29 us
  transfers between devices with their start and end apart: 2, of which 1 were waited for; matrix products, arithmetic and copies ran while one was open for 2% of the time, Pallas kernels for 1%

profile of v3, /device:TPU:1, one launch (start us, length us, event | category | flops | bytes accessed | tf_op | source)
XLA Modules:
  0.0 82.7 jit_solution(10726251663136726923)
XLA Ops:
  0.6 3.3 %collective-permute-start = (s32[12]{0:T(128)}, s32[12]{0:T(128)S(1)}, u32[]{:S(2)}, u32[]{:S(2)}) collective-permute-start(s32[12]{0:T(128)} %param.9), channel_id=1, source_target_pairs={{0,4},{4,0},{1,5},{5,1},{2,6},{6,2},{3,7},{7,3},{8,12},{12,8},{9,1... | collective-permute-start | bytes 152 | tf_op jit(solution)/shard_map/ppermute | solution.py:308
  3.9 1.0 %collective-permute-done.far.partner = s32[12]{0:T(128)S(1)} collective-permute-done((s32[12]{0:T(128)}, s32[12]{0:T(128)S(1)}, u32[]{:S(2)}, u32[]{:S(2)}) %collective-permute-start) | collective-permute-done | bytes 80 | tf_op jit(solution)/shard_map/ppermute | solution.py:308
  4.9 0.3 collective-permute-start.1
  5.2 0.8 reshape.11
  6.0 0.8 concatenate.3.table
  6.7 1.0 %pack.1 = bf16[32,16,512]{2,1,0:T(8,128)(2,1)S(1)} custom-call(bf16[4,4,501]{2,1,0:T(4,128)(2,1)} %public.3, s32[36]{0:T(128)S(1)} %concatenate.3.table, s32[12]{0:T(128)S(1)} %collective-permute-done.far.partner), custom_call_target="tpu_custom_call" | custom-call | tf_op jit(solution)/shard_map/pack/pallas_call | solution.py:311
  7.7 25.8 %all_to_all.15.own = bf16[32,16,512]{2,1,0:T(8,128)(2,1)S(1)} all-to-all(bf16[32,16,512]{2,1,0:T(8,128)(2,1)S(1)} %pack.1), channel_id=1, replica_groups=mesh['ref_0'=8,'ref_1'=4,'ref_2'=2,'voc'=4] {'ref_0','ref_1'}, dimensions={0} | all-to-all | bytes 1048576 | tf_op jit(solution)/shard_map/all_to_all | solution.py:320
  33.5 0.0 copy-start
  33.5 0.0 copy-start.1
  33.5 0.0 collective-permute-done.1.swapped
  33.5 3.8 %chip_sums.1 = s16[32,16,512]{2,1,0:T(8,128)(2,1)S(1)} custom-call(s32[36]{0:T(128)S(1)} %concatenate.3.table, s32[12]{0:T(128)S(1)} %collective-permute-done.far.partner, bf16[12,4,32064]{2,1,0:T(4,128)(2,1)} %source.1, bf16[12,4,32064]{2,1,0:T(4,128)(2,1)S(1)} %collective-permute-done.1.swapped, bf16[32,16,512]{2,1,0:T(8,128)(2,1)S(1)} %all_to_all.15.own), custom_call_target="tpu_custom_call" | custom-call | tf_op jit(solution)/shard_map/chip_sums/pallas_call | solution.py:197
  37.3 20.4 %all_to_all.16.parts = s16[32,16,512]{2,1,0:T(8,128)(2,1)S(1)} all-to-all(s16[32,16,512]{2,1,0:T(8,128)(2,1)S(1)} %chip_sums.1), channel_id=1, replica_groups=mesh['ref_0'=8,'ref_1'=4,'ref_2'=2,'voc'=4] {'ref_0','ref_1'}, dimensions={0} | all-to-all | bytes 1048576 | tf_op jit(solution)/shard_map/all_to_all | solution.py:324
  57.7 0.0 copy-done
  57.7 0.0 copy-done.1
  57.7 0.8 finish.1
  58.5 0.1 broadcast_in_dim.3
  58.6 23.3 %all_to_all.17 = f32[256,1,128]{2,1,0:T(1,128)S(1)} all-to-all(f32[256,1,128]{2,1,0:T(1,128)S(1)} %broadcast_in_dim.3), channel_id=1, replica_groups=mesh['ref_0'=8,'ref_1'=4,'ref_2'=2,'voc'=4] {'ref_0','ref_1','ref_2','voc'}, dimensions={0} | all-to-all | bytes 262144 | tf_op jit(solution)/shard_map/all_to_all | solution.py:341
  81.9 0.9 %last.1 = (f32[4,4,501]{2,1,0:T(4,128)}, f32[4,4]{1,0:T(4,128)}) custom-call(f32[256,128]{1,0:T(8,128)S(1)} %bitcast.6, f32[16,512]{1,0:T(8,128)S(1)} %get-tuple-element.9.combined), custom_call_target="tpu_custom_call" | custom-call | tf_op jit(solution)/shard_map/last/pallas_call | solution.py:344
Async XLA Ops:
  0.6 4.2 %collective-permute-start = (s32[12]{0:T(128)}, s32[12]{0:T(128)S(1)}, u32[]{:S(2)}, u32[]{:S(2)}) collective-permute-start(s32[12]{0:T(128)} %param.9), channel_id=1, source_target_pairs={{0,4},{4,0},{1,5},{5,1},{2,6},{6,2},{3,7},{7,3},{8,12},{12,8},{9,1... | collective-permute-start | bytes 152 | tf_op jit(solution)/shard_map/ppermute | solution.py:308
  4.9 28.6 %collective-permute-start.1 = (bf16[12,4,32064]{2,1,0:T(4,128)(2,1)}, bf16[12,4,32064]{2,1,0:T(4,128)(2,1)S(1)}, u32[]{:S(2)}, u32[]{:S(2)}) collective-permute-start(bf16[12,4,32064]{2,1,0:T(4,128)(2,1)} %source.1), channel_id=1, source_target_pairs={{0,4},{4,0},{1,5},{5,1},{2,6},{6,2},{3,7},{7,3},{8,12},{12,8},{9,1... | collective-permute-start | bytes 9234440 | tf_op jit(solution)/shard_map/ppermute | solution.py:310
  33.5 24.2 %copy-start = (bf16[4,4,501]{2,1,0:T(4,128)(2,1)S(1)}, bf16[4,4,501]{2,1,0:T(4,128)(2,1)}, u32[]{:S(2)}) copy-start(bf16[4,4,501]{2,1,0:T(4,128)(2,1)} %public.3) | copy-start | bytes 48100
  33.5 24.2 %copy-start.1 = (bf16[4,4,501]{2,1,0:T(4,128)(2,1)S(1)}, bf16[4,4,501]{2,1,0:T(4,128)(2,1)}, u32[]{:S(2)}) copy-start(bf16[4,4,501]{2,1,0:T(4,128)(2,1)} %noise.1) | copy-start | bytes 48100

commit v4 on v3

--- a/solution.py
+++ b/solution.py
@@ -21,7 +21,7 @@
 GROUP = 4
 LEAD = LANES
 
-CHIP_AT, CORE_AT, SHIFT, FIRST, COUNTS, TOKENS, OWNER = 0, 1, 2, 3, 4, 8, 24
+CHIP_AT, CORE_AT, SHIFT, FIRST = range(4)
 
 PARAMS = pltpu.CompilerParams(vmem_limit_bytes=16 << 20)
 SMEM = pl.BlockSpec(memory_space=pltpu.SMEM)
@@ -48,37 +48,57 @@
     return lax.broadcasted_iota(jnp.int32, shape, len(shape) - 1)
 
 
-def pack_kernel(public, table, far, out, flat_rows):
-    texts, positions, piece = public.shape
-    flat = texts * positions
+def rows_of(array, scratch):
+    texts, positions, piece = array.shape
     for t in range(texts):
-        flat_rows[t * positions : (t + 1) * positions, :piece] = public[t].astype(jnp.float32)
-    row = lax.broadcasted_iota(jnp.int32, (flat, LANES), 0)
-    lane = lanes_of((flat, LANES))
-    number = jnp.zeros((flat, LANES), jnp.float32)
-    for t in range(texts):
-        held = jnp.int32(0)
-        for r in range(far.shape[0]):
-            held += jnp.where(table[OWNER + r] == t, 1, 0) + jnp.where(far[r] == t, 1, 0)
-        inside = (row >= t * positions) & (row < (t + 1) * positions)
-        number = jnp.where(inside, held.astype(jnp.float32), number)
-    values = flat_rows[...]
-    tiles = [
-        jnp.where(lane + k * LANES < piece, tile_of(values, k), number) for k in range(TILES)
+        part = slice(t * positions, (t + 1) * positions)
+        scratch[part, :piece] = array[t].astype(jnp.float32)
+    values = scratch[...]
+    lane = lanes_of((texts * positions, LANES))
+    return [
+        jnp.where(lane + k * LANES < piece, tile_of(values, k), 0.0) for k in range(TILES)
     ]
-    tiles = [tile.astype(out.dtype) for tile in turned(tiles, table[SHIFT], lane)]
-    for j in range(out.shape[0]):
+
+
+def column_of(lane, k, shift):
+    return (lane + k * LANES - shift) & (WIDE - 1)
+
+
+def turn_kernel(public, ids, out, scratch):
+    lane = lanes_of((out.shape[0], LANES))
+    for k, tile in enumerate(turned(rows_of(public, scratch), ids[SHIFT], lane)):
+        out[:, k * LANES : (k + 1) * LANES] = tile
+
+
+def mark_kernel(piece, positions):
+    def kernel(one, near, far, ids, out):
+        flat = one.shape[0]
+        row = lax.broadcasted_iota(jnp.int32, (flat, LANES), 0)
+        lane = lanes_of((flat, LANES))
+        number = jnp.zeros((flat, LANES), jnp.float32)
+        for t in range(flat // positions):
+            held = jnp.int32(0)
+            for r in range(near.shape[0]):
+                held += jnp.where(near[r] == t, 1, 0) + jnp.where(far[r] == t, 1, 0)
+            inside = (row >= t * positions) & (row < (t + 1) * positions)
+            number = jnp.where(inside, held.astype(jnp.float32), number)
         for k in range(TILES):
-            out[j, :, k * LANES : (k + 1) * LANES] = tiles[k]
+            tile = one[:, k * LANES : (k + 1) * LANES]
+            tile = jnp.where(column_of(lane, k, ids[SHIFT]) < piece, tile, number)
+            tile = tile.astype(out.dtype)
+            for j in range(out.shape[0]):
+                out[j, :, k * LANES : (k + 1) * LANES] = tile
+
+    return kernel
 
 
 def sums_kernel(piece, scale):
-    def kernel(table, partner, source, swapped, own, out, priv, pub, acc, left, arrived):
+    def kernel(owner, partner, counts, ids, source, swapped, own, out, priv, pub, acc, left, arrived):
         rows, positions, columns = priv.shape
         texts = pub.shape[0]
         chips, flat, _ = own.shape
         groups = chips // GROUP
-        chip, core = table[CHIP_AT], table[CORE_AT]
+        chip, core = ids[CHIP_AT], ids[CORE_AT]
 
         stride = 2 * GROUP * piece
         stride = -(-stride // LANES) * LANES
@@ -119,15 +139,17 @@
             free = jnp.where(j < chip, free, LANES)
             return earlier + jnp.where(lane == free, tile, 0.0)
 
-        earlier = lax.fori_loop(0, chips, widen, jnp.zeros((flat, LANES), jnp.float32))
+        earlier = lax.fori_loop(
+            0, chips, widen, jnp.zeros((flat, LANES), jnp.float32), unroll=4
+        )
         for t in range(texts):
             here = jnp.where(row == t * positions, earlier, 0.0)
-            left[t] = table[COUNTS + t] - jnp.sum(here).astype(jnp.int32)
+            left[t] = counts[t] - jnp.sum(here).astype(jnp.int32)
 
         slots = [[None] * rows, [None] * rows]
         for c in range(2):
             for r in range(rows):
-                text = jnp.where(core == c, table[OWNER + r], partner[r])
+                text = jnp.where(core == c, owner[r], partner[r])
                 still = left[text]
                 left[text] = still - 1
                 slots[c][r] = jnp.where(still > 0, text, texts)
@@ -143,7 +165,7 @@
                     )
             for r in range(rows):
                 for held, text, c in (
-                    (priv, table[OWNER + r], core),
+                    (priv, owner[r], core),
                     (swapped, partner[r], 1 - core),
                 ):
                     slot = jnp.where(c == 0, slots[0][r], slots[1][r])
@@ -191,13 +213,14 @@
     return kernel
 
 
-def chip_sums(private_logits, swapped, own, table, partner, texts, piece, scale):
+def chip_sums(private_logits, swapped, own, owner, partner, counts, ids, piece, scale):
     rows, positions, columns = private_logits.shape
+    texts = counts.shape[0]
     chips, flat, wide = own.shape
     return pl.pallas_call(
         sums_kernel(piece, scale),
         out_shape=pltpu.VMEM((chips, flat, wide), jnp.int16),
-        in_specs=[SMEM, SMEM, HBM, VMEM, VMEM],
+        in_specs=[SMEM, SMEM, SMEM, SMEM, HBM, VMEM, VMEM],
         out_specs=VMEM,
         scratch_shapes=[
             pltpu.VMEM(private_logits.shape, private_logits.dtype),
@@ -208,58 +231,71 @@
         ],
         compiler_params=PARAMS,
         name="chip_sums",
-    )(table, partner, private_logits, swapped, own)
-
-
-def finish_kernel(inverse):
-    def kernel(table, parts, public, noise, combined, stats, base):
+    )(owner, partner, counts, ids, private_logits, swapped, own)
+
+
+def prepare_kernel(inverse):
+    def kernel(public, noise, counts, tokens, ids, base, chosen, level, scale, scratch):
         texts, positions, piece = public.shape
         flat = texts * positions
-        lane = lanes_of((flat, LANES))
-        row = lax.broadcasted_iota(jnp.int32, (flat, LANES), 0)
-        base[...] = jnp.full(base.shape, -jnp.inf, jnp.float32)
-        for t in range(texts):
-            part = slice(t * positions, (t + 1) * positions)
-            base[0, part, :piece] = public[t].astype(jnp.float32)
-            base[1, part, :piece] = noise[t].astype(jnp.float32)
-        scale = jnp.zeros((flat, LANES), jnp.float32)
-        token = jnp.zeros((flat, LANES), jnp.int32)
+        square = (flat, LANES)
+        lane = lanes_of(square)
+        row = lax.broadcasted_iota(jnp.int32, square, 0)
+        factor = jnp.zeros(square, jnp.float32)
+        token = jnp.zeros(square, jnp.int32)
         for t in range(texts):
             inside = (row >= t * positions) & (row < (t + 1) * positions)
-            number = jnp.where(inside, table[COUNTS + t].astype(jnp.float32), 1.0)
-            scale = jnp.where(inside, inverse / (clip_bound * jnp.sqrt(number)), scale)
+            number = jnp.where(inside, counts[t].astype(jnp.float32), 1.0)
+            factor = jnp.where(inside, inverse / (clip_bound * jnp.sqrt(number)), factor)
             for p in range(positions):
-                at = t * positions + p
-                token = jnp.where(row == at, table[TOKENS + at], token)
-        token = token - table[FIRST]
-        total = []
+                token = jnp.where(row == t * positions + p, tokens[t, p], token)
+        scale[...] = factor
+        token = token - ids[FIRST]
+        public_tiles = turned(rows_of(public, scratch.at[0]), ids[SHIFT], lane)
+        noise_tiles = turned(rows_of(noise, scratch.at[1]), ids[SHIFT], lane)
+        top = jnp.full(square, -jnp.inf, jnp.float32)
         for k in range(TILES):
-            tile = parts[0, :, k * LANES : (k + 1) * LANES].astype(jnp.int32)
-            for j in range(1, parts.shape[0]):
-                tile = tile + parts[j, :, k * LANES : (k + 1) * LANES].astype(jnp.int32)
-            total.append(tile.astype(jnp.float32))
-        total = turned_back(total, table[SHIFT], lane)
-        public_tiles = [base[0, :, k * LANES : (k + 1) * LANES] for k in range(TILES)]
-        level = public_tiles[0]
-        for k in range(1, TILES):
-            level = jnp.maximum(level, public_tiles[k])
-        level = jnp.max(level, axis=1, keepdims=True)
-        terms = jnp.zeros((flat, LANES), jnp.float32)
-        picked = jnp.zeros((flat, LANES), jnp.float32)
-        for k in range(TILES):
-            tile = public_tiles[k] + total[k] * scale + base[1, :, k * LANES : (k + 1) * LANES]
-            inside = lane + k * LANES < piece
-            combined[:, k * LANES : (k + 1) * LANES] = tile
-            terms = terms + jnp.where(inside, jnp.exp(tile - level), 0.0)
-            picked = picked + jnp.where((lane + k * LANES == token) & inside, tile, 0.0)
-        terms = jnp.sum(terms, axis=1, keepdims=True)
-        picked = jnp.sum(picked, axis=1, keepdims=True)
-        spread = jnp.where(lane == row, terms, 0.0)
-        spread = spread + jnp.where(lane == row + flat, picked, 0.0)
-        spread = spread + jnp.where(lane == row + 2 * flat, level, 0.0)
-        stats[...] = jnp.sum(spread, axis=0, keepdims=True)
+            column = column_of(lane, k, ids[SHIFT])
+            inside = column < piece
+            part = slice(k * LANES, (k + 1) * LANES)
+            top = jnp.maximum(top, jnp.where(inside, public_tiles[k], -jnp.inf))
+            base[:, part] = jnp.where(inside, public_tiles[k] + noise_tiles[k], -jnp.inf)
+            chosen[:, part] = jnp.where(inside & (column == token), 1.0, 0.0)
+        level[...] = jnp.broadcast_to(jnp.max(top, axis=1, keepdims=True), square)
 
     return kernel
+
+
+def finish_kernel(parts, base, chosen, level, scale, combined, stats):
+    flat = base.shape[0]
+    square = (flat, LANES)
+    lane = lanes_of(square)
+    row = lax.broadcasted_iota(jnp.int32, square, 0)
+    terms = jnp.zeros(square, jnp.float32)
+    picked = jnp.zeros(square, jnp.float32)
+    for k in range(TILES):
+        part = slice(k * LANES, (k + 1) * LANES)
+        total = parts[0, :, part].astype(jnp.int32)
+        for j in range(1, parts.shape[0]):
+            total = total + parts[j, :, part].astype(jnp.int32)
+        tile = base[:, part] + total.astype(jnp.float32) * scale[...]
+        combined[:, part] = tile
+        terms = terms + jnp.exp(tile - level[...])
+        picked = picked + jnp.where(chosen[:, part] > 0.0, tile, 0.0)
+    terms = jnp.sum(terms, axis=1, keepdims=True)
+    picked = jnp.sum(picked, axis=1, keepdims=True)
+    spread = jnp.where(lane == row, terms, 0.0)
+    spread = spread + jnp.where(lane == row + flat, picked, 0.0)
+    spread = spread + jnp.where(lane == row + 2 * flat, level[...], 0.0)
+    stats[...] = jnp.sum(spread, axis=0, keepdims=True)
+
+
+def untwist_kernel(combined, ids, out):
+    lane = lanes_of((combined.shape[0], LANES))
+    values = combined[...]
+    tiles = turned_back([tile_of(values, k) for k in range(TILES)], ids[SHIFT], lane)
+    for k in range(TILES):
+        out[:, k * LANES : (k + 1) * LANES] = tiles[k]
 
 
 def last_kernel(everyone, combined, logprobs, target):
@@ -296,51 +332,77 @@
     scale = float(32767 // (2 * rows * int(clip_bound)))
     place = lax.axis_index(REF)
     first_column = (lax.axis_index("voc") * lax.axis_size(REF) + place) * piece
-    table = jnp.concatenate(
-        [
-            jnp.stack([chip, core, place * piece % LANES, first_column]).astype(jnp.int32),
-            counts,
-            tokens.reshape(-1),
-            owner,
-        ]
+    ids = jnp.stack([chip, core, place * piece % LANES, first_column]).astype(jnp.int32)
+    owner_there, counts_there, tokens_there, public_there = (
+        pltpu.with_memory_space_constraint(x, pltpu.HBM)
+        for x in (owner, counts, tokens, public_logits)
     )
 
     partner = lax.ppermute(owner, CORE, swap)
-    partner, private_later = lax.optimization_barrier((partner, private_logits))
+    one = pl.pallas_call(
+        turn_kernel,
+        out_shape=pltpu.VMEM((flat, WIDE), jnp.float32),
+        in_specs=[VMEM, SMEM],
+        out_specs=VMEM,
+        scratch_shapes=[pltpu.VMEM((flat, WIDE), jnp.float32)],
+        compiler_params=PARAMS,
+        name="turn",
+    )(public_there, ids)
+    partner, private_later, one = lax.optimization_barrier((partner, private_logits, one))
     swapped = lax.ppermute(private_later, CORE, swap)
     packed = pl.pallas_call(
-        pack_kernel,
+        mark_kernel(piece, positions),
         out_shape=pltpu.VMEM((chips, flat, WIDE), jnp.bfloat16),
-        in_specs=[VMEM, SMEM, SMEM],
+        in_specs=[VMEM, SMEM, SMEM, SMEM],
         out_specs=VMEM,
-        scratch_shapes=[pltpu.VMEM((flat, WIDE), jnp.float32)],
-        compiler_params=PARAMS,
-        name="pack",
-    )(pltpu.with_memory_space_constraint(public_logits, pltpu.HBM), table, partner)
+        compiler_params=PARAMS,
+        name="mark",
+    )(one, owner_there, partner, ids)
     own = lax.all_to_all(packed, CHIP, split_axis=0, concat_axis=0, tiled=True)
     swapped, own = (pltpu.with_memory_space_constraint(x, pltpu.VMEM) for x in (swapped, own))
     source = pltpu.with_memory_space_constraint(private_logits, pltpu.HBM)
-    sums = chip_sums(source, swapped, own, table, partner, texts, piece, scale)
+    sums = chip_sums(
+        source, swapped, own, owner_there, partner, counts_there, ids, piece, scale
+    )
+    sums, public_later, noise_later = lax.optimization_barrier((sums, public_logits, noise))
     parts = lax.all_to_all(sums, CHIP, split_axis=0, concat_axis=0, tiled=True)
+    public_later, noise_later = (
+        pltpu.with_memory_space_constraint(x, pltpu.HBM) for x in (public_later, noise_later)
+    )
+    square = pltpu.VMEM((flat, LANES), jnp.float32)
+    long = pltpu.VMEM((flat, WIDE), jnp.float32)
+    base, chosen, level, factor = pl.pallas_call(
+        prepare_kernel(1.0 / scale),
+        out_shape=(long, long, square, square),
+        in_specs=[VMEM, VMEM, SMEM, SMEM, SMEM],
+        out_specs=(VMEM, VMEM, VMEM, VMEM),
+        scratch_shapes=[pltpu.VMEM((2, flat, WIDE), jnp.float32)],
+        compiler_params=PARAMS,
+        name="prepare",
+    )(public_later, noise_later, counts_there, tokens_there, ids)
 
     parts = pltpu.with_memory_space_constraint(parts, pltpu.VMEM)
     combined, stats = pl.pallas_call(
-        finish_kernel(1.0 / scale),
-        out_shape=(
-            pltpu.VMEM((flat, WIDE), jnp.float32),
-            pltpu.VMEM((1, LANES), jnp.float32),
-        ),
-        in_specs=[SMEM, VMEM, VMEM, VMEM],
+        finish_kernel,
+        out_shape=(long, pltpu.VMEM((1, LANES), jnp.float32)),
+        in_specs=[VMEM, VMEM, VMEM, VMEM, VMEM],
         out_specs=(VMEM, VMEM),
-        scratch_shapes=[pltpu.VMEM((2, flat, WIDE), jnp.float32)],
         compiler_params=PARAMS,
         name="finish",
-    )(table, parts, public_logits, noise)
+    )(parts, base, chosen, level, factor)
 
     devices = lax.axis_size(REF_VOC)
     everyone = lax.all_to_all(
         jnp.broadcast_to(stats, (devices, 1, LANES)), REF_VOC, split_axis=0, concat_axis=0, tiled=True
     ).reshape(devices, LANES)
+    combined = pl.pallas_call(
+        untwist_kernel,
+        out_shape=long,
+        in_specs=[VMEM, SMEM],
+        out_specs=VMEM,
+        compiler_params=PARAMS,
+        name="untwist",
+    )(combined, ids)
     return pl.pallas_call(
         last_kernel,
         out_shape=(

time: 83 us -> 82.9 us (level)
  blocking collectives: 69.5 us -> 25.8 us
  waiting for transfers between devices: 0.96 us -> 26.6 us
  starting transfers between devices: 3.63 us -> 19.4 us
  Pallas kernels: 6.42 us -> 9.09 us
  local copies, waits for them, and re-layouts: 1.6 us -> 0.73 us
    all_to_all x2 -> x0, blocking collectives: 43.7 us -> none  [the longest x1 23.3 us: body(): lax.all_to_all(jnp.broadcast_to(stats, (devices, 1, LANES)), REF_VOC, spl...]
    all_to_all x0 -> x2, waiting for transfers between devices: none -> 26.5 us  [the longest x1 14.4 us: body(): parts = lax.all_to_all(sums, CHIP, split_axis=0, concat_axis=0, tiled=True)]
    all_to_all x0 -> x2, starting transfers between devices: none -> 15.8 us  [the longest x1 10.7 us: body(): lax.all_to_all(jnp.broadcast_to(stats, (devices, 1, LANES)), REF_VOC, spl...]
    pallas_call x2 -> x5, Pallas kernels: 1.76 us -> 3.49 us  [the longest x1 1.01 us: body(): pl.pallas_call(prepare_kernel(1.0 / scale), out_shape=(long, long, square...]
    pallas_call x1, Pallas kernels: 3.8 us -> 4.75 us  [chip_sums(): pl.pallas_call(sums_kernel(piece, scale), out_shape=pltpu.VMEM((chips, fl...]
    ppermute x1, waiting for transfers between devices: 0.95 us -> 0.07 us  [body(): partner = lax.ppermute(owner, CORE, swap)]
  transfers between devices with their start and end apart: 2 -> 4, of which waited for: 1 -> 3; matrix products, arithmetic and copies ran while one was open for 2% -> 0% of each run, Pallas kernels for 1% -> 4%
where the time goes in v4:
time: 82.9 us; the launch traced here: 82.4 us
  waiting for transfers between devices  26.6 us (32%)
  blocking collectives  25.8 us (31%)
  starting transfers between devices  19.4 us (23%)
  Pallas kernels  9.09 us (11%)
    all_to_all x1, blocking collectives, body(): own = lax.all_to_all(packed, CHIP, split_axis=0, concat_axis=0, tiled=True)  25.8 us
    all_to_all x1, waiting for transfers between devices, body(): parts = lax.all_to_all(sums, CHIP, split_axis=0, concat_axis=0, tiled=True)  14.4 us
    all_to_all x1, waiting for transfers between devices, body(): lax.all_to_all(jnp.broadcast_to(stats, (devices, 1, LANES)), REF_VOC, spl...  12.1 us
    all_to_all x1, starting transfers between devices, body(): lax.all_to_all(jnp.broadcast_to(stats, (devices, 1, LANES)), REF_VOC, spl...  10.7 us
    all_to_all x1, starting transfers between devices, body(): parts = lax.all_to_all(sums, CHIP, split_axis=0, concat_axis=0, tiled=True)  5.06 us
    pallas_call x1, Pallas kernels, chip_sums(): pl.pallas_call(sums_kernel(piece, scale), out_shape=pltpu.VMEM((chips, fl...  4.75 us
    ppermute x1, starting transfers between devices, body(): partner = lax.ppermute(owner, CORE, swap)  3.29 us
  transfers between devices with their start and end apart: 4, of which 3 were waited for; matrix products, arithmetic and copies ran while one was open for 0% of the time, Pallas kernels for 4%

profile of v4, /device:TPU:1, one launch (start us, length us, event | category | flops | bytes accessed | tf_op | source)
XLA Modules:
  0.0 82.4 jit_solution(8855570587004434911)
XLA Ops:
  0.6 3.3 %collective-permute-start = (s32[12]{0:T(128)}, s32[12]{0:T(128)S(1)}, u32[]{:S(2)}, u32[]{:S(2)}) collective-permute-start(s32[12]{0:T(128)} %owner.1), channel_id=1, source_target_pairs={{0,4},{4,0},{1,5},{5,1},{2,6},{6,2},{3,7},{7,3},{8,12},{12,8},{9,1... | collective-permute-start | bytes 152 | tf_op jit(solution)/shard_map/ppermute | solution.py:341
  3.9 0.1 pad_add_fusion.ids
  4.0 0.8 turn.1.one
  4.8 0.1 collective-permute-done.far.partner
  4.9 0.3 collective-permute-start.1
  5.2 0.9 %mark.1 = bf16[32,16,512]{2,1,0:T(8,128)(2,1)S(1)} custom-call(f32[16,512]{1,0:T(8,128)S(1)} %turn.1.one, s32[12]{0:T(128)} %owner.1, s32[12]{0:T(128)S(1)} %collective-permute-done.far.partner, s32[4]{0:T(128)S(1)} %pad_add_fusion.ids), custom_call_target="tpu_custom_call" | custom-call | tf_op jit(solution)/shard_map/mark/pallas_call | solution.py:353
  6.1 25.8 %all_to_all.15.own = bf16[32,16,512]{2,1,0:T(8,128)(2,1)S(1)} all-to-all(bf16[32,16,512]{2,1,0:T(8,128)(2,1)S(1)} %mark.1), channel_id=1, replica_groups=mesh['ref_0'=8,'ref_1'=4,'ref_2'=2,'voc'=4] {'ref_0','ref_1'}, dimensions={0} | all-to-all | bytes 1048576 | tf_op jit(solution)/shard_map/all_to_all | solution.py:361
  31.9 0.0 collective-permute-done.1.swapped
  31.9 4.7 %chip_sums.1 = s16[32,16,512]{2,1,0:T(8,128)(2,1)} custom-call(s32[12]{0:T(128)} %owner.1, s32[12]{0:T(128)S(1)} %collective-permute-done.far.partner, s32[4]{0:T(128)} %counts.3, s32[4]{0:T(128)S(1)} %pad_add_fusion.ids, bf16[12,4,32064]{2,1,0:T(4,128)(2,1)} %source.1, bf16[12,4,32064]{2,1,0:T(4,128)(2,1)S(1)} %collective-permute-done.1.swapped, ...), custom_call_target="tpu_custom_call" | custom-call | tf_op jit(solution)/shard_map/chip_sums/pallas_call | solution.py:220
  36.6 5.1 %all-to-all-start.1 = ((s16[32,16,512]{2,1,0:T(8,128)(2,1)}), s16[32,16,512]{2,1,0:T(8,128)(2,1)S(1)}, u32[]{:S(2)}, u32[]{:S(2)}) async-start(s16[32,16,512]{2,1,0:T(8,128)(2,1)} %chip_sums.1), calls=%async_computation.1 | async-start | bytes 1048576 | tf_op jit(solution)/shard_map/all_to_all | solution.py:368
  41.7 1.0 %prepare.1 = (f32[16,512]{1,0:T(8,128)S(1)}, f32[16,512]{1,0:T(8,128)S(1)}, f32[16,128]{1,0:T(8,128)S(1)}, f32[16,128]{1,0:T(8,128)S(1)}) custom-call(bf16[4,4,501]{2,1,0:T(4,128)(2,1)} %public.2, bf16[4,4,501]{2,1,0:T(4,128)(2,1)} %noise, s32[4]{0:T(128)} %counts.3, s32[4,4]{1,0:T(4,128)} %tokens.1, s32[4]{0:T(128)S(1)} %pad_add_fusion.ids), custom_call_target="tpu_custom_call" | custom-call | tf_op jit(solution)/shard_map/prepare/pallas_call | solution.py:374
  42.7 14.4 %all-to-all-done.1.parts = s16[32,16,512]{2,1,0:T(8,128)(2,1)S(1)} async-done(((s16[32,16,512]{2,1,0:T(8,128)(2,1)}), s16[32,16,512]{2,1,0:T(8,128)(2,1)S(1)}, u32[]{:S(2)}, u32[]{:S(2)}) %all-to-all-start.1) | async-done | bytes 524320 | tf_op jit(solution)/shard_map/all_to_all | solution.py:368
  57.1 0.2 finish.1
  57.3 0.7 broadcast_in_dim.3
  58.1 10.7 %all-to-all-start.2 = ((f32[256,1,128]{2,1,0:T(1,128)}), f32[256,1,128]{2,1,0:T(1,128)S(1)}, u32[]{:S(2)}, u32[]{:S(2)}) async-start(f32[256,1,128]{2,1,0:T(1,128)} %broadcast_in_dim.3), calls=%async_computation.2 | async-start | bytes 262144 | tf_op jit(solution)/shard_map/all_to_all | solution.py:395
  68.8 0.6 untwist.1.combined
  69.4 12.1 %all-to-all-done.2 = f32[256,1,128]{2,1,0:T(1,128)S(1)} async-done(((f32[256,1,128]{2,1,0:T(1,128)}), f32[256,1,128]{2,1,0:T(1,128)S(1)}, u32[]{:S(2)}, u32[]{:S(2)}) %all-to-all-start.2) | async-done | bytes 131104 | tf_op jit(solution)/shard_map/all_to_all | solution.py:395
  81.5 0.9 %last.1 = (f32[4,4,501]{2,1,0:T(4,128)}, f32[4,4]{1,0:T(4,128)}) custom-call(f32[256,128]{1,0:T(8,128)S(1)} %bitcast.6, f32[16,512]{1,0:T(8,128)S(1)} %untwist.1.combined), custom_call_target="tpu_custom_call" | custom-call | tf_op jit(solution)/shard_map/last/pallas_call | solution.py:406
Async XLA Ops:
  0.6 4.2 %collective-permute-start = (s32[12]{0:T(128)}, s32[12]{0:T(128)S(1)}, u32[]{:S(2)}, u32[]{:S(2)}) collective-permute-start(s32[12]{0:T(128)} %owner.1), channel_id=1, source_target_pairs={{0,4},{4,0},{1,5},{5,1},{2,6},{6,2},{3,7},{7,3},{8,12},{12,8},{9,1... | collective-permute-start | bytes 152 | tf_op jit(solution)/shard_map/ppermute | solution.py:341
  4.9 27.0 %collective-permute-start.1 = (bf16[12,4,32064]{2,1,0:T(4,128)(2,1)}, bf16[12,4,32064]{2,1,0:T(4,128)(2,1)S(1)}, u32[]{:S(2)}, u32[]{:S(2)}) collective-permute-start(bf16[12,4,32064]{2,1,0:T(4,128)(2,1)} %source.1), channel_id=1, source_target_pairs={{0,4},{4,0},{1,5},{5,1},{2,6},{6,2},{3,7},{7,3},{8,12},{12,8},{9,1... | collective-permute-start | bytes 9234440 | tf_op jit(solution)/shard_map/ppermute | solution.py:352
  36.6 20.5 %all-to-all-start.1 = ((s16[32,16,512]{2,1,0:T(8,128)(2,1)}), s16[32,16,512]{2,1,0:T(8,128)(2,1)S(1)}, u32[]{:S(2)}, u32[]{:S(2)}) async-start(s16[32,16,512]{2,1,0:T(8,128)(2,1)} %chip_sums.1), calls=%async_computation.1 | async-start | bytes 1048576 | tf_op jit(solution)/shard_map/all_to_all | solution.py:368
  58.1 23.5 %all-to-all-start.2 = ((f32[256,1,128]{2,1,0:T(1,128)}), f32[256,1,128]{2,1,0:T(1,128)S(1)}, u32[]{:S(2)}, u32[]{:S(2)}) async-start(f32[256,1,128]{2,1,0:T(1,128)} %broadcast_in_dim.3), calls=%async_computation.2 | async-start | bytes 262144 | tf_op jit(solution)/shard_map/all_to_all | solution.py:395

commit v5 on v4

v5 whole, which is shorter than its diff:
```python
import jax
import jax.numpy as jnp
from jax import lax
from jax.experimental import pallas as pl
from jax.experimental.pallas import tpu as pltpu
from jax.sharding import Mesh
from jax.sharding import PartitionSpec as P

REF_VOC = ("ref_0", "ref_1", "ref_2", "voc")
REF = ("ref_0", "ref_1", "ref_2")
CHIP = ("ref_0", "ref_1")
CORE = "ref_2"
VOC_REF = ("voc", "ref_0", "ref_1", "ref_2")

clip_bound = 2.0

LANES = 128
WIDE = 512
TILES = WIDE // LANES
WINDOW = WIDE + LANES
GROUP = 4
LEAD = LANES

PARAMS = pltpu.CompilerParams(vmem_limit_bytes=16 << 20)
SMEM = pl.BlockSpec(memory_space=pltpu.SMEM)
VMEM = pl.BlockSpec(memory_space=pltpu.VMEM)
HBM = pl.BlockSpec(memory_space=pltpu.HBM)


def tile_of(x, k):
    return x[:, k * LANES : (k + 1) * LANES]


def turned(tiles, shift, lane):
    spun = [pltpu.roll(tile, shift, 1) for tile in tiles]
    return [jnp.where(lane >= shift, spun[k], spun[k - 1]) for k in range(TILES)]


def turned_back(tiles, shift, lane):
    back = LANES - shift
    spun = [pltpu.roll(tile, back, 1) for tile in tiles]
    return [jnp.where(lane < back, spun[k], spun[(k + 1) % TILES]) for k in range(TILES)]


def lanes_of(shape):
    return lax.broadcasted_iota(jnp.int32, shape, len(shape) - 1)


def rows_of(array, scratch):
    texts, positions, piece = array.shape
    for t in range(texts):
        part = slice(t * positions, (t + 1) * positions)
        scratch[part, :piece] = array[t].astype(jnp.float32)
    values = scratch[...]
    lane = lanes_of((texts * positions, LANES))
    return [
        jnp.where(lane + k * LANES < piece, tile_of(values, k), 0.0) for k in range(TILES)
    ]


def column_of(lane, k, shift):
    return (lane + k * LANES - shift) & (WIDE - 1)


def place_of(sizes):
    chip = lax.axis_index("ref_0") * sizes[1] + lax.axis_index("ref_1")
    return chip, lax.axis_index("ref_2")


def turn_of(sizes, piece):
    chip, core = place_of(sizes)
    return ((2 * chip + core) * piece) & (LANES - 1)


def inside_text(row, t, positions):
    return (row >= t * positions) & (row < (t + 1) * positions)


def turn_kernel(sizes):
    def kernel(public, near, out, number, scratch):
        texts, positions, piece = public.shape
        square = number.shape
        lane = lanes_of(square)
        row = lax.broadcasted_iota(jnp.int32, square, 0)
        shift = turn_of(sizes, piece)
        for k, tile in enumerate(turned(rows_of(public, scratch), shift, lane)):
            out[:, k * LANES : (k + 1) * LANES] = tile
        many = jnp.zeros(square, jnp.float32)
        for t in range(texts):
            held = jnp.int32(0)
            for r in range(near.shape[0]):
                held += jnp.where(near[r] == t, 1, 0)
            many = jnp.where(inside_text(row, t, positions), held.astype(jnp.float32), many)
        number[...] = many

    return kernel


def mark_kernel(sizes, piece, positions):
    def kernel(one, number, far, out):
        square = number.shape
        row = lax.broadcasted_iota(jnp.int32, square, 0)
        lane = lanes_of(square)
        shift = turn_of(sizes, piece)
        many = number[...]
        for t in range(square[0] // positions):
            held = jnp.sum(jnp.where(far[...] == t, 1.0, 0.0), axis=1, keepdims=True)
            held = jnp.broadcast_to(held, square)
            many = many + jnp.where(inside_text(row, t, positions), held, 0.0)
        for k in range(TILES):
            tile = one[:, k * LANES : (k + 1) * LANES]
            tile = jnp.where(column_of(lane, k, shift) < piece, tile, many)
            tile = tile.astype(out.dtype)
            for j in range(out.shape[0]):
                out[j, :, k * LANES : (k + 1) * LANES] = tile

    return kernel


def sums_kernel(sizes, scale):
    def kernel(
        owner_there, partner_there, counts_there, tokens_there, public_there, noise_there,
        source, swapped, own,
        out, base, chosen, level, factor,
        priv, pub, acc, public, noise, scratch, owner, partner, counts, tokens, left, arrived, small,
    ):
        piece = public.shape[2]
        rows, positions, columns = priv.shape
        texts = pub.shape[0]
        chips, flat, _ = own.shape
        groups = chips // GROUP
        chip, core = place_of(sizes)

        stride = 2 * GROUP * piece
        stride = -(-stride // LANES) * LANES

        def copy_of(i, start, width):
            return pltpu.make_async_copy(
                source.at[:, :, pl.ds(start, width)],
                priv.at[:, :, pl.ds(start, width)],
                arrived.at[i],
            )

        first_chunk = (0, 0, stride + LEAD)
        last_start = LEAD + (groups - 1) * stride
        last_chunk = (groups - 1, last_start, columns - last_start)
        pairs = (
            (owner_there, owner),
            (partner_there, partner),
            (counts_there, counts),
            (tokens_there, tokens),
            (public_there, public),
            (noise_there, noise),
        )
        little = [
            pltpu.make_async_copy(there, here, small.at[i]) for i, (there, here) in enumerate(pairs)
        ]
        for copy in little:
            copy.start()
        copy_of(*first_chunk).start()
        for i in range(1, groups - 1):
            copy_of(i, LEAD + i * stride, stride).start()
        copy_of(*last_chunk).start()

        lane = lanes_of((flat, LANES))
        row = lax.broadcasted_iota(jnp.int32, (flat, LANES), 0)
        last = columns // LANES * LANES

        def begins(j):
            start = (2 * j + core) * piece
            base = start // LANES * LANES
            return pl.multiple_of(base, LANES), start - base

        def widen(j, earlier):
            value = own[j].astype(jnp.float32)
            for t in range(texts):
                part = value[t * positions : (t + 1) * positions]
                pub[t, :, pl.ds(pl.multiple_of(j * WINDOW, LANES), WIDE)] = part
                pub[t, :, pl.ds(pl.multiple_of(j * WINDOW + WIDE, LANES), LANES)] = part[:, :LANES]
            shift = begins(j)[1]
            free = jnp.where(shift == 0, LANES - 1, shift - 1)
            tile = jnp.where(shift == 0, tile_of(value, TILES - 1), tile_of(value, 0))
            free = jnp.where(j < chip, free, LANES)
            return earlier + jnp.where(lane == free, tile, 0.0)

        earlier = lax.fori_loop(
            0, chips, widen, jnp.zeros((flat, LANES), jnp.float32), unroll=4
        )
        for copy in little:
            copy.wait()
        prepare(sizes, scale, public, noise, counts, tokens, scratch, base, chosen, level, factor)

        for t in range(texts):
            here = jnp.where(row == t * positions, earlier, 0.0)
            left[t] = counts[t] - jnp.sum(here).astype(jnp.int32)

        slots = [[None] * rows, [None] * rows]
        for c in range(2):
            for r in range(rows):
                text = jnp.where(core == c, owner[r], partner[r])
                still = left[text]
                left[text] = still - 1
                slots[c][r] = jnp.where(still > 0, text, texts)
        acc[texts] = jnp.zeros(acc.shape[1:], jnp.float32)

        def accumulate(first, many, size):
            places = [first + g for g in range(many)]
            bases = [begins(j)[0] for j in places]
            for t in range(texts):
                for g in range(many):
                    acc[t, :, g * WINDOW : g * WINDOW + size[g]] = jnp.zeros(
                        (positions, size[g]), jnp.float32
                    )
            for r in range(rows):
                for held, text, c in (
                    (priv, owner[r], core),
                    (swapped, partner[r], 1 - core),
                ):
                    slot = jnp.where(c == 0, slots[0][r], slots[1][r])
                    for g, j in enumerate(places):
                        at = pl.multiple_of(j * WINDOW, LANES)
                        value = held[r, :, pl.ds(bases[g], size[g])].astype(jnp.float32)
                        value = value - pub[text, :, pl.ds(at, size[g])]
                        value = jnp.clip(value, -clip_bound, clip_bound)
                        where = slice(g * WINDOW, g * WINDOW + size[g])
                        acc[slot, :, where] = acc[slot, :, where] + value
            for g, j in enumerate(places):
                shift = begins(j)[1]
                tiles = [
                    jnp.concatenate(
                        [
                            acc[t, :, g * WINDOW + k * LANES : g * WINDOW + (k + 1) * LANES]
                            for t in range(texts)
                        ],
                        axis=0,
                    )
                    for k in range(TILES + 1)
                ]
                tiles[0] = jnp.where(lane >= shift, tiles[0], tiles[TILES])
                for k in range(TILES):
                    fixed = jnp.round(tiles[k] * scale).astype(jnp.int32).astype(jnp.int16)
                    out[j, :, k * LANES : (k + 1) * LANES] = fixed

        def some(i, carry):
            copy_of(i, pl.multiple_of(LEAD + i * stride, LANES), stride).wait()
            accumulate(i * GROUP, GROUP, [WINDOW] * GROUP)
            return carry

        copy_of(*first_chunk).wait()
        accumulate(jnp.int32(0), GROUP, [WINDOW] * GROUP)
        lax.fori_loop(1, groups - 1, some, 0)
        copy_of(*last_chunk).wait()
        accumulate(chips - GROUP, GROUP - 1, [WINDOW] * (GROUP - 1))
        for c in range(2):
            start = (2 * chips - 2 + c) * piece // LANES * LANES

            @pl.when(core == c)
            def _():
                accumulate(jnp.int32(chips - 1), 1, [min(WINDOW, columns - start)])

    return kernel


def chip_sums(sizes, owner, partner, counts, tokens, public, noise, source, swapped, own, scale):
    rows, positions, columns = source.shape
    texts = counts.shape[0]
    chips, flat, wide = own.shape
    long = pltpu.VMEM((flat, wide), jnp.float32)
    square = pltpu.VMEM((flat, LANES), jnp.float32)
    return pl.pallas_call(
        sums_kernel(sizes, scale),
        out_shape=(pltpu.VMEM((chips, flat, wide), jnp.int16), long, long, square, square),
        in_specs=[HBM, VMEM, HBM, HBM, HBM, HBM, HBM, VMEM, VMEM],
        out_specs=(VMEM,) * 5,
        scratch_shapes=[
            pltpu.VMEM(source.shape, source.dtype),
            pltpu.VMEM((texts, positions, chips * WINDOW), jnp.float32),
            pltpu.VMEM((texts + 1, positions, GROUP * WINDOW), jnp.float32),
            pltpu.VMEM(public.shape, public.dtype),
            pltpu.VMEM(noise.shape, noise.dtype),
            pltpu.VMEM((2, flat, wide), jnp.float32),
            pltpu.SMEM((rows,), jnp.int32),
            pltpu.SMEM((rows,), jnp.int32),
            pltpu.SMEM((texts,), jnp.int32),
            pltpu.SMEM((texts, positions), jnp.int32),
            pltpu.SMEM((texts,), jnp.int32),
            pltpu.SemaphoreType.DMA((chips // GROUP,)),
            pltpu.SemaphoreType.DMA((6,)),
        ],
        compiler_params=PARAMS,
        name="chip_sums",
    )(owner, partner, counts, tokens, public, noise, source, swapped, own)


def prepare(sizes, scale_of, public, noise, counts, tokens, scratch, base, chosen, level, factor):
    texts, positions, piece = public.shape
    square = (texts * positions, LANES)
    lane = lanes_of(square)
    row = lax.broadcasted_iota(jnp.int32, square, 0)
    shift = turn_of(sizes, piece)
    chip, core = place_of(sizes)
    chips = sizes[0] * sizes[1]
    first = (lax.axis_index("voc") * 2 * chips + 2 * chip + core) * piece
    number = jnp.ones(square, jnp.float32)
    token = jnp.zeros(square, jnp.int32)
    for t in range(texts):
        number = jnp.where(inside_text(row, t, positions), counts[t].astype(jnp.float32), number)
        for p in range(positions):
            token = jnp.where(row == t * positions + p, tokens[t, p] - first, token)
    factor[...] = (1.0 / scale_of) / (clip_bound * jnp.sqrt(number))
    public_tiles = turned(rows_of(public, scratch.at[0]), shift, lane)
    noise_tiles = turned(rows_of(noise, scratch.at[1]), shift, lane)
    top = jnp.full(square, -jnp.inf, jnp.float32)
    for k in range(TILES):
        column = column_of(lane, k, shift)
        inside = column < piece
        part = slice(k * LANES, (k + 1) * LANES)
        top = jnp.maximum(top, jnp.where(inside, public_tiles[k], -jnp.inf))
        base[:, part] = jnp.where(inside, public_tiles[k] + noise_tiles[k], -jnp.inf)
        chosen[:, part] = jnp.where(inside & (column == token), 1.0, 0.0)
    level[...] = jnp.broadcast_to(jnp.max(top, axis=1, keepdims=True), square)


def finish_kernel(parts, base, chosen, level, scale, combined, stats):
    flat = base.shape[0]
    square = (flat, LANES)
    lane = lanes_of(square)
    row = lax.broadcasted_iota(jnp.int32, square, 0)
    terms = jnp.zeros(square, jnp.float32)
    picked = jnp.zeros(square, jnp.float32)
    for k in range(TILES):
        part = slice(k * LANES, (k + 1) * LANES)
        total = parts[0, :, part].astype(jnp.int32)
        for j in range(1, parts.shape[0]):
            total = total + parts[j, :, part].astype(jnp.int32)
        tile = base[:, part] + total.astype(jnp.float32) * scale[...]
        combined[:, part] = tile
        terms = terms + jnp.exp(tile - level[...])
        picked = picked + jnp.where(chosen[:, part] > 0.0, tile, 0.0)
    terms = jnp.sum(terms, axis=1, keepdims=True)
    picked = jnp.sum(picked, axis=1, keepdims=True)
    spread = jnp.where(lane == row, terms, 0.0)
    spread = spread + jnp.where(lane == row + flat, picked, 0.0)
    spread = spread + jnp.where(lane == row + 2 * flat, level[...], 0.0)
    stats[...] = jnp.sum(spread, axis=0, keepdims=True)


def last_kernel(sizes):
    def kernel(everyone, combined, logprobs, target, natural):
        texts, positions, piece = logprobs.shape
        flat = texts * positions
        values = everyone[...]
        lane = lanes_of((1, LANES))
        level = jnp.max(values, axis=0, keepdims=True)
        weight = pltpu.roll(jnp.exp(values - level), LANES - 2 * flat, 1)
        total = jnp.sum(values * weight, axis=0, keepdims=True)
        picked = pltpu.roll(jnp.sum(values, axis=0, keepdims=True), LANES - flat, 1)
        level = pltpu.roll(level, LANES - 2 * flat, 1)
        own = lane < flat
        lse = jnp.where(own, level + jnp.log(jnp.where(own, total, 1.0)), 0.0)
        picked = picked - lse
        square = (flat, LANES)
        mine = lanes_of(square) == lax.broadcasted_iota(jnp.int32, square, 0)
        column = jnp.sum(jnp.where(mine, jnp.broadcast_to(lse, square), 0.0), axis=1, keepdims=True)
        tiles = [combined[:, k * LANES : (k + 1) * LANES] - column for k in range(TILES)]
        for k, tile in enumerate(turned_back(tiles, turn_of(sizes, piece), lanes_of(square))):
            natural[:, k * LANES : (k + 1) * LANES] = tile
        shifted = natural[:, :piece]
        for t in range(texts):
            logprobs[t] = shifted[t * positions : (t + 1) * positions]
        for t in range(texts):
            turn = picked if t == 0 else pltpu.roll(picked, LANES - t * positions, 1)
            target[t : t + 1, :] = turn[:, :positions]

    return kernel


def body(private_logits, public_logits, noise, owner, counts, tokens):
    texts, positions, piece = public_logits.shape
    rows = owner.shape[0]
    flat = texts * positions
    sizes = (lax.axis_size("ref_0"), lax.axis_size("ref_1"))
    chips = sizes[0] * sizes[1]
    swap = [(0, 1), (1, 0)]
    scale = float(32767 // (2 * rows * int(clip_bound)))
    square = pltpu.VMEM((flat, LANES), jnp.float32)
    long = pltpu.VMEM((flat, WIDE), jnp.float32)
    owner_there, counts_there, tokens_there, public_there, noise_there, private_there = (
        pltpu.with_memory_space_constraint(x, pltpu.HBM)
        for x in (owner, counts, tokens, public_logits, noise, private_logits)
    )

    partner = lax.ppermute(owner, CORE, swap)
    one, number = pl.pallas_call(
        turn_kernel(sizes),
        out_shape=(long, square),
        in_specs=[VMEM, SMEM],
        out_specs=(VMEM, VMEM),
        scratch_shapes=[pltpu.VMEM((flat, WIDE), jnp.float32)],
        compiler_params=PARAMS,
        name="turn",
    )(public_there, owner_there)
    partner, private_later, one = lax.optimization_barrier((partner, private_logits, one))
    swapped = lax.ppermute(private_later, CORE, swap)
    packed = pl.pallas_call(
        mark_kernel(sizes, piece, positions),
        out_shape=pltpu.VMEM((chips, flat, WIDE), jnp.bfloat16),
        in_specs=[VMEM, VMEM, VMEM],
        out_specs=VMEM,
        compiler_params=PARAMS,
        name="mark",
    )(one, number, partner.reshape(1, rows))
    own = lax.all_to_all(packed, CHIP, split_axis=0, concat_axis=0, tiled=True)
    swapped, own, partner = (
        pltpu.with_memory_space_constraint(x, pltpu.VMEM) for x in (swapped, own, partner)
    )
    sums, base, chosen, level, factor = chip_sums(
        sizes, owner_there, partner, counts_there, tokens_there, public_there, noise_there,
        private_there, swapped, own, scale,
    )
    parts = lax.all_to_all(sums, CHIP, split_axis=0, concat_axis=0, tiled=True)
    parts = pltpu.with_memory_space_constraint(parts, pltpu.VMEM)
    combined, stats = pl.pallas_call(
        finish_kernel,
        out_shape=(long, pltpu.VMEM((1, LANES), jnp.float32)),
        in_specs=[VMEM] * 5,
        out_specs=(VMEM, VMEM),
        compiler_params=PARAMS,
        name="finish",
    )(parts, base, chosen, level, factor)

    devices = lax.axis_size(REF_VOC)
    everyone = lax.all_to_all(
        jnp.broadcast_to(stats, (devices, 1, LANES)), REF_VOC, split_axis=0, concat_axis=0, tiled=True
    ).reshape(devices, LANES)
    return pl.pallas_call(
        last_kernel(sizes),
        out_shape=(
            jax.ShapeDtypeStruct(public_logits.shape, jnp.float32),
            jax.ShapeDtypeStruct((texts, positions), jnp.float32),
        ),
        in_specs=[VMEM, VMEM],
        out_specs=(VMEM, VMEM),
        scratch_shapes=[pltpu.VMEM((flat, WIDE), jnp.float32)],
        compiler_params=PARAMS,
        name="last",
    )(pltpu.with_memory_space_constraint(everyone, pltpu.VMEM), combined)


def solution(mesh):
    finer = Mesh(
        mesh.devices.reshape(8, 4, 2, mesh.shape["voc"]), ("ref_0", "ref_1", "ref_2", "voc")
    )
    placed = (P(REF, None, "voc"), P(None, None, VOC_REF), P(None, None, VOC_REF), P(REF), P(), P())
    return jax.shard_map(
        body, mesh=finer, in_specs=placed, out_specs=(P(None, None, VOC_REF), P()), check_vma=False
    )
```

time: 82.9 us -> 80.6 us (0.972)
  blocking collectives: 25.8 us -> 69.4 us
  waiting for transfers between devices: 26.6 us -> 0.07 us
  starting transfers between devices: 19.4 us -> 3.63 us
  Pallas kernels: 9.09 us -> 6.48 us
    all_to_all x0 -> x2, blocking collectives: none -> 43.6 us  [the longest x1 23.3 us: body(): lax.all_to_all(jnp.broadcast_to(stats, (devices, 1, LANES)), REF_VOC, spl...]
    all_to_all x2 -> x0, waiting for transfers between devices: 26.5 us -> none  [the longest x1 14.4 us: body(): parts = lax.all_to_all(sums, CHIP, split_axis=0, concat_axis=0, tiled=True)]
    all_to_all x2 -> x0, starting transfers between devices: 15.8 us -> none  [the longest x1 10.7 us: body(): lax.all_to_all(jnp.broadcast_to(stats, (devices, 1, LANES)), REF_VOC, spl...]
    pallas_call x6 -> x4, Pallas kernels: 8.9 us -> 6.3 us  [the longest x1 4.3 us: chip_sums(): pl.pallas_call(sums_kernel(sizes, scale), out_shape=(pltpu.VMEM((chips, f...]
  transfers between devices with their start and end apart: 4 -> 2, of which waited for: 3 -> 1; matrix products, arithmetic and copies ran while one was open for 0% -> 0% of each run, Pallas kernels for 4% -> 1%
where the time goes in v5:
time: 80.6 us; the launch traced here: 80.3 us
  blocking collectives  69.4 us (86%)
  Pallas kernels  6.48 us (8%)
  starting transfers between devices  3.63 us (5%)
    all_to_all x1, blocking collectives, body(): own = lax.all_to_all(packed, CHIP, split_axis=0, concat_axis=0, tiled=True)  25.8 us
    all_to_all x1, blocking collectives, body(): lax.all_to_all(jnp.broadcast_to(stats, (devices, 1, LANES)), REF_VOC, spl...  23.3 us
    all_to_all x1, blocking collectives, body(): parts = lax.all_to_all(sums, CHIP, split_axis=0, concat_axis=0, tiled=True)  20.3 us
    pallas_call x1, Pallas kernels, chip_sums(): pl.pallas_call(sums_kernel(sizes, scale), out_shape=(pltpu.VMEM((chips, f...  4.3 us
    ppermute x1, starting transfers between devices, body(): partner = lax.ppermute(owner, CORE, swap)  3.29 us
  transfers between devices with their start and end apart: 2, of which 1 were waited for; matrix products, arithmetic and copies ran while one was open for 0% of the time, Pallas kernels for 1%

profile of v5, /device:TPU:1, one launch (start us, length us, event | category | flops | bytes accessed | tf_op | source)
XLA Modules:
  0.0 80.3 jit_solution(5415755864265975726)
XLA Ops:
  0.6 3.3 %collective-permute-start = (s32[12]{0:T(128)}, s32[12]{0:T(128)S(1)}, u32[]{:S(2)}, u32[]{:S(2)}) collective-permute-start(s32[12]{0:T(128)} %owner_there.1), channel_id=1, source_target_pairs={{0,4},{4,0},{1,5},{5,1},{2,6},{6,2},{3,7},{7,3},{8,12},{12,8},{9,1... | collective-permute-start | bytes 152 | tf_op jit(solution)/shard_map/ppermute | solution.py:393
  3.9 0.9 %turn.1 = (f32[16,512]{1,0:T(8,128)S(1)}, f32[16,128]{1,0:T(8,128)S(1)}) custom-call(bf16[4,4,501]{2,1,0:T(4,128)(2,1)} %public_there.1, s32[12]{0:T(128)} %owner_there.1), custom_call_target="tpu_custom_call" | custom-call | tf_op jit(solution)/shard_map/turn/pallas_call | solution.py:394
  4.8 0.1 collective-permute-done.partner_there
  4.9 0.3 collective-permute-start.1
  5.2 0.2 mark.1
  5.4 25.8 %all_to_all.15.own = bf16[32,16,512]{2,1,0:T(8,128)(2,1)S(1)} all-to-all(bf16[32,16,512]{2,1,0:T(8,128)(2,1)S(1)} %mark.1), channel_id=1, replica_groups=mesh['ref_0'=8,'ref_1'=4,'ref_2'=2,'voc'=4] {'ref_0','ref_1'}, dimensions={0} | all-to-all | bytes 1048576 | tf_op jit(solution)/shard_map/all_to_all | solution.py:413
  31.2 0.0 collective-permute-done.1.swapped
  31.2 4.3 %chip_sums.1 = (s16[32,16,512]{2,1,0:T(8,128)(2,1)S(1)}, f32[16,512]{1,0:T(8,128)S(1)}, f32[16,512]{1,0:T(8,128)S(1)}, f32[16,128]{1,0:T(8,128)S(1)}, f32[16,128]{1,0:T(8,128)S(1)}) custom-call(s32[12]{0:T(128)} %owner_there.1, s32[12]{0:T(128)S(1)} %collective-permute-done.partner_there, s32[4]{0:T(128)} %counts_there.1, s32[4,4]{1,0:T(4,128)} %tokens_there.1, ...), custom_call_target="tpu_custom_call" | custom-call | tf_op jit(solution)/shard_map/chip_sums/pallas_call | solution.py:270
  35.5 20.3 %all_to_all.16.parts = s16[32,16,512]{2,1,0:T(8,128)(2,1)S(1)} all-to-all(s16[32,16,512]{2,1,0:T(8,128)(2,1)S(1)} %get-tuple-element.19), channel_id=1, replica_groups=mesh['ref_0'=8,'ref_1'=4,'ref_2'=2,'voc'=4] {'ref_0','ref_1'}, dimensions={0} | all-to-all | bytes 1048576 | tf_op jit(solution)/shard_map/all_to_all | solution.py:421
  55.8 0.2 finish.1
  56.0 0.1 broadcast_in_dim.3
  56.1 23.3 %all_to_all.17 = f32[256,1,128]{2,1,0:T(1,128)S(1)} all-to-all(f32[256,1,128]{2,1,0:T(1,128)S(1)} %broadcast_in_dim.3), channel_id=1, replica_groups=mesh['ref_0'=8,'ref_1'=4,'ref_2'=2,'voc'=4] {'ref_0','ref_1','ref_2','voc'}, dimensions={0} | all-to-all | bytes 262144 | tf_op jit(solution)/shard_map/all_to_all | solution.py:433
  79.4 0.9 %last.1 = (f32[4,4,501]{2,1,0:T(4,128)}, f32[4,4]{1,0:T(4,128)}) custom-call(f32[256,128]{1,0:T(8,128)S(1)} %bitcast.3, f32[16,512]{1,0:T(8,128)S(1)} %get-tuple-element.25.combined), custom_call_target="tpu_custom_call" | custom-call | tf_op jit(solution)/shard_map/last/pallas_call | solution.py:436
Async XLA Ops:
  0.6 4.2 %collective-permute-start = (s32[12]{0:T(128)}, s32[12]{0:T(128)S(1)}, u32[]{:S(2)}, u32[]{:S(2)}) collective-permute-start(s32[12]{0:T(128)} %owner_there.1), channel_id=1, source_target_pairs={{0,4},{4,0},{1,5},{5,1},{2,6},{6,2},{3,7},{7,3},{8,12},{12,8},{9,1... | collective-permute-start | bytes 152 | tf_op jit(solution)/shard_map/ppermute | solution.py:393
  4.9 26.3 %collective-permute-start.1 = (bf16[12,4,32064]{2,1,0:T(4,128)(2,1)}, bf16[12,4,32064]{2,1,0:T(4,128)(2,1)S(1)}, u32[]{:S(2)}, u32[]{:S(2)}) collective-permute-start(bf16[12,4,32064]{2,1,0:T(4,128)(2,1)} %source.1), channel_id=1, source_target_pairs={{0,4},{4,0},{1,5},{5,1},{2,6},{6,2},{3,7},{7,3},{8,12},{12,8},{9,1... | collective-permute-start | bytes 9234440 | tf_op jit(solution)/shard_map/ppermute | solution.py:404

commit v6 on v5

--- a/solution.py
+++ b/solution.py
@@ -19,6 +19,7 @@
 TILES = WIDE // LANES
 WINDOW = WIDE + LANES
 GROUP = 4
+AROUND = (2, 1, 3, 0)
 LEAD = LANES
 
 PARAMS = pltpu.CompilerParams(vmem_limit_bytes=16 << 20)
@@ -117,21 +118,111 @@
     return kernel
 
 
-def sums_kernel(sizes, scale):
+class Rows:
+    def __init__(self, plan, priv, swapped):
+        rows, self.positions, self.columns = priv.shape
+        self.entries = []
+        for h, held in enumerate((priv, swapped)):
+            for r in range(rows):
+                at = h * rows + r
+                self.entries.append((held, r, plan[at], plan[2 * rows + at]))
+
+    def clipped(self, entry, start, pub, at, width):
+        held, r, text, _ = entry
+        value = held[r, :, pl.ds(start, width)].astype(jnp.float32)
+        value = value - pub[text, :, pl.ds(at, width)]
+        return jnp.clip(value, -clip_bound, clip_bound)
+
+
+def begins(j, core, piece):
+    start = (2 * j + core) * piece
+    base = start // LANES * LANES
+    return pl.multiple_of(base, LANES), start - base
+
+
+def widen_into(pub, place, value, positions):
+    for t in range(pub.shape[0]):
+        part = value[t * positions : (t + 1) * positions]
+        pub[t, :, pl.ds(pl.multiple_of(place * WINDOW, LANES), WIDE)] = part
+        pub[t, :, pl.ds(pl.multiple_of(place * WINDOW + WIDE, LANES), LANES)] = part[:, :LANES]
+
+
+def sum_windows(rows, pub, acc, core, piece, scale, windows, may_end=None):
+    texts = pub.shape[0]
+    sizes = [WIDE if may_end is not None and g in may_end else WINDOW for g in range(len(windows))]
+    bases = [begins(j, core, piece)[0] for j, _, _ in windows]
+    at = [pl.multiple_of(place * WINDOW, LANES) for _, place, _ in windows]
+    for t in range(texts):
+        for g, size in enumerate(sizes):
+            acc[t, :, g * WINDOW : g * WINDOW + size] = jnp.zeros((rows.positions, size), jnp.float32)
+    for entry in rows.entries:
+        slot = entry[3]
+        for g, size in enumerate(sizes):
+            value = rows.clipped(entry, bases[g], pub, at[g], size)
+            where = slice(g * WINDOW, g * WINDOW + size)
+            acc[slot, :, where] = acc[slot, :, where] + value
+
+    def edge(g, width):
+        sums = [jnp.zeros((rows.positions, width), jnp.float32) for _ in range(texts)]
+        start = pl.multiple_of(bases[g] + WIDE, LANES)
+        for entry in rows.entries:
+            value = rows.clipped(entry, start, pub, pl.multiple_of(at[g] + WIDE, LANES), width)
+            for t in range(texts):
+                sums[t] = sums[t] + jnp.where(entry[3] == t, value, 0.0)
+        for t in range(texts):
+            acc[t, :, g * WINDOW + WIDE : g * WINDOW + WIDE + width] = sums[t]
+
+    for g in may_end or ():
+        rest = rows.columns % LANES
+        ends = bases[g] + WINDOW > rows.columns
+
+        @pl.when(ends)
+        def _():
+            edge(g, rest)
+
+        @pl.when(jnp.logical_not(ends))
+        def _():
+            edge(g, LANES)
+
+    lane = lanes_of((texts * rows.positions, LANES))
+    for g, (j, _, store) in enumerate(windows):
+        shift = begins(j, core, piece)[1]
+        tiles = [
+            jnp.concatenate(
+                [acc[t, :, g * WINDOW + k * LANES : g * WINDOW + (k + 1) * LANES] for t in range(texts)],
+                axis=0,
+            )
+            for k in range(TILES + 1)
+        ]
+        tiles[0] = jnp.where(lane >= shift, tiles[0], tiles[TILES])
+        for k in range(TILES):
+            fixed = jnp.round(tiles[k] * scale).astype(jnp.int32).astype(jnp.int16)
+            store(slice(k * LANES, (k + 1) * LANES), fixed)
+
+
+def storing(out, index):
+    def store(part, value):
+        out[index, :, part] = value
+
+    return store
+
+
+def away_kernel(sizes, scale, piece):
     def kernel(
-        owner_there, partner_there, counts_there, tokens_there, public_there, noise_there,
-        source, swapped, own,
-        out, base, chosen, level, factor,
-        priv, pub, acc, public, noise, scratch, owner, partner, counts, tokens, left, arrived, small,
+        owner_there, partner_there, counts_there, source, swapped, own,
+        away_0, away_1, away_2, priv, plan,
+        pub, acc, owner, partner, counts, left, arrived, small,
     ):
-        piece = public.shape[2]
         rows, positions, columns = priv.shape
         texts = pub.shape[0]
         chips, flat, _ = own.shape
-        groups = chips // GROUP
+        lines, beside = sizes
         chip, core = place_of(sizes)
-
-        stride = 2 * GROUP * piece
+        mine = lax.axis_index("ref_1")
+        lane = lanes_of((flat, LANES))
+        row = lax.broadcasted_iota(jnp.int32, (flat, LANES), 0)
+
+        stride = 2 * beside * piece
         stride = -(-stride // LANES) * LANES
 
         def copy_of(i, start, width):
@@ -142,154 +233,102 @@
             )
 
         first_chunk = (0, 0, stride + LEAD)
-        last_start = LEAD + (groups - 1) * stride
-        last_chunk = (groups - 1, last_start, columns - last_start)
-        pairs = (
-            (owner_there, owner),
-            (partner_there, partner),
-            (counts_there, counts),
-            (tokens_there, tokens),
-            (public_there, public),
-            (noise_there, noise),
-        )
+        last_start = LEAD + (lines - 1) * stride
+        last_chunk = (lines - 1, last_start, columns - last_start)
+        pairs = ((owner_there, owner), (partner_there, partner), (counts_there, counts))
         little = [
             pltpu.make_async_copy(there, here, small.at[i]) for i, (there, here) in enumerate(pairs)
         ]
         for copy in little:
             copy.start()
         copy_of(*first_chunk).start()
-        for i in range(1, groups - 1):
+        for i in range(1, lines - 1):
             copy_of(i, LEAD + i * stride, stride).start()
         copy_of(*last_chunk).start()
 
-        lane = lanes_of((flat, LANES))
-        row = lax.broadcasted_iota(jnp.int32, (flat, LANES), 0)
-        last = columns // LANES * LANES
-
-        def begins(j):
-            start = (2 * j + core) * piece
-            base = start // LANES * LANES
-            return pl.multiple_of(base, LANES), start - base
-
-        def widen(j, earlier):
-            value = own[j].astype(jnp.float32)
-            for t in range(texts):
-                part = value[t * positions : (t + 1) * positions]
-                pub[t, :, pl.ds(pl.multiple_of(j * WINDOW, LANES), WIDE)] = part
-                pub[t, :, pl.ds(pl.multiple_of(j * WINDOW + WIDE, LANES), LANES)] = part[:, :LANES]
-            shift = begins(j)[1]
-            free = jnp.where(shift == 0, LANES - 1, shift - 1)
-            tile = jnp.where(shift == 0, tile_of(value, TILES - 1), tile_of(value, 0))
-            free = jnp.where(j < chip, free, LANES)
-            return earlier + jnp.where(lane == free, tile, 0.0)
-
-        earlier = lax.fori_loop(
-            0, chips, widen, jnp.zeros((flat, LANES), jnp.float32), unroll=4
-        )
+        def widen(i, earlier):
+            for n in range(beside):
+                j = beside * i + (mine ^ AROUND[n])
+                value = own[j].astype(jnp.float32)
+                if n < beside - 1:
+                    widen_into(pub, i * (beside - 1) + n, value, positions)
+                shift = begins(j, core, piece)[1]
+                free = jnp.where(shift == 0, LANES - 1, shift - 1)
+                tile = jnp.where(shift == 0, tile_of(value, TILES - 1), tile_of(value, 0))
+                free = jnp.where(j < chip, free, LANES)
+                earlier = earlier + jnp.where(lane == free, tile, 0.0)
+            return earlier
+
+        earlier = lax.fori_loop(0, lines, widen, jnp.zeros((flat, LANES), jnp.float32))
         for copy in little:
             copy.wait()
-        prepare(sizes, scale, public, noise, counts, tokens, scratch, base, chosen, level, factor)
-
         for t in range(texts):
             here = jnp.where(row == t * positions, earlier, 0.0)
             left[t] = counts[t] - jnp.sum(here).astype(jnp.int32)
 
-        slots = [[None] * rows, [None] * rows]
         for c in range(2):
             for r in range(rows):
                 text = jnp.where(core == c, owner[r], partner[r])
                 still = left[text]
                 left[text] = still - 1
-                slots[c][r] = jnp.where(still > 0, text, texts)
+                at = jnp.where(core == c, r, rows + r)
+                plan[at] = text
+                plan[2 * rows + at] = jnp.where(still > 0, text, texts)
         acc[texts] = jnp.zeros(acc.shape[1:], jnp.float32)
-
-        def accumulate(first, many, size):
-            places = [first + g for g in range(many)]
-            bases = [begins(j)[0] for j in places]
-            for t in range(texts):
-                for g in range(many):
-                    acc[t, :, g * WINDOW : g * WINDOW + size[g]] = jnp.zeros(
-                        (positions, size[g]), jnp.float32
-                    )
-            for r in range(rows):
-                for held, text, c in (
-                    (priv, owner[r], core),
-                    (swapped, partner[r], 1 - core),
-                ):
-                    slot = jnp.where(c == 0, slots[0][r], slots[1][r])
-                    for g, j in enumerate(places):
-                        at = pl.multiple_of(j * WINDOW, LANES)
-                        value = held[r, :, pl.ds(bases[g], size[g])].astype(jnp.float32)
-                        value = value - pub[text, :, pl.ds(at, size[g])]
-                        value = jnp.clip(value, -clip_bound, clip_bound)
-                        where = slice(g * WINDOW, g * WINDOW + size[g])
-                        acc[slot, :, where] = acc[slot, :, where] + value
-            for g, j in enumerate(places):
-                shift = begins(j)[1]
-                tiles = [
-                    jnp.concatenate(
-                        [
-                            acc[t, :, g * WINDOW + k * LANES : g * WINDOW + (k + 1) * LANES]
-                            for t in range(texts)
-                        ],
-                        axis=0,
-                    )
-                    for k in range(TILES + 1)
-                ]
-                tiles[0] = jnp.where(lane >= shift, tiles[0], tiles[TILES])
-                for k in range(TILES):
-                    fixed = jnp.round(tiles[k] * scale).astype(jnp.int32).astype(jnp.int16)
-                    out[j, :, k * LANES : (k + 1) * LANES] = fixed
+        held = Rows(plan, priv, swapped)
+        outs = (away_0, away_1, away_2)
+
+        def line(i, may_end=None):
+            windows = [
+                (beside * i + (mine ^ AROUND[n]), i * (beside - 1) + n, storing(outs[n], i))
+                for n in range(beside - 1)
+            ]
+            sum_windows(held, pub, acc, core, piece, scale, windows, may_end)
 
         def some(i, carry):
             copy_of(i, pl.multiple_of(LEAD + i * stride, LANES), stride).wait()
-            accumulate(i * GROUP, GROUP, [WINDOW] * GROUP)
+            line(i)
             return carry
 
         copy_of(*first_chunk).wait()
-        accumulate(jnp.int32(0), GROUP, [WINDOW] * GROUP)
-        lax.fori_loop(1, groups - 1, some, 0)
+        line(jnp.int32(0))
+        lax.fori_loop(1, lines - 1, some, 0)
         copy_of(*last_chunk).wait()
-        accumulate(chips - GROUP, GROUP - 1, [WINDOW] * (GROUP - 1))
-        for c in range(2):
-            start = (2 * chips - 2 + c) * piece // LANES * LANES
-
-            @pl.when(core == c)
-            def _():
-                accumulate(jnp.int32(chips - 1), 1, [min(WINDOW, columns - start)])
+        line(jnp.int32(lines - 1), range(beside - 1))
 
     return kernel
 
 
-def chip_sums(sizes, owner, partner, counts, tokens, public, noise, source, swapped, own, scale):
-    rows, positions, columns = source.shape
-    texts = counts.shape[0]
-    chips, flat, wide = own.shape
-    long = pltpu.VMEM((flat, wide), jnp.float32)
-    square = pltpu.VMEM((flat, LANES), jnp.float32)
-    return pl.pallas_call(
-        sums_kernel(sizes, scale),
-        out_shape=(pltpu.VMEM((chips, flat, wide), jnp.int16), long, long, square, square),
-        in_specs=[HBM, VMEM, HBM, HBM, HBM, HBM, HBM, VMEM, VMEM],
-        out_specs=(VMEM,) * 5,
-        scratch_shapes=[
-            pltpu.VMEM(source.shape, source.dtype),
-            pltpu.VMEM((texts, positions, chips * WINDOW), jnp.float32),
-            pltpu.VMEM((texts + 1, positions, GROUP * WINDOW), jnp.float32),
-            pltpu.VMEM(public.shape, public.dtype),
-            pltpu.VMEM(noise.shape, noise.dtype),
-            pltpu.VMEM((2, flat, wide), jnp.float32),
-            pltpu.SMEM((rows,), jnp.int32),
-            pltpu.SMEM((rows,), jnp.int32),
-            pltpu.SMEM((texts,), jnp.int32),
-            pltpu.SMEM((texts, positions), jnp.int32),
-            pltpu.SMEM((texts,), jnp.int32),
-            pltpu.SemaphoreType.DMA((chips // GROUP,)),
-            pltpu.SemaphoreType.DMA((6,)),
-        ],
-        compiler_params=PARAMS,
-        name="chip_sums",
-    )(owner, partner, counts, tokens, public, noise, source, swapped, own)
+def own_kernel(sizes, scale, piece):
+    def kernel(
+        public, noise, counts, tokens, plan, priv, swapped, own,
+        out, base, chosen, level, factor,
+        pub, acc, scratch,
+    ):
+        texts = pub.shape[0]
+        lines, beside = sizes
+        chip, core = place_of(sizes)
+        mine = lax.axis_index("ref_1")
+        held = Rows(plan, priv, swapped)
+        for i in range(lines):
+            widen_into(pub, i, own[beside * i + mine].astype(jnp.float32), held.positions)
+        acc[texts] = jnp.zeros(acc.shape[1:], jnp.float32)
+        for first in range(0, lines, GROUP):
+            windows = [(beside * i + mine, i, storing(out, i)) for i in range(first, first + GROUP)]
+            may_end = (GROUP - 1,) if first + GROUP == lines else None
+            sum_windows(held, pub, acc, core, piece, scale, windows, may_end)
+        prepare(sizes, scale / beside, public, noise, counts, tokens, scratch, base, chosen, level, factor)
+
+    return kernel
+
+
+def join_kernel(a, b, c, d, out):
+    for i in range(out.shape[0]):
+        total = (a[i].astype(jnp.int32) + b[i].astype(jnp.int32)) + (
+            c[i].astype(jnp.int32) + d[i].astype(jnp.int32)
+        )
+        total = jnp.round(total.astype(jnp.float32) * 0.25)
+        out[i] = total.astype(jnp.int32).astype(jnp.int16)
 
 
 def prepare(sizes, scale_of, public, noise, counts, tokens, scratch, base, chosen, level, factor):
@@ -414,11 +453,57 @@
     swapped, own, partner = (
         pltpu.with_memory_space_constraint(x, pltpu.VMEM) for x in (swapped, own, partner)
     )
-    sums, base, chosen, level, factor = chip_sums(
-        sizes, owner_there, partner, counts_there, tokens_there, public_there, noise_there,
-        private_there, swapped, own, scale,
-    )
-    parts = lax.all_to_all(sums, CHIP, split_axis=0, concat_axis=0, tiled=True)
+    lines, beside = sizes
+    line_sums = pltpu.VMEM((lines, flat, WIDE), jnp.int16)
+    windows = lines * WINDOW
+    *away, private_here, plan = pl.pallas_call(
+        away_kernel(sizes, scale, piece),
+        out_shape=(
+            *[line_sums] * (beside - 1),
+            pltpu.VMEM(private_logits.shape, private_logits.dtype),
+            jax.ShapeDtypeStruct((4 * rows,), jnp.int32),
+        ),
+        in_specs=[HBM, VMEM, HBM, HBM, VMEM, VMEM],
+        out_specs=(VMEM,) * beside + (SMEM,),
+        scratch_shapes=[
+            pltpu.VMEM((texts, positions, (beside - 1) * windows), jnp.float32),
+            pltpu.VMEM((texts + 1, positions, (beside - 1) * WINDOW), jnp.float32),
+            pltpu.SMEM((rows,), jnp.int32),
+            pltpu.SMEM((rows,), jnp.int32),
+            pltpu.SMEM((texts,), jnp.int32),
+            pltpu.SMEM((texts,), jnp.int32),
+            pltpu.SemaphoreType.DMA((lines,)),
+            pltpu.SemaphoreType.DMA((3,)),
+        ],
+        compiler_params=PARAMS,
+        name="away_sums",
+    )(owner_there, partner, counts_there, private_there, swapped, own)
+    got = [
+        lax.ppermute(x, "ref_1", [(k, k ^ m) for k in range(beside)])
+        for x, m in zip(away, AROUND)
+    ]
+    line, base, chosen, level, factor = pl.pallas_call(
+        own_kernel(sizes, scale, piece),
+        out_shape=(line_sums, long, long, square, square),
+        in_specs=[VMEM, VMEM, SMEM, SMEM, SMEM, VMEM, VMEM, VMEM],
+        out_specs=(VMEM,) * 5,
+        scratch_shapes=[
+            pltpu.VMEM((texts, positions, windows), jnp.float32),
+            pltpu.VMEM((texts + 1, positions, GROUP * WINDOW), jnp.float32),
+            pltpu.VMEM((2, flat, WIDE), jnp.float32),
+        ],
+        compiler_params=PARAMS,
+        name="own_sums",
+    )(public_there, noise_there, counts_there, tokens_there, plan, private_here, swapped, own)
+    joined = pl.pallas_call(
+        join_kernel,
+        out_shape=line_sums,
+        in_specs=[VMEM] * 4,
+        out_specs=VMEM,
+        compiler_params=PARAMS,
+        name="join",
+    )(line, *[pltpu.with_memory_space_constraint(x, pltpu.VMEM) for x in got])
+    parts = lax.all_to_all(joined, "ref_0", split_axis=0, concat_axis=0, tiled=True)
     parts = pltpu.with_memory_space_constraint(parts, pltpu.VMEM)
     combined, stats = pl.pallas_call(
         finish_kernel,

time: 80.6 us -> 78.5 us (0.974)
  blocking collectives: 69.4 us -> 57.8 us
  waiting for transfers between devices: 0.07 us -> 4.97 us
  starting transfers between devices: 3.63 us -> 6.97 us
  Pallas kernels: 6.48 us -> 7.59 us
    all_to_all x1, blocking collectives: 20.3 us -> 10.9 us  [body(): lax.all_to_all(joined, 'ref_0', split_axis=0, concat_axis=0, tiled=True)]
    ppermute x0 -> x3, waiting for transfers between devices: none -> 4.9 us  [body(): lax.ppermute(x, 'ref_1', [(k, k ^ m) for k in range(beside)])]
    ppermute x0 -> x3, starting transfers between devices: none -> 3.34 us  [body(): lax.ppermute(x, 'ref_1', [(k, k ^ m) for k in range(beside)])]
    all_to_all x1, blocking collectives: 23.3 us -> 21 us  [body(): lax.all_to_all(jnp.broadcast_to(stats, (devices, 1, LANES)), REF_VOC, spl...]
    pallas_call x1 -> x3, Pallas kernels: 4.3 us -> 5.48 us  [the longest x1 3.82 us: body(): pl.pallas_call(away_kernel(sizes, scale, piece), out_shape=(*[line_sums]...]
  transfers between devices with their start and end apart: 2 -> 5, of which waited for: 1 -> 4; matrix products, arithmetic and copies ran while one was open for 0% -> 0% of each run, Pallas kernels for 1% -> 3%
where the time goes in v6:
time: 78.5 us; the launch traced here: 78 us
  blocking collectives  57.8 us (74%)
  Pallas kernels  7.59 us (10%)
  starting transfers between devices  6.97 us (9%)
  waiting for transfers between devices  4.97 us (6%)
    all_to_all x1, blocking collectives, body(): own = lax.all_to_all(packed, CHIP, split_axis=0, concat_axis=0, tiled=True)  25.8 us
    all_to_all x1, blocking collectives, body(): lax.all_to_all(jnp.broadcast_to(stats, (devices, 1, LANES)), REF_VOC, spl...  21 us
    all_to_all x1, blocking collectives, body(): lax.all_to_all(joined, 'ref_0', split_axis=0, concat_axis=0, tiled=True)  10.9 us
    ppermute x3, waiting for transfers between devices, body(): lax.ppermute(x, 'ref_1', [(k, k ^ m) for k in range(beside)])  4.9 us
    pallas_call x1, Pallas kernels, body(): pl.pallas_call(away_kernel(sizes, scale, piece), out_shape=(*[line_sums]...  3.82 us
    ppermute x3, starting transfers between devices, body(): lax.ppermute(x, 'ref_1', [(k, k ^ m) for k in range(beside)])  3.34 us
    ppermute x1, starting transfers between devices, body(): partner = lax.ppermute(owner, CORE, swap)  3.29 us
  transfers between devices with their start and end apart: 5, of which 4 were waited for; matrix products, arithmetic and copies ran while one was open for 0% of the time, Pallas kernels for 3%

profile of v6, /device:TPU:1, one launch (start us, length us, event | category | flops | bytes accessed | tf_op | source)
XLA Modules:
  0.0 78.0 jit_solution(8956875280976708947)
XLA Ops:
  0.6 3.3 %collective-permute-start = (s32[12]{0:T(128)}, s32[12]{0:T(128)S(1)}, u32[]{:S(2)}, u32[]{:S(2)}) collective-permute-start(s32[12]{0:T(128)} %owner_there.1), channel_id=1, source_target_pairs={{0,4},{4,0},{1,5},{5,1},{2,6},{6,2},{3,7},{7,3},{8,12},{12,8},{9,1... | collective-permute-start | bytes 152 | tf_op jit(solution)/shard_map/ppermute | solution.py:432
  3.9 0.9 %turn.1 = (f32[16,512]{1,0:T(8,128)S(1)}, f32[16,128]{1,0:T(8,128)S(1)}) custom-call(bf16[4,4,501]{2,1,0:T(4,128)(2,1)} %public.3, s32[12]{0:T(128)} %owner_there.1), custom_call_target="tpu_custom_call" | custom-call | tf_op jit(solution)/shard_map/turn/pallas_call | solution.py:433
  4.8 0.1 collective-permute-done.partner_there
  4.9 0.3 collective-permute-start.1
  5.2 0.2 mark.1
  5.4 25.8 %all_to_all.15.own = bf16[32,16,512]{2,1,0:T(8,128)(2,1)S(1)} all-to-all(bf16[32,16,512]{2,1,0:T(8,128)(2,1)S(1)} %mark.1), channel_id=1, replica_groups=mesh['ref_0'=8,'ref_1'=4,'ref_2'=2,'voc'=4] {'ref_0','ref_1'}, dimensions={0} | all-to-all | bytes 1048576 | tf_op jit(solution)/shard_map/all_to_all | solution.py:452
  31.2 0.0 collective-permute-done.1.swapped
  31.2 3.8 %away_sums.1 = (s16[8,16,512]{2,1,0:T(8,128)(2,1)S(1)}, s16[8,16,512]{2,1,0:T(8,128)(2,1)S(1)}, s16[8,16,512]{2,1,0:T(8,128)(2,1)S(1)}, bf16[12,4,32064]{2,1,0:T(4,128)(2,1)S(1)}, s32[48]{0:T(128)S(1)}) custom-call(s32[12]{0:T(128)} %owner_there.1, s32[12]{0:T(128)S(1)} %collective-permute-done.partner_there, s32[4]{0:T(128)} %counts.1, ...), custom_call_target="tpu_custom_call" | custom-call | tf_op jit(solution)/shard_map/away_sums/pallas_call | solution.py:459
  35.0 2.3 %collective-permute-start.2 = (s16[8,16,512]{2,1,0:T(8,128)(2,1)S(1)}, s16[8,16,512]{2,1,0:T(8,128)(2,1)S(1)}, u32[]{:S(2)}, u32[]{:S(2)}) collective-permute-start(s16[8,16,512]{2,1,0:T(8,128)(2,1)S(1)} %get-tuple-element.27), channel_id=1, source_target_pairs={{0,16},{8,24},{16,0},{24,8},{1,17},{9,25},{17,1},{25,9},{2,18},{10... | collective-permute-start | bytes 393224 | tf_op jit(solution)/shard_map/ppermute | solution.py:482
  37.3 0.7 collective-permute-start.3
  38.0 0.4 collective-permute-start.4
  38.4 1.6 %own_sums.1 = (s16[8,16,512]{2,1,0:T(8,128)(2,1)S(1)}, f32[16,512]{1,0:T(8,128)S(1)}, f32[16,512]{1,0:T(8,128)S(1)}, f32[16,128]{1,0:T(8,128)S(1)}, f32[16,128]{1,0:T(8,128)S(1)}) custom-call(bf16[4,4,501]{2,1,0:T(4,128)(2,1)} %public.3, bf16[4,4,501]{2,1,0:T(4,128)(2,1)} %noise.1, s32[4]{0:T(128)} %counts.1, s32[4,4]{1,0:T(4,128)} %tokens.1, ...), custom_call_target="tpu_custom_call" | custom-call | tf_op jit(solution)/shard_map/own_sums/pallas_call | solution.py:485
  39.9 0.5 collective-permute-done.2.b
  40.4 2.3 %collective-permute-done.3.c = s16[8,16,512]{2,1,0:T(8,128)(2,1)S(1)} collective-permute-done((s16[8,16,512]{2,1,0:T(8,128)(2,1)S(1)}, s16[8,16,512]{2,1,0:T(8,128)(2,1)S(1)}, u32[]{:S(2)}, u32[]{:S(2)}) %collective-permute-start.3) | collective-permute-done | bytes 131104 | tf_op jit(solution)/shard_map/ppermute | solution.py:482
  42.8 2.1 %collective-permute-done.4.d = s16[8,16,512]{2,1,0:T(8,128)(2,1)S(1)} collective-permute-done((s16[8,16,512]{2,1,0:T(8,128)(2,1)S(1)}, s16[8,16,512]{2,1,0:T(8,128)(2,1)S(1)}, u32[]{:S(2)}, u32[]{:S(2)}) %collective-permute-start.4) | collective-permute-done | bytes 131104 | tf_op jit(solution)/shard_map/ppermute | solution.py:482
  44.8 0.1 join.1
  44.9 10.9 %all_to_all.16.parts = s16[8,16,512]{2,1,0:T(8,128)(2,1)S(1)} all-to-all(s16[8,16,512]{2,1,0:T(8,128)(2,1)S(1)} %join.1), channel_id=1, replica_groups=mesh['ref_0'=8,'ref_1'=4,'ref_2'=2,'voc'=4] {'ref_0'}, dimensions={0} | all-to-all | bytes 262144 | tf_op jit(solution)/shard_map/all_to_all | solution.py:506
  55.9 0.1 finish.1
  56.0 0.1 broadcast_in_dim.3
  56.1 21.0 %all_to_all.17 = f32[256,1,128]{2,1,0:T(1,128)S(1)} all-to-all(f32[256,1,128]{2,1,0:T(1,128)S(1)} %broadcast_in_dim.3), channel_id=1, replica_groups=mesh['ref_0'=8,'ref_1'=4,'ref_2'=2,'voc'=4] {'ref_0','ref_1','ref_2','voc'}, dimensions={0} | all-to-all | bytes 262144 | tf_op jit(solution)/shard_map/all_to_all | solution.py:518
  77.1 0.9 %last.1 = (f32[4,4,501]{2,1,0:T(4,128)}, f32[4,4]{1,0:T(4,128)}) custom-call(f32[256,128]{1,0:T(8,128)S(1)} %bitcast.3, f32[16,512]{1,0:T(8,128)S(1)} %get-tuple-element.35.combined), custom_call_target="tpu_custom_call" | custom-call | tf_op jit(solution)/shard_map/last/pallas_call | solution.py:521
Async XLA Ops:
  0.6 4.2 %collective-permute-start = (s32[12]{0:T(128)}, s32[12]{0:T(128)S(1)}, u32[]{:S(2)}, u32[]{:S(2)}) collective-permute-start(s32[12]{0:T(128)} %owner_there.1), channel_id=1, source_target_pairs={{0,4},{4,0},{1,5},{5,1},{2,6},{6,2},{3,7},{7,3},{8,12},{12,8},{9,1... | collective-permute-start | bytes 152 | tf_op jit(solution)/shard_map/ppermute | solution.py:432
  4.9 26.3 %collective-permute-start.1 = (bf16[12,4,32064]{2,1,0:T(4,128)(2,1)}, bf16[12,4,32064]{2,1,0:T(4,128)(2,1)S(1)}, u32[]{:S(2)}, u32[]{:S(2)}) collective-permute-start(bf16[12,4,32064]{2,1,0:T(4,128)(2,1)} %source.1), channel_id=1, source_target_pairs={{0,4},{4,0},{1,5},{5,1},{2,6},{6,2},{3,7},{7,3},{8,12},{12,8},{9,1... | collective-permute-start | bytes 9234440 | tf_op jit(solution)/shard_map/ppermute | solution.py:443
  35.0 5.4 %collective-permute-start.2 = (s16[8,16,512]{2,1,0:T(8,128)(2,1)S(1)}, s16[8,16,512]{2,1,0:T(8,128)(2,1)S(1)}, u32[]{:S(2)}, u32[]{:S(2)}) collective-permute-start(s16[8,16,512]{2,1,0:T(8,128)(2,1)S(1)} %get-tuple-element.27), channel_id=1, source_target_pairs={{0,16},{8,24},{16,0},{24,8},{1,17},{9,25},{17,1},{25,9},{2,18},{10... | collective-permute-start | bytes 393224 | tf_op jit(solution)/shard_map/ppermute | solution.py:482
  37.3 5.5 %collective-permute-start.3 = (s16[8,16,512]{2,1,0:T(8,128)(2,1)S(1)}, s16[8,16,512]{2,1,0:T(8,128)(2,1)S(1)}, u32[]{:S(2)}, u32[]{:S(2)}) collective-permute-start(s16[8,16,512]{2,1,0:T(8,128)(2,1)S(1)} %get-tuple-element.28), channel_id=1, source_target_pairs={{0,8},{8,0},{16,24},{24,16},{1,9},{9,1},{17,25},{25,17},{2,10},{10... | collective-permute-start | bytes 393224 | tf_op jit(solution)/shard_map/ppermute | solution.py:482
  38.0 6.9 %collective-permute-start.4 = (s16[8,16,512]{2,1,0:T(8,128)(2,1)S(1)}, s16[8,16,512]{2,1,0:T(8,128)(2,1)S(1)}, u32[]{:S(2)}, u32[]{:S(2)}) collective-permute-start(s16[8,16,512]{2,1,0:T(8,128)(2,1)S(1)} %get-tuple-element.29), channel_id=1, source_target_pairs={{0,24},{8,16},{16,8},{24,0},{1,25},{9,17},{17,9},{25,1},{2,26},{10... | collective-permute-start | bytes 393224 | tf_op jit(solution)/shard_map/ppermute | solution.py:482

commit v7 on v6

--- a/solution.py
+++ b/solution.py
@@ -127,12 +127,6 @@
                 at = h * rows + r
                 self.entries.append((held, r, plan[at], plan[2 * rows + at]))
 
-    def clipped(self, entry, start, pub, at, width):
-        held, r, text, _ = entry
-        value = held[r, :, pl.ds(start, width)].astype(jnp.float32)
-        value = value - pub[text, :, pl.ds(at, width)]
-        return jnp.clip(value, -clip_bound, clip_bound)
-
 
 def begins(j, core, piece):
     start = (2 * j + core) * piece
@@ -147,43 +141,37 @@
         pub[t, :, pl.ds(pl.multiple_of(place * WINDOW + WIDE, LANES), LANES)] = part[:, :LANES]
 
 
-def sum_windows(rows, pub, acc, core, piece, scale, windows, may_end=None):
+def fill_strip(rows, strip):
+    last = rows.columns // LANES * LANES
+    strip[...] = jnp.zeros(strip.shape, strip.dtype)
+    for e, (held, r, _, _) in enumerate(rows.entries):
+        strip[e, :, : rows.columns - last] = held[r, :, last:]
+
+
+def sum_windows(rows, pub, acc, core, piece, scale, windows, strip=None):
     texts = pub.shape[0]
-    sizes = [WIDE if may_end is not None and g in may_end else WINDOW for g in range(len(windows))]
+    whole = rows.columns // LANES * LANES
     bases = [begins(j, core, piece)[0] for j, _, _ in windows]
     at = [pl.multiple_of(place * WINDOW, LANES) for _, place, _ in windows]
-    for t in range(texts):
-        for g, size in enumerate(sizes):
-            acc[t, :, g * WINDOW : g * WINDOW + size] = jnp.zeros((rows.positions, size), jnp.float32)
-    for entry in rows.entries:
-        slot = entry[3]
-        for g, size in enumerate(sizes):
-            value = rows.clipped(entry, bases[g], pub, at[g], size)
-            where = slice(g * WINDOW, g * WINDOW + size)
-            acc[slot, :, where] = acc[slot, :, where] + value
-
-    def edge(g, width):
-        sums = [jnp.zeros((rows.positions, width), jnp.float32) for _ in range(texts)]
-        start = pl.multiple_of(bases[g] + WIDE, LANES)
-        for entry in rows.entries:
-            value = rows.clipped(entry, start, pub, pl.multiple_of(at[g] + WIDE, LANES), width)
-            for t in range(texts):
-                sums[t] = sums[t] + jnp.where(entry[3] == t, value, 0.0)
-        for t in range(texts):
-            acc[t, :, g * WINDOW + WIDE : g * WINDOW + WIDE + width] = sums[t]
-
-    for g in may_end or ():
-        rest = rows.columns % LANES
-        ends = bases[g] + WINDOW > rows.columns
-
-        @pl.when(ends)
-        def _():
-            edge(g, rest)
-
-        @pl.when(jnp.logical_not(ends))
-        def _():
-            edge(g, LANES)
-
+    acc[:texts, :, : len(windows) * WINDOW] = jnp.zeros(
+        (texts, rows.positions, len(windows) * WINDOW), jnp.float32
+    )
+    if strip is not None:
+        fill_strip(rows, strip)
+        ends = [base + WINDOW > rows.columns for base in bases]
+        edges = [pl.multiple_of(jnp.minimum(base + WIDE, whole - LANES), LANES) for base in bases]
+    for e, (held, r, text, slot) in enumerate(rows.entries):
+        for g in range(len(windows)):
+            size = WINDOW if strip is None else WIDE
+            parts = [(0, held[r, :, pl.ds(bases[g], size)])]
+            if strip is not None:
+                parts.append((WIDE, jnp.where(ends[g], strip[e], held[r, :, pl.ds(edges[g], LANES)])))
+            for offset, value in parts:
+                width = value.shape[1]
+                beside = pub[text, :, pl.ds(pl.multiple_of(at[g] + offset, LANES), width)]
+                value = jnp.clip(value.astype(jnp.float32) - beside, -clip_bound, clip_bound)
+                where = slice(g * WINDOW + offset, g * WINDOW + offset + width)
+                acc[slot, :, where] = acc[slot, :, where] + value
     lane = lanes_of((texts * rows.positions, LANES))
     for g, (j, _, store) in enumerate(windows):
         shift = begins(j, core, piece)[1]
@@ -207,11 +195,11 @@
     return store
 
 
-def away_kernel(sizes, scale, piece):
+def far_kernel(sizes, scale, piece):
     def kernel(
         owner_there, partner_there, counts_there, source, swapped, own,
-        away_0, away_1, away_2, priv, plan,
-        pub, acc, owner, partner, counts, left, arrived, small,
+        out, priv, plan,
+        pub, acc, strip, owner, partner, counts, left, arrived, small,
     ):
         rows, positions, columns = priv.shape
         texts = pub.shape[0]
@@ -250,8 +238,8 @@
             for n in range(beside):
                 j = beside * i + (mine ^ AROUND[n])
                 value = own[j].astype(jnp.float32)
-                if n < beside - 1:
-                    widen_into(pub, i * (beside - 1) + n, value, positions)
+                if n == 0:
+                    widen_into(pub, i, value, positions)
                 shift = begins(j, core, piece)[1]
                 free = jnp.where(shift == 0, LANES - 1, shift - 1)
                 tile = jnp.where(shift == 0, tile_of(value, TILES - 1), tile_of(value, 0))
@@ -276,25 +264,47 @@
                 plan[2 * rows + at] = jnp.where(still > 0, text, texts)
         acc[texts] = jnp.zeros(acc.shape[1:], jnp.float32)
         held = Rows(plan, priv, swapped)
-        outs = (away_0, away_1, away_2)
-
-        def line(i, may_end=None):
-            windows = [
-                (beside * i + (mine ^ AROUND[n]), i * (beside - 1) + n, storing(outs[n], i))
-                for n in range(beside - 1)
-            ]
-            sum_windows(held, pub, acc, core, piece, scale, windows, may_end)
-
-        def some(i, carry):
-            copy_of(i, pl.multiple_of(LEAD + i * stride, LANES), stride).wait()
-            line(i)
+        for i in range(lines):
+            copies = {0: first_chunk, lines - 1: last_chunk}
+            copy_of(*copies.get(i, (i, LEAD + i * stride, stride))).wait()
+            if i % GROUP == GROUP - 1:
+                windows = [
+                    (beside * k + (mine ^ AROUND[0]), k, storing(out, k))
+                    for k in range(i + 1 - GROUP, i + 1)
+                ]
+                last = i == lines - 1
+                sum_windows(held, pub, acc, core, piece, scale, windows, strip if last else None)
+
+    return kernel
+
+
+def near_kernel(sizes, scale, piece):
+    def kernel(plan, priv, swapped, own, out_1, out_2, pub, acc, strip):
+        texts = pub.shape[0]
+        lines, beside = sizes
+        chip, core = place_of(sizes)
+        mine = lax.axis_index("ref_1")
+        held = Rows(plan, priv, swapped)
+        acc[texts] = jnp.zeros(acc.shape[1:], jnp.float32)
+        step = GROUP // 2
+
+        def some(first, strip=None):
+            windows = []
+            for k in range(step):
+                i = first + k
+                for n, out in ((1, out_1), (2, out_2)):
+                    j = beside * i + (mine ^ AROUND[n])
+                    place = 2 * k + n - 1
+                    widen_into(pub, place, own[j].astype(jnp.float32), held.positions)
+                    windows.append((j, place, storing(out, i)))
+            sum_windows(held, pub, acc, core, piece, scale, windows, strip)
+
+        def looped(b, carry):
+            some(b * step)
             return carry
 
-        copy_of(*first_chunk).wait()
-        line(jnp.int32(0))
-        lax.fori_loop(1, lines - 1, some, 0)
-        copy_of(*last_chunk).wait()
-        line(jnp.int32(lines - 1), range(beside - 1))
+        lax.fori_loop(0, lines // step - 1, looped, 0)
+        some(lines - step, strip)
 
     return kernel
 
@@ -303,7 +313,7 @@
     def kernel(
         public, noise, counts, tokens, plan, priv, swapped, own,
         out, base, chosen, level, factor,
-        pub, acc, scratch,
+        pub, acc, strip, scratch,
     ):
         texts = pub.shape[0]
         lines, beside = sizes
@@ -315,8 +325,8 @@
         acc[texts] = jnp.zeros(acc.shape[1:], jnp.float32)
         for first in range(0, lines, GROUP):
             windows = [(beside * i + mine, i, storing(out, i)) for i in range(first, first + GROUP)]
-            may_end = (GROUP - 1,) if first + GROUP == lines else None
-            sum_windows(held, pub, acc, core, piece, scale, windows, may_end)
+            last = first + GROUP == lines
+            sum_windows(held, pub, acc, core, piece, scale, windows, strip if last else None)
         prepare(sizes, scale / beside, public, noise, counts, tokens, scratch, base, chosen, level, factor)
 
     return kernel
@@ -456,18 +466,25 @@
     lines, beside = sizes
     line_sums = pltpu.VMEM((lines, flat, WIDE), jnp.int16)
     windows = lines * WINDOW
-    *away, private_here, plan = pl.pallas_call(
-        away_kernel(sizes, scale, piece),
+    sums_scratch = pltpu.VMEM((texts + 1, positions, GROUP * WINDOW), jnp.float32)
+    strip = pltpu.VMEM((2 * rows, positions, LANES), private_logits.dtype)
+
+    def beyond(x, m):
+        return lax.ppermute(x, "ref_1", [(k, k ^ m) for k in range(beside)])
+
+    far, private_here, plan = pl.pallas_call(
+        far_kernel(sizes, scale, piece),
         out_shape=(
-            *[line_sums] * (beside - 1),
+            line_sums,
             pltpu.VMEM(private_logits.shape, private_logits.dtype),
             jax.ShapeDtypeStruct((4 * rows,), jnp.int32),
         ),
         in_specs=[HBM, VMEM, HBM, HBM, VMEM, VMEM],
-        out_specs=(VMEM,) * beside + (SMEM,),
+        out_specs=(VMEM, VMEM, SMEM),
         scratch_shapes=[
-            pltpu.VMEM((texts, positions, (beside - 1) * windows), jnp.float32),
-            pltpu.VMEM((texts + 1, positions, (beside - 1) * WINDOW), jnp.float32),
+            pltpu.VMEM((texts, positions, windows), jnp.float32),
+            sums_scratch,
+            strip,
             pltpu.SMEM((rows,), jnp.int32),
             pltpu.SMEM((rows,), jnp.int32),
             pltpu.SMEM((texts,), jnp.int32),
@@ -476,12 +493,24 @@
             pltpu.SemaphoreType.DMA((3,)),
         ],
         compiler_params=PARAMS,
-        name="away_sums",
+        name="far_sums",
     )(owner_there, partner, counts_there, private_there, swapped, own)
-    got = [
-        lax.ppermute(x, "ref_1", [(k, k ^ m) for k in range(beside)])
-        for x, m in zip(away, AROUND)
-    ]
+    got = [beyond(far, AROUND[0])]
+    near = pl.pallas_call(
+        near_kernel(sizes, scale, piece),
+        out_shape=(line_sums, line_sums),
+        in_specs=[SMEM, VMEM, VMEM, VMEM],
+        out_specs=(VMEM, VMEM),
+        scratch_shapes=[
+            pltpu.VMEM((texts, positions, GROUP * WINDOW), jnp.float32),
+            sums_scratch,
+            strip,
+        ],
+        compiler_params=PARAMS,
+        name="near_sums",
+    )(plan, private_here, swapped, own)
+    got += [beyond(x, m) for x, m in zip(near, AROUND[1:])]
+    near_done, own_later = lax.optimization_barrier((near[0], own))
     line, base, chosen, level, factor = pl.pallas_call(
         own_kernel(sizes, scale, piece),
         out_shape=(line_sums, long, long, square, square),
@@ -489,12 +518,13 @@
         out_specs=(VMEM,) * 5,
         scratch_shapes=[
             pltpu.VMEM((texts, positions, windows), jnp.float32),
-            pltpu.VMEM((texts + 1, positions, GROUP * WINDOW), jnp.float32),
+            sums_scratch,
+            strip,
             pltpu.VMEM((2, flat, WIDE), jnp.float32),
         ],
         compiler_params=PARAMS,
         name="own_sums",
-    )(public_there, noise_there, counts_there, tokens_there, plan, private_here, swapped, own)
+    )(public_there, noise_there, counts_there, tokens_there, plan, private_here, swapped, own_later)
     joined = pl.pallas_call(
         join_kernel,
         out_shape=line_sums,

time: 78.5 us -> 78.5 us (level)
  waiting for transfers between devices: 4.97 us -> 3 us
  blocking collectives: 57.8 us -> 59.5 us
    ppermute x3, waiting for transfers between devices: 4.9 us -> 2.93 us  [beyond(): return lax.ppermute(x, 'ref_1', [(k, k ^ m) for k in range(beside)])]
    all_to_all x1, blocking collectives: 21 us -> 22.2 us  [body(): lax.all_to_all(jnp.broadcast_to(stats, (devices, 1, LANES)), REF_VOC, spl...]
    pallas_call x1 -> x2, Pallas kernels: 3.82 us -> 4.28 us  [the longest x1 2.6 us: body(): pl.pallas_call(far_kernel(sizes, scale, piece), out_shape=(line_sums, plt...]
  transfers between devices with their start and end apart: 5 -> 5, of which waited for: 4 -> 2; matrix products, arithmetic and copies ran while one was open for 0% -> 0% of each run, Pallas kernels for 3% -> 5%
where the time goes in v7:
time: 78.5 us; the launch traced here: 78 us
  blocking collectives  59.5 us (76%)
  Pallas kernels  7.96 us (10%)
  starting transfers between devices  6.85 us (9%)
  waiting for transfers between devices  3 us (4%)
    all_to_all x1, blocking collectives, body(): own = lax.all_to_all(packed, CHIP, split_axis=0, concat_axis=0, tiled=True)  25.8 us
    all_to_all x1, blocking collectives, body(): lax.all_to_all(jnp.broadcast_to(stats, (devices, 1, LANES)), REF_VOC, spl...  22.2 us
    all_to_all x1, blocking collectives, body(): lax.all_to_all(joined, 'ref_0', split_axis=0, concat_axis=0, tiled=True)  11.5 us
    ppermute x1, starting transfers between devices, body(): partner = lax.ppermute(owner, CORE, swap)  3.29 us
    ppermute x3, starting transfers between devices, beyond(): return lax.ppermute(x, 'ref_1', [(k, k ^ m) for k in range(beside)])  3.22 us
    ppermute x3, waiting for transfers between devices, beyond(): return lax.ppermute(x, 'ref_1', [(k, k ^ m) for k in range(beside)])  2.93 us
    pallas_call x1, Pallas kernels, body(): pl.pallas_call(far_kernel(sizes, scale, piece), out_shape=(line_sums, plt...  2.6 us
    pallas_call x1, Pallas kernels, body(): pl.pallas_call(near_kernel(sizes, scale, piece), out_shape=(line_sums, li...  1.68 us
  transfers between devices with their start and end apart: 5, of which 2 were waited for; matrix products, arithmetic and copies ran while one was open for 0% of the time, Pallas kernels for 5%

profile of v7, /device:TPU:1, one launch (start us, length us, event | category | flops | bytes accessed | tf_op | source)
XLA Modules:
  0.0 78.0 jit_solution(11847592093993358058)
XLA Ops:
  0.6 3.3 %collective-permute-start = (s32[12]{0:T(128)}, s32[12]{0:T(128)S(1)}, u32[]{:S(2)}, u32[]{:S(2)}) collective-permute-start(s32[12]{0:T(128)} %owner_there.1), channel_id=1, source_target_pairs={{0,4},{4,0},{1,5},{5,1},{2,6},{6,2},{3,7},{7,3},{8,12},{12,8},{9,1... | collective-permute-start | bytes 152 | tf_op jit(solution)/shard_map/ppermute | solution.py:442
  3.9 0.9 %turn.1 = (f32[16,512]{1,0:T(8,128)S(1)}, f32[16,128]{1,0:T(8,128)S(1)}) custom-call(bf16[4,4,501]{2,1,0:T(4,128)(2,1)} %public.3, s32[12]{0:T(128)} %owner_there.1), custom_call_target="tpu_custom_call" | custom-call | tf_op jit(solution)/shard_map/turn/pallas_call | solution.py:443
  4.8 0.1 collective-permute-done.partner_there
  4.9 0.3 collective-permute-start.1
  5.2 0.2 mark.1
  5.4 25.8 %all_to_all.15.own = bf16[32,16,512]{2,1,0:T(8,128)(2,1)S(1)} all-to-all(bf16[32,16,512]{2,1,0:T(8,128)(2,1)S(1)} %mark.1), channel_id=1, replica_groups=mesh['ref_0'=8,'ref_1'=4,'ref_2'=2,'voc'=4] {'ref_0','ref_1'}, dimensions={0} | all-to-all | bytes 1048576 | tf_op jit(solution)/shard_map/all_to_all | solution.py:462
  31.2 0.0 collective-permute-done.1.swapped
  31.2 2.6 %far_sums.1 = (s16[8,16,512]{2,1,0:T(8,128)(2,1)S(1)}, bf16[12,4,32064]{2,1,0:T(4,128)(2,1)S(1)}, s32[48]{0:T(128)S(1)}) custom-call(s32[12]{0:T(128)} %owner_there.1, s32[12]{0:T(128)S(1)} %collective-permute-done.partner_there, s32[4]{0:T(128)} %counts.1, bf16[12,4,32064]{2,1,0:T(4,128)(2,1)} %source.1, ...), custom_call_target="tpu_custom_call" | custom-call | tf_op jit(solution)/shard_map/far_sums/pallas_call | solution.py:475
  33.8 2.3 %collective-permute-start.2 = (s16[8,16,512]{2,1,0:T(8,128)(2,1)S(1)}, s16[8,16,512]{2,1,0:T(8,128)(2,1)S(1)}, u32[]{:S(2)}, u32[]{:S(2)}) collective-permute-start(s16[8,16,512]{2,1,0:T(8,128)(2,1)S(1)} %get-tuple-element.30), channel_id=1, source_target_pairs={{0,16},{8,24},{16,0},{24,8},{1,17},{9,25},{17,1},{25,9},{2,18},{10... | collective-permute-start | bytes 393224 | tf_op jit(solution)/shard_map/ppermute | solution.py:473
  36.1 1.7 %near_sums.1 = (s16[8,16,512]{2,1,0:T(8,128)(2,1)S(1)}, s16[8,16,512]{2,1,0:T(8,128)(2,1)S(1)}) custom-call(s32[48]{0:T(128)S(1)} %get-tuple-element.25.plan, bf16[12,4,32064]{2,1,0:T(4,128)(2,1)S(1)} %get-tuple-element.26.priv, bf16[12,4,32064]{2,1,0:T(4,128)(2,1)S(1)} %collective-permute-done.1.swapped, bf16[32,16,512]{2,1,0:T(8,128)(2,1)S(1)} %all_to_all.15.own), custom_call_target="tpu_custom_call" | custom-call | tf_op jit(solution)/shard_map/near_sums/pallas_call | solution.py:499
  37.7 1.0 %collective-permute-start.4 = (s16[8,16,512]{2,1,0:T(8,128)(2,1)S(1)}, s16[8,16,512]{2,1,0:T(8,128)(2,1)S(1)}, u32[]{:S(2)}, u32[]{:S(2)}) collective-permute-start(s16[8,16,512]{2,1,0:T(8,128)(2,1)S(1)} %get-tuple-element.31), channel_id=1, source_target_pairs={{0,24},{8,16},{16,8},{24,0},{1,25},{9,17},{17,9},{25,1},{2,26},{10... | collective-permute-start | bytes 393224 | tf_op jit(solution)/shard_map/ppermute | solution.py:473
  38.7 0.0 collective-permute-start.3
  38.7 1.5 %own_sums.1 = (s16[8,16,512]{2,1,0:T(8,128)(2,1)S(1)}, f32[16,512]{1,0:T(8,128)S(1)}, f32[16,512]{1,0:T(8,128)S(1)}, f32[16,128]{1,0:T(8,128)S(1)}, f32[16,128]{1,0:T(8,128)S(1)}) custom-call(bf16[4,4,501]{2,1,0:T(4,128)(2,1)} %public.3, bf16[4,4,501]{2,1,0:T(4,128)(2,1)} %noise.1, s32[4]{0:T(128)} %counts.1, s32[4,4]{1,0:T(4,128)} %tokens.1, ...), custom_call_target="tpu_custom_call" | custom-call | tf_op jit(solution)/shard_map/own_sums/pallas_call | solution.py:514
  40.2 0.0 collective-permute-done.2.b
  40.2 2.9 %collective-permute-done.4.d = s16[8,16,512]{2,1,0:T(8,128)(2,1)S(1)} collective-permute-done((s16[8,16,512]{2,1,0:T(8,128)(2,1)S(1)}, s16[8,16,512]{2,1,0:T(8,128)(2,1)S(1)}, u32[]{:S(2)}, u32[]{:S(2)}) %collective-permute-start.4) | collective-permute-done | bytes 131104 | tf_op jit(solution)/shard_map/ppermute | solution.py:473
  43.1 0.0 collective-permute-done.3.c
  43.1 0.1 join.1
  43.2 11.5 %all_to_all.16.parts = s16[8,16,512]{2,1,0:T(8,128)(2,1)S(1)} all-to-all(s16[8,16,512]{2,1,0:T(8,128)(2,1)S(1)} %join.1), channel_id=1, replica_groups=mesh['ref_0'=8,'ref_1'=4,'ref_2'=2,'voc'=4] {'ref_0'}, dimensions={0} | all-to-all | bytes 262144 | tf_op jit(solution)/shard_map/all_to_all | solution.py:536
  54.7 0.1 finish.1
  54.9 0.1 broadcast_in_dim.3
  54.9 22.2 %all_to_all.17 = f32[256,1,128]{2,1,0:T(1,128)S(1)} all-to-all(f32[256,1,128]{2,1,0:T(1,128)S(1)} %broadcast_in_dim.3), channel_id=1, replica_groups=mesh['ref_0'=8,'ref_1'=4,'ref_2'=2,'voc'=4] {'ref_0','ref_1','ref_2','voc'}, dimensions={0} | all-to-all | bytes 262144 | tf_op jit(solution)/shard_map/all_to_all | solution.py:548
  77.1 0.9 %last.1 = (f32[4,4,501]{2,1,0:T(4,128)}, f32[4,4]{1,0:T(4,128)}) custom-call(f32[256,128]{1,0:T(8,128)S(1)} %bitcast.3, f32[16,512]{1,0:T(8,128)S(1)} %get-tuple-element.37.combined), custom_call_target="tpu_custom_call" | custom-call | tf_op jit(solution)/shard_map/last/pallas_call | solution.py:551
Async XLA Ops:
  0.6 4.2 %collective-permute-start = (s32[12]{0:T(128)}, s32[12]{0:T(128)S(1)}, u32[]{:S(2)}, u32[]{:S(2)}) collective-permute-start(s32[12]{0:T(128)} %owner_there.1), channel_id=1, source_target_pairs={{0,4},{4,0},{1,5},{5,1},{2,6},{6,2},{3,7},{7,3},{8,12},{12,8},{9,1... | collective-permute-start | bytes 152 | tf_op jit(solution)/shard_map/ppermute | solution.py:442
  4.9 26.3 %collective-permute-start.1 = (bf16[12,4,32064]{2,1,0:T(4,128)(2,1)}, bf16[12,4,32064]{2,1,0:T(4,128)(2,1)S(1)}, u32[]{:S(2)}, u32[]{:S(2)}) collective-permute-start(bf16[12,4,32064]{2,1,0:T(4,128)(2,1)} %source.1), channel_id=1, source_target_pairs={{0,4},{4,0},{1,5},{5,1},{2,6},{6,2},{3,7},{7,3},{8,12},{12,8},{9,1... | collective-permute-start | bytes 9234440 | tf_op jit(solution)/shard_map/ppermute | solution.py:453
  33.8 6.4 %collective-permute-start.2 = (s16[8,16,512]{2,1,0:T(8,128)(2,1)S(1)}, s16[8,16,512]{2,1,0:T(8,128)(2,1)S(1)}, u32[]{:S(2)}, u32[]{:S(2)}) collective-permute-start(s16[8,16,512]{2,1,0:T(8,128)(2,1)S(1)} %get-tuple-element.30), channel_id=1, source_target_pairs={{0,16},{8,24},{16,0},{24,8},{1,17},{9,25},{17,1},{25,9},{2,18},{10... | collective-permute-start | bytes 393224 | tf_op jit(solution)/shard_map/ppermute | solution.py:473
  37.7 5.4 %collective-permute-start.4 = (s16[8,16,512]{2,1,0:T(8,128)(2,1)S(1)}, s16[8,16,512]{2,1,0:T(8,128)(2,1)S(1)}, u32[]{:S(2)}, u32[]{:S(2)}) collective-permute-start(s16[8,16,512]{2,1,0:T(8,128)(2,1)S(1)} %get-tuple-element.31), channel_id=1, source_target_pairs={{0,24},{8,16},{16,8},{24,0},{1,25},{9,17},{17,9},{25,1},{2,26},{10... | collective-permute-start | bytes 393224 | tf_op jit(solution)/shard_map/ppermute | solution.py:473
  38.7 4.4 %collective-permute-start.3 = (s16[8,16,512]{2,1,0:T(8,128)(2,1)S(1)}, s16[8,16,512]{2,1,0:T(8,128)(2,1)S(1)}, u32[]{:S(2)}, u32[]{:S(2)}) collective-permute-start(s16[8,16,512]{2,1,0:T(8,128)(2,1)S(1)} %get-tuple-element.27), channel_id=1, source_target_pairs={{0,8},{8,0},{16,24},{24,16},{1,9},{9,1},{17,25},{25,17},{2,10},{10... | collective-permute-start | bytes 393224 | tf_op jit(solution)/shard_map/ppermute | solution.py:473

commit v8 on v7

--- a/solution.py
+++ b/solution.py
@@ -20,7 +20,6 @@
 WINDOW = WIDE + LANES
 GROUP = 4
 AROUND = (2, 1, 3, 0)
-LEAD = LANES
 
 PARAMS = pltpu.CompilerParams(vmem_limit_bytes=16 << 20)
 SMEM = pl.BlockSpec(memory_space=pltpu.SMEM)
@@ -197,9 +196,9 @@
 
 def far_kernel(sizes, scale, piece):
     def kernel(
-        owner_there, partner_there, counts_there, source, swapped, own,
-        out, priv, plan,
-        pub, acc, strip, owner, partner, counts, left, arrived, small,
+        owner_there, partner_there, counts_there, priv, swapped, own,
+        out, plan,
+        pub, acc, strip, owner, partner, counts, left, small,
     ):
         rows, positions, columns = priv.shape
         texts = pub.shape[0]
@@ -210,29 +209,12 @@
         lane = lanes_of((flat, LANES))
         row = lax.broadcasted_iota(jnp.int32, (flat, LANES), 0)
 
-        stride = 2 * beside * piece
-        stride = -(-stride // LANES) * LANES
-
-        def copy_of(i, start, width):
-            return pltpu.make_async_copy(
-                source.at[:, :, pl.ds(start, width)],
-                priv.at[:, :, pl.ds(start, width)],
-                arrived.at[i],
-            )
-
-        first_chunk = (0, 0, stride + LEAD)
-        last_start = LEAD + (lines - 1) * stride
-        last_chunk = (lines - 1, last_start, columns - last_start)
         pairs = ((owner_there, owner), (partner_there, partner), (counts_there, counts))
         little = [
             pltpu.make_async_copy(there, here, small.at[i]) for i, (there, here) in enumerate(pairs)
         ]
         for copy in little:
             copy.start()
-        copy_of(*first_chunk).start()
-        for i in range(1, lines - 1):
-            copy_of(i, LEAD + i * stride, stride).start()
-        copy_of(*last_chunk).start()
 
         def widen(i, earlier):
             for n in range(beside):
@@ -265,8 +247,6 @@
         acc[texts] = jnp.zeros(acc.shape[1:], jnp.float32)
         held = Rows(plan, priv, swapped)
         for i in range(lines):
-            copies = {0: first_chunk, lines - 1: last_chunk}
-            copy_of(*copies.get(i, (i, LEAD + i * stride, stride))).wait()
             if i % GROUP == GROUP - 1:
                 windows = [
                     (beside * k + (mine ^ AROUND[0]), k, storing(out, k))
@@ -434,9 +414,9 @@
     scale = float(32767 // (2 * rows * int(clip_bound)))
     square = pltpu.VMEM((flat, LANES), jnp.float32)
     long = pltpu.VMEM((flat, WIDE), jnp.float32)
-    owner_there, counts_there, tokens_there, public_there, noise_there, private_there = (
+    owner_there, counts_there, tokens_there, public_there, noise_there = (
         pltpu.with_memory_space_constraint(x, pltpu.HBM)
-        for x in (owner, counts, tokens, public_logits, noise, private_logits)
+        for x in (owner, counts, tokens, public_logits, noise)
     )
 
     partner = lax.ppermute(owner, CORE, swap)
@@ -451,6 +431,7 @@
     )(public_there, owner_there)
     partner, private_later, one = lax.optimization_barrier((partner, private_logits, one))
     swapped = lax.ppermute(private_later, CORE, swap)
+    private_here = lax.ppermute(private_later, CORE, [(0, 0), (1, 1)])
     packed = pl.pallas_call(
         mark_kernel(sizes, piece, positions),
         out_shape=pltpu.VMEM((chips, flat, WIDE), jnp.bfloat16),
@@ -460,8 +441,9 @@
         name="mark",
     )(one, number, partner.reshape(1, rows))
     own = lax.all_to_all(packed, CHIP, split_axis=0, concat_axis=0, tiled=True)
-    swapped, own, partner = (
-        pltpu.with_memory_space_constraint(x, pltpu.VMEM) for x in (swapped, own, partner)
+    swapped, own, partner, private_here = (
+        pltpu.with_memory_space_constraint(x, pltpu.VMEM)
+        for x in (swapped, own, partner, private_here)
     )
     lines, beside = sizes
     line_sums = pltpu.VMEM((lines, flat, WIDE), jnp.int16)
@@ -472,15 +454,14 @@
     def beyond(x, m):
         return lax.ppermute(x, "ref_1", [(k, k ^ m) for k in range(beside)])
 
-    far, private_here, plan = pl.pallas_call(
+    far, plan = pl.pallas_call(
         far_kernel(sizes, scale, piece),
         out_shape=(
             line_sums,
-            pltpu.VMEM(private_logits.shape, private_logits.dtype),
             jax.ShapeDtypeStruct((4 * rows,), jnp.int32),
         ),
-        in_specs=[HBM, VMEM, HBM, HBM, VMEM, VMEM],
-        out_specs=(VMEM, VMEM, SMEM),
+        in_specs=[HBM, VMEM, HBM, VMEM, VMEM, VMEM],
+        out_specs=(VMEM, SMEM),
         scratch_shapes=[
             pltpu.VMEM((texts, positions, windows), jnp.float32),
             sums_scratch,
@@ -489,12 +470,11 @@
             pltpu.SMEM((rows,), jnp.int32),
             pltpu.SMEM((texts,), jnp.int32),
             pltpu.SMEM((texts,), jnp.int32),
-            pltpu.SemaphoreType.DMA((lines,)),
             pltpu.SemaphoreType.DMA((3,)),
         ],
         compiler_params=PARAMS,
         name="far_sums",
-    )(owner_there, partner, counts_there, private_there, swapped, own)
+    )(owner_there, partner, counts_there, private_here, swapped, own)
     got = [beyond(far, AROUND[0])]
     near = pl.pallas_call(
         near_kernel(sizes, scale, piece),

time: 78.5 us -> 79.7 us (1.015)
  starting transfers between devices: 6.85 us -> 8.74 us
    ppermute x0 -> x1, starting transfers between devices: none -> 1.87 us  [body(): private_here = lax.ppermute(private_later, CORE, [(0, 0), (1, 1)])]
  transfers between devices with their start and end apart: 5 -> 6, of which waited for: 2 -> 2; matrix products, arithmetic and copies ran while one was open for 0% -> 0% of each run, Pallas kernels for 5% -> 5%
where the time goes in v8:
time: 79.7 us; the launch traced here: 79.2 us
  blocking collectives  59.5 us (75%)
  starting transfers between devices  8.74 us (11%)
  Pallas kernels  7.25 us (9%)
  waiting for transfers between devices  2.99 us (4%)
    all_to_all x1, blocking collectives, body(): own = lax.all_to_all(packed, CHIP, split_axis=0, concat_axis=0, tiled=True)  25.8 us
    all_to_all x1, blocking collectives, body(): lax.all_to_all(jnp.broadcast_to(stats, (devices, 1, LANES)), REF_VOC, spl...  22.2 us
    all_to_all x1, blocking collectives, body(): lax.all_to_all(joined, 'ref_0', split_axis=0, concat_axis=0, tiled=True)  11.5 us
    ppermute x1, starting transfers between devices, body(): partner = lax.ppermute(owner, CORE, swap)  3.29 us
    ppermute x3, starting transfers between devices, beyond(): return lax.ppermute(x, 'ref_1', [(k, k ^ m) for k in range(beside)])  3.23 us
    ppermute x3, waiting for transfers between devices, beyond(): return lax.ppermute(x, 'ref_1', [(k, k ^ m) for k in range(beside)])  2.92 us
    pallas_call x1, Pallas kernels, body(): pl.pallas_call(far_kernel(sizes, scale, piece), out_shape=(line_sums, jax...  1.88 us
    ppermute x1, starting transfers between devices, body(): private_here = lax.ppermute(private_later, CORE, [(0, 0), (1, 1)])  1.87 us
  transfers between devices with their start and end apart: 6, of which 2 were waited for; matrix products, arithmetic and copies ran while one was open for 0% of the time, Pallas kernels for 5%

profile of v8, /device:TPU:1, one launch (start us, length us, event | category | flops | bytes accessed | tf_op | source)
XLA Modules:
  0.0 79.2 jit_solution(5432359063549747893)
XLA Ops:
  0.6 3.3 %collective-permute-start = (s32[12]{0:T(128)}, s32[12]{0:T(128)S(1)}, u32[]{:S(2)}, u32[]{:S(2)}) collective-permute-start(s32[12]{0:T(128)} %owner_there.1), channel_id=1, source_target_pairs={{0,4},{4,0},{1,5},{5,1},{2,6},{6,2},{3,7},{7,3},{8,12},{12,8},{9,1... | collective-permute-start | bytes 152 | tf_op jit(solution)/shard_map/ppermute | solution.py:422
  3.9 0.9 %turn.1 = (f32[16,512]{1,0:T(8,128)S(1)}, f32[16,128]{1,0:T(8,128)S(1)}) custom-call(bf16[4,4,501]{2,1,0:T(4,128)(2,1)} %public.3, s32[12]{0:T(128)} %owner_there.1), custom_call_target="tpu_custom_call" | custom-call | tf_op jit(solution)/shard_map/turn/pallas_call | solution.py:423
  4.8 0.1 collective-permute-done.partner_there
  4.9 0.3 collective-permute-start.2
  5.2 1.9 %collective-permute-start.1 = (bf16[12,4,32064]{2,1,0:T(4,128)(2,1)}, bf16[12,4,32064]{2,1,0:T(4,128)(2,1)S(1)}, u32[]{:S(2)}, u32[]{:S(2)}) collective-permute-start(bf16[12,4,32064]{2,1,0:T(4,128)(2,1)} %param.6), channel_id=1, source_target_pairs={{0,0},{4,4},{1,1},{5,5},{2,2},{6,6},{3,3},{7,7},{8,8},{12,12},{9,9... | collective-permute-start | bytes 9234440 | tf_op jit(solution)/shard_map/ppermute | solution.py:434
  7.1 0.2 mark.1
  7.3 25.8 %all_to_all.15.own = bf16[32,16,512]{2,1,0:T(8,128)(2,1)S(1)} all-to-all(bf16[32,16,512]{2,1,0:T(8,128)(2,1)S(1)} %mark.1), channel_id=1, replica_groups=mesh['ref_0'=8,'ref_1'=4,'ref_2'=2,'voc'=4] {'ref_0','ref_1'}, dimensions={0} | all-to-all | bytes 1048576 | tf_op jit(solution)/shard_map/all_to_all | solution.py:443
  33.1 0.0 collective-permute-done.2.swapped
  33.1 0.0 collective-permute-done.1.priv
  33.1 1.9 %far_sums.1 = (s16[8,16,512]{2,1,0:T(8,128)(2,1)S(1)}, s32[48]{0:T(128)S(1)}) custom-call(s32[12]{0:T(128)} %owner_there.1, s32[12]{0:T(128)S(1)} %collective-permute-done.partner_there, s32[4]{0:T(128)} %counts.1, bf16[12,4,32064]{2,1,0:T(4,128)(2,1)S(1)} %collective-permute-done.1.priv, bf16[12,4,32064]{2,1,0:T(4,128)(2,1)S(1)} %collective-permute-done.2.swapped, ...), custom_call_target="tpu_custom_call" | custom-call | tf_op jit(solution)/shard_map/far_sums/pallas_call | solution.py:457
  35.0 2.3 %collective-permute-start.3 = (s16[8,16,512]{2,1,0:T(8,128)(2,1)S(1)}, s16[8,16,512]{2,1,0:T(8,128)(2,1)S(1)}, u32[]{:S(2)}, u32[]{:S(2)}) collective-permute-start(s16[8,16,512]{2,1,0:T(8,128)(2,1)S(1)} %get-tuple-element.28), channel_id=1, source_target_pairs={{0,16},{8,24},{16,0},{24,8},{1,17},{9,25},{17,1},{25,9},{2,18},{10... | collective-permute-start | bytes 393224 | tf_op jit(solution)/shard_map/ppermute | solution.py:455
  37.2 1.7 %near_sums.1 = (s16[8,16,512]{2,1,0:T(8,128)(2,1)S(1)}, s16[8,16,512]{2,1,0:T(8,128)(2,1)S(1)}) custom-call(s32[48]{0:T(128)S(1)} %get-tuple-element.24.plan, bf16[12,4,32064]{2,1,0:T(4,128)(2,1)S(1)} %collective-permute-done.1.priv, bf16[12,4,32064]{2,1,0:T(4,128)(2,1)S(1)} %collective-permute-done.2.swapped, bf16[32,16,512]{2,1,0:T(8,128)(2,1)S(1)} %all_to_all.15.own), custom_call_target="tpu_custom_call" | custom-call | tf_op jit(solution)/shard_map/near_sums/pallas_call | solution.py:479
  38.9 1.0 %collective-permute-start.5 = (s16[8,16,512]{2,1,0:T(8,128)(2,1)S(1)}, s16[8,16,512]{2,1,0:T(8,128)(2,1)S(1)}, u32[]{:S(2)}, u32[]{:S(2)}) collective-permute-start(s16[8,16,512]{2,1,0:T(8,128)(2,1)S(1)} %get-tuple-element.29), channel_id=1, source_target_pairs={{0,24},{8,16},{16,8},{24,0},{1,25},{9,17},{17,9},{25,1},{2,26},{10... | collective-permute-start | bytes 393224 | tf_op jit(solution)/shard_map/ppermute | solution.py:455
  39.9 0.0 collective-permute-start.4
  39.9 1.5 %own_sums.1 = (s16[8,16,512]{2,1,0:T(8,128)(2,1)S(1)}, f32[16,512]{1,0:T(8,128)S(1)}, f32[16,512]{1,0:T(8,128)S(1)}, f32[16,128]{1,0:T(8,128)S(1)}, f32[16,128]{1,0:T(8,128)S(1)}) custom-call(bf16[4,4,501]{2,1,0:T(4,128)(2,1)} %public.3, bf16[4,4,501]{2,1,0:T(4,128)(2,1)} %noise.1, s32[4]{0:T(128)} %counts.1, s32[4,4]{1,0:T(4,128)} %tokens.1, ...), custom_call_target="tpu_custom_call" | custom-call | tf_op jit(solution)/shard_map/own_sums/pallas_call | solution.py:494
  41.4 0.0 collective-permute-done.3.b
  41.4 2.9 %collective-permute-done.5.d = s16[8,16,512]{2,1,0:T(8,128)(2,1)S(1)} collective-permute-done((s16[8,16,512]{2,1,0:T(8,128)(2,1)S(1)}, s16[8,16,512]{2,1,0:T(8,128)(2,1)S(1)}, u32[]{:S(2)}, u32[]{:S(2)}) %collective-permute-start.5) | collective-permute-done | bytes 131104 | tf_op jit(solution)/shard_map/ppermute | solution.py:455
  44.3 0.0 collective-permute-done.4.c
  44.3 0.1 join.1
  44.4 11.5 %all_to_all.16.parts = s16[8,16,512]{2,1,0:T(8,128)(2,1)S(1)} all-to-all(s16[8,16,512]{2,1,0:T(8,128)(2,1)S(1)} %join.1), channel_id=1, replica_groups=mesh['ref_0'=8,'ref_1'=4,'ref_2'=2,'voc'=4] {'ref_0'}, dimensions={0} | all-to-all | bytes 262144 | tf_op jit(solution)/shard_map/all_to_all | solution.py:516
  55.9 0.1 finish.1
  56.0 0.1 broadcast_in_dim.3
  56.1 22.2 %all_to_all.17 = f32[256,1,128]{2,1,0:T(1,128)S(1)} all-to-all(f32[256,1,128]{2,1,0:T(1,128)S(1)} %broadcast_in_dim.3), channel_id=1, replica_groups=mesh['ref_0'=8,'ref_1'=4,'ref_2'=2,'voc'=4] {'ref_0','ref_1','ref_2','voc'}, dimensions={0} | all-to-all | bytes 262144 | tf_op jit(solution)/shard_map/all_to_all | solution.py:528
  78.3 0.9 %last.1 = (f32[4,4,501]{2,1,0:T(4,128)}, f32[4,4]{1,0:T(4,128)}) custom-call(f32[256,128]{1,0:T(8,128)S(1)} %bitcast.3, f32[16,512]{1,0:T(8,128)S(1)} %get-tuple-element.35.combined), custom_call_target="tpu_custom_call" | custom-call | tf_op jit(solution)/shard_map/last/pallas_call | solution.py:531
Async XLA Ops:
  0.6 4.2 %collective-permute-start = (s32[12]{0:T(128)}, s32[12]{0:T(128)S(1)}, u32[]{:S(2)}, u32[]{:S(2)}) collective-permute-start(s32[12]{0:T(128)} %owner_there.1), channel_id=1, source_target_pairs={{0,4},{4,0},{1,5},{5,1},{2,6},{6,2},{3,7},{7,3},{8,12},{12,8},{9,1... | collective-permute-start | bytes 152 | tf_op jit(solution)/shard_map/ppermute | solution.py:422
  4.9 28.2 %collective-permute-start.2 = (bf16[12,4,32064]{2,1,0:T(4,128)(2,1)}, bf16[12,4,32064]{2,1,0:T(4,128)(2,1)S(1)}, u32[]{:S(2)}, u32[]{:S(2)}) collective-permute-start(bf16[12,4,32064]{2,1,0:T(4,128)(2,1)} %param.6), channel_id=1, source_target_pairs={{0,4},{4,0},{1,5},{5,1},{2,6},{6,2},{3,7},{7,3},{8,12},{12,8},{9,1... | collective-permute-start | bytes 9234440 | tf_op jit(solution)/shard_map/ppermute | solution.py:433
  5.2 27.9 %collective-permute-start.1 = (bf16[12,4,32064]{2,1,0:T(4,128)(2,1)}, bf16[12,4,32064]{2,1,0:T(4,128)(2,1)S(1)}, u32[]{:S(2)}, u32[]{:S(2)}) collective-permute-start(bf16[12,4,32064]{2,1,0:T(4,128)(2,1)} %param.6), channel_id=1, source_target_pairs={{0,0},{4,4},{1,1},{5,5},{2,2},{6,6},{3,3},{7,7},{8,8},{12,12},{9,9... | collective-permute-start | bytes 9234440 | tf_op jit(solution)/shard_map/ppermute | solution.py:434
  35.0 6.4 %collective-permute-start.3 = (s16[8,16,512]{2,1,0:T(8,128)(2,1)S(1)}, s16[8,16,512]{2,1,0:T(8,128)(2,1)S(1)}, u32[]{:S(2)}, u32[]{:S(2)}) collective-permute-start(s16[8,16,512]{2,1,0:T(8,128)(2,1)S(1)} %get-tuple-element.28), channel_id=1, source_target_pairs={{0,16},{8,24},{16,0},{24,8},{1,17},{9,25},{17,1},{25,9},{2,18},{10... | collective-permute-start | bytes 393224 | tf_op jit(solution)/shard_map/ppermute | solution.py:455
  38.9 5.4 %collective-permute-start.5 = (s16[8,16,512]{2,1,0:T(8,128)(2,1)S(1)}, s16[8,16,512]{2,1,0:T(8,128)(2,1)S(1)}, u32[]{:S(2)}, u32[]{:S(2)}) collective-permute-start(s16[8,16,512]{2,1,0:T(8,128)(2,1)S(1)} %get-tuple-element.29), channel_id=1, source_target_pairs={{0,24},{8,16},{16,8},{24,0},{1,25},{9,17},{17,9},{25,1},{2,26},{10... | collective-permute-start | bytes 393224 | tf_op jit(solution)/shard_map/ppermute | solution.py:455
  39.9 4.4 %collective-permute-start.4 = (s16[8,16,512]{2,1,0:T(8,128)(2,1)S(1)}, s16[8,16,512]{2,1,0:T(8,128)(2,1)S(1)}, u32[]{:S(2)}, u32[]{:S(2)}) collective-permute-start(s16[8,16,512]{2,1,0:T(8,128)(2,1)S(1)} %get-tuple-element.25), channel_id=1, source_target_pairs={{0,8},{8,0},{16,24},{24,16},{1,9},{9,1},{17,25},{25,17},{2,10},{10... | collective-permute-start | bytes 393224 | tf_op jit(solution)/shard_map/ppermute | solution.py:455

commit v9 on v7

--- a/solution.py
+++ b/solution.py
@@ -141,26 +141,37 @@
         pub[t, :, pl.ds(pl.multiple_of(place * WINDOW + WIDE, LANES), LANES)] = part[:, :LANES]
 
 
-def fill_strip(rows, strip):
+def fill_strip(rows, strip, entries):
     last = rows.columns // LANES * LANES
-    strip[...] = jnp.zeros(strip.shape, strip.dtype)
-    for e, (held, r, _, _) in enumerate(rows.entries):
+    for e in entries:
+        held, r = rows.entries[e][:2]
+        strip[e] = jnp.zeros(strip.shape[1:], strip.dtype)
         strip[e, :, : rows.columns - last] = held[r, :, last:]
 
 
 def sum_windows(rows, pub, acc, core, piece, scale, windows, strip=None):
-    texts = pub.shape[0]
+    clear(rows, acc, 0, len(windows))
+    add_rows(rows, pub, acc, core, piece, windows, range(len(rows.entries)), 0, strip)
+    store_sums(rows, acc, core, piece, scale, windows, 0)
+
+
+def clear(rows, acc, first, many):
+    texts = acc.shape[0] - 1
+    acc[:texts, :, first * WINDOW : (first + many) * WINDOW] = jnp.zeros(
+        (texts, rows.positions, many * WINDOW), jnp.float32
+    )
+
+
+def add_rows(rows, pub, acc, core, piece, windows, entries, first, strip=None):
     whole = rows.columns // LANES * LANES
     bases = [begins(j, core, piece)[0] for j, _, _ in windows]
     at = [pl.multiple_of(place * WINDOW, LANES) for _, place, _ in windows]
-    acc[:texts, :, : len(windows) * WINDOW] = jnp.zeros(
-        (texts, rows.positions, len(windows) * WINDOW), jnp.float32
-    )
     if strip is not None:
-        fill_strip(rows, strip)
+        fill_strip(rows, strip, entries)
         ends = [base + WINDOW > rows.columns for base in bases]
         edges = [pl.multiple_of(jnp.minimum(base + WIDE, whole - LANES), LANES) for base in bases]
-    for e, (held, r, text, slot) in enumerate(rows.entries):
+    for e in entries:
+        held, r, text, slot = rows.entries[e]
         for g in range(len(windows)):
             size = WINDOW if strip is None else WIDE
             parts = [(0, held[r, :, pl.ds(bases[g], size)])]
@@ -170,14 +181,18 @@
                 width = value.shape[1]
                 beside = pub[text, :, pl.ds(pl.multiple_of(at[g] + offset, LANES), width)]
                 value = jnp.clip(value.astype(jnp.float32) - beside, -clip_bound, clip_bound)
-                where = slice(g * WINDOW + offset, g * WINDOW + offset + width)
-                acc[slot, :, where] = acc[slot, :, where] + value
+                start = (first + g) * WINDOW + offset
+                acc[slot, :, start : start + width] = acc[slot, :, start : start + width] + value
+
+
+def store_sums(rows, acc, core, piece, scale, windows, first):
+    texts = acc.shape[0] - 1
     lane = lanes_of((texts * rows.positions, LANES))
     for g, (j, _, store) in enumerate(windows):
         shift = begins(j, core, piece)[1]
         tiles = [
             jnp.concatenate(
-                [acc[t, :, g * WINDOW + k * LANES : g * WINDOW + (k + 1) * LANES] for t in range(texts)],
+                [tile_at(acc, t, (first + g) * WINDOW + k * LANES) for t in range(texts)],
                 axis=0,
             )
             for k in range(TILES + 1)
@@ -186,6 +201,10 @@
         for k in range(TILES):
             fixed = jnp.round(tiles[k] * scale).astype(jnp.int32).astype(jnp.int16)
             store(slice(k * LANES, (k + 1) * LANES), fixed)
+
+
+def tile_at(acc, t, start):
+    return acc[t, :, start : start + LANES]
 
 
 def storing(out, index):
@@ -264,16 +283,22 @@
                 plan[2 * rows + at] = jnp.where(still > 0, text, texts)
         acc[texts] = jnp.zeros(acc.shape[1:], jnp.float32)
         held = Rows(plan, priv, swapped)
-        for i in range(lines):
-            copies = {0: first_chunk, lines - 1: last_chunk}
-            copy_of(*copies.get(i, (i, LEAD + i * stride, stride))).wait()
-            if i % GROUP == GROUP - 1:
-                windows = [
-                    (beside * k + (mine ^ AROUND[0]), k, storing(out, k))
-                    for k in range(i + 1 - GROUP, i + 1)
-                ]
-                last = i == lines - 1
-                sum_windows(held, pub, acc, core, piece, scale, windows, strip if last else None)
+        windows = [(beside * i + (mine ^ AROUND[0]), i, storing(out, i)) for i in range(lines)]
+        clear(held, acc, 0, lines)
+
+        def add(entries, first):
+            batch = windows[first : first + GROUP]
+            edge = strip if first + GROUP == lines else None
+            add_rows(held, pub, acc, core, piece, batch, entries, first, edge)
+
+        for first in range(0, lines, GROUP):
+            add(range(rows, 2 * rows), first)
+        copies = {0: first_chunk, lines - 1: last_chunk}
+        for first in range(0, lines, GROUP):
+            for i in range(first, first + GROUP):
+                copy_of(*copies.get(i, (i, LEAD + i * stride, stride))).wait()
+            add(range(rows), first)
+            store_sums(held, acc, core, piece, scale, windows[first : first + GROUP], first)
 
     return kernel
 
@@ -483,7 +508,7 @@
         out_specs=(VMEM, VMEM, SMEM),
         scratch_shapes=[
             pltpu.VMEM((texts, positions, windows), jnp.float32),
-            sums_scratch,
+            pltpu.VMEM((texts + 1, positions, windows), jnp.float32),
             strip,
             pltpu.SMEM((rows,), jnp.int32),
             pltpu.SMEM((rows,), jnp.int32),

time: 78.5 us -> 78.4 us (level)
  no operation moved by 1% of the time
where the time goes in v9:
time: 78.4 us; the launch traced here: 78 us
  blocking collectives  59.5 us (76%)
  Pallas kernels  7.9 us (10%)
  starting transfers between devices  6.86 us (9%)
  waiting for transfers between devices  2.99 us (4%)
    all_to_all x1, blocking collectives, body(): own = lax.all_to_all(packed, CHIP, split_axis=0, concat_axis=0, tiled=True)  25.8 us
    all_to_all x1, blocking collectives, body(): lax.all_to_all(jnp.broadcast_to(stats, (devices, 1, LANES)), REF_VOC, spl...  22.2 us
    all_to_all x1, blocking collectives, body(): lax.all_to_all(joined, 'ref_0', split_axis=0, concat_axis=0, tiled=True)  11.5 us
    ppermute x1, starting transfers between devices, body(): partner = lax.ppermute(owner, CORE, swap)  3.29 us
    ppermute x3, starting transfers between devices, beyond(): return lax.ppermute(x, 'ref_1', [(k, k ^ m) for k in range(beside)])  3.23 us
    ppermute x3, waiting for transfers between devices, beyond(): return lax.ppermute(x, 'ref_1', [(k, k ^ m) for k in range(beside)])  2.92 us
    pallas_call x1, Pallas kernels, body(): pl.pallas_call(far_kernel(sizes, scale, piece), out_shape=(line_sums, plt...  2.54 us
    pallas_call x1, Pallas kernels, body(): pl.pallas_call(near_kernel(sizes, scale, piece), out_shape=(line_sums, li...  1.68 us
  transfers between devices with their start and end apart: 5, of which 2 were waited for; matrix products, arithmetic and copies ran while one was open for 0% of the time, Pallas kernels for 5%

profile of v9, /device:TPU:1, one launch (start us, length us, event | category | flops | bytes accessed | tf_op | source)
XLA Modules:
  0.0 78.0 jit_solution(16398677083894937284)
XLA Ops:
  0.6 3.3 %collective-permute-start = (s32[12]{0:T(128)}, s32[12]{0:T(128)S(1)}, u32[]{:S(2)}, u32[]{:S(2)}) collective-permute-start(s32[12]{0:T(128)} %owner_there.1), channel_id=1, source_target_pairs={{0,4},{4,0},{1,5},{5,1},{2,6},{6,2},{3,7},{7,3},{8,12},{12,8},{9,1... | collective-permute-start | bytes 152 | tf_op jit(solution)/shard_map/ppermute | solution.py:467
  3.9 0.9 %turn.1 = (f32[16,512]{1,0:T(8,128)S(1)}, f32[16,128]{1,0:T(8,128)S(1)}) custom-call(bf16[4,4,501]{2,1,0:T(4,128)(2,1)} %public.3, s32[12]{0:T(128)} %owner_there.1), custom_call_target="tpu_custom_call" | custom-call | tf_op jit(solution)/shard_map/turn/pallas_call | solution.py:468
  4.8 0.1 collective-permute-done.partner_there
  4.9 0.3 collective-permute-start.1
  5.2 0.2 mark.1
  5.4 25.8 %all_to_all.15.own = bf16[32,16,512]{2,1,0:T(8,128)(2,1)S(1)} all-to-all(bf16[32,16,512]{2,1,0:T(8,128)(2,1)S(1)} %mark.1), channel_id=1, replica_groups=mesh['ref_0'=8,'ref_1'=4,'ref_2'=2,'voc'=4] {'ref_0','ref_1'}, dimensions={0} | all-to-all | bytes 1048576 | tf_op jit(solution)/shard_map/all_to_all | solution.py:487
  31.2 0.0 collective-permute-done.1.swapped
  31.2 2.5 %far_sums.1 = (s16[8,16,512]{2,1,0:T(8,128)(2,1)S(1)}, bf16[12,4,32064]{2,1,0:T(4,128)(2,1)S(1)}, s32[48]{0:T(128)S(1)}) custom-call(s32[12]{0:T(128)} %owner_there.1, s32[12]{0:T(128)S(1)} %collective-permute-done.partner_there, s32[4]{0:T(128)} %counts.1, bf16[12,4,32064]{2,1,0:T(4,128)(2,1)} %source.1, ...), custom_call_target="tpu_custom_call" | custom-call | tf_op jit(solution)/shard_map/far_sums/pallas_call | solution.py:500
  33.8 2.3 %collective-permute-start.2 = (s16[8,16,512]{2,1,0:T(8,128)(2,1)S(1)}, s16[8,16,512]{2,1,0:T(8,128)(2,1)S(1)}, u32[]{:S(2)}, u32[]{:S(2)}) collective-permute-start(s16[8,16,512]{2,1,0:T(8,128)(2,1)S(1)} %get-tuple-element.30), channel_id=1, source_target_pairs={{0,16},{8,24},{16,0},{24,8},{1,17},{9,25},{17,1},{25,9},{2,18},{10... | collective-permute-start | bytes 393224 | tf_op jit(solution)/shard_map/ppermute | solution.py:498
  36.0 1.7 %near_sums.1 = (s16[8,16,512]{2,1,0:T(8,128)(2,1)S(1)}, s16[8,16,512]{2,1,0:T(8,128)(2,1)S(1)}) custom-call(s32[48]{0:T(128)S(1)} %get-tuple-element.25.plan, bf16[12,4,32064]{2,1,0:T(4,128)(2,1)S(1)} %get-tuple-element.26.priv, bf16[12,4,32064]{2,1,0:T(4,128)(2,1)S(1)} %collective-permute-done.1.swapped, bf16[32,16,512]{2,1,0:T(8,128)(2,1)S(1)} %all_to_all.15.own), custom_call_target="tpu_custom_call" | custom-call | tf_op jit(solution)/shard_map/near_sums/pallas_call | solution.py:524
  37.7 1.0 %collective-permute-start.4 = (s16[8,16,512]{2,1,0:T(8,128)(2,1)S(1)}, s16[8,16,512]{2,1,0:T(8,128)(2,1)S(1)}, u32[]{:S(2)}, u32[]{:S(2)}) collective-permute-start(s16[8,16,512]{2,1,0:T(8,128)(2,1)S(1)} %get-tuple-element.31), channel_id=1, source_target_pairs={{0,24},{8,16},{16,8},{24,0},{1,25},{9,17},{17,9},{25,1},{2,26},{10... | collective-permute-start | bytes 393224 | tf_op jit(solution)/shard_map/ppermute | solution.py:498
  38.7 0.0 collective-permute-start.3
  38.7 1.5 %own_sums.1 = (s16[8,16,512]{2,1,0:T(8,128)(2,1)S(1)}, f32[16,512]{1,0:T(8,128)S(1)}, f32[16,512]{1,0:T(8,128)S(1)}, f32[16,128]{1,0:T(8,128)S(1)}, f32[16,128]{1,0:T(8,128)S(1)}) custom-call(bf16[4,4,501]{2,1,0:T(4,128)(2,1)} %public.3, bf16[4,4,501]{2,1,0:T(4,128)(2,1)} %noise.1, s32[4]{0:T(128)} %counts.1, s32[4,4]{1,0:T(4,128)} %tokens.1, ...), custom_call_target="tpu_custom_call" | custom-call | tf_op jit(solution)/shard_map/own_sums/pallas_call | solution.py:539
  40.1 0.0 collective-permute-done.2.b
  40.2 2.9 %collective-permute-done.4.d = s16[8,16,512]{2,1,0:T(8,128)(2,1)S(1)} collective-permute-done((s16[8,16,512]{2,1,0:T(8,128)(2,1)S(1)}, s16[8,16,512]{2,1,0:T(8,128)(2,1)S(1)}, u32[]{:S(2)}, u32[]{:S(2)}) %collective-permute-start.4) | collective-permute-done | bytes 131104 | tf_op jit(solution)/shard_map/ppermute | solution.py:498
  43.1 0.0 collective-permute-done.3.c
  43.1 0.1 join.1
  43.2 11.5 %all_to_all.16.parts = s16[8,16,512]{2,1,0:T(8,128)(2,1)S(1)} all-to-all(s16[8,16,512]{2,1,0:T(8,128)(2,1)S(1)} %join.1), channel_id=1, replica_groups=mesh['ref_0'=8,'ref_1'=4,'ref_2'=2,'voc'=4] {'ref_0'}, dimensions={0} | all-to-all | bytes 262144 | tf_op jit(solution)/shard_map/all_to_all | solution.py:561
  54.7 0.1 finish.1
  54.8 0.1 broadcast_in_dim.3
  54.9 22.2 %all_to_all.17 = f32[256,1,128]{2,1,0:T(1,128)S(1)} all-to-all(f32[256,1,128]{2,1,0:T(1,128)S(1)} %broadcast_in_dim.3), channel_id=1, replica_groups=mesh['ref_0'=8,'ref_1'=4,'ref_2'=2,'voc'=4] {'ref_0','ref_1','ref_2','voc'}, dimensions={0} | all-to-all | bytes 262144 | tf_op jit(solution)/shard_map/all_to_all | solution.py:573
  77.1 0.9 %last.1 = (f32[4,4,501]{2,1,0:T(4,128)}, f32[4,4]{1,0:T(4,128)}) custom-call(f32[256,128]{1,0:T(8,128)S(1)} %bitcast.3, f32[16,512]{1,0:T(8,128)S(1)} %get-tuple-element.37.combined), custom_call_target="tpu_custom_call" | custom-call | tf_op jit(solution)/shard_map/last/pallas_call | solution.py:576
Async XLA Ops:
  0.6 4.2 %collective-permute-start = (s32[12]{0:T(128)}, s32[12]{0:T(128)S(1)}, u32[]{:S(2)}, u32[]{:S(2)}) collective-permute-start(s32[12]{0:T(128)} %owner_there.1), channel_id=1, source_target_pairs={{0,4},{4,0},{1,5},{5,1},{2,6},{6,2},{3,7},{7,3},{8,12},{12,8},{9,1... | collective-permute-start | bytes 152 | tf_op jit(solution)/shard_map/ppermute | solution.py:467
  4.9 26.3 %collective-permute-start.1 = (bf16[12,4,32064]{2,1,0:T(4,128)(2,1)}, bf16[12,4,32064]{2,1,0:T(4,128)(2,1)S(1)}, u32[]{:S(2)}, u32[]{:S(2)}) collective-permute-start(bf16[12,4,32064]{2,1,0:T(4,128)(2,1)} %source.1), channel_id=1, source_target_pairs={{0,4},{4,0},{1,5},{5,1},{2,6},{6,2},{3,7},{7,3},{8,12},{12,8},{9,1... | collective-permute-start | bytes 9234440 | tf_op jit(solution)/shard_map/ppermute | solution.py:478
  33.8 6.4 %collective-permute-start.2 = (s16[8,16,512]{2,1,0:T(8,128)(2,1)S(1)}, s16[8,16,512]{2,1,0:T(8,128)(2,1)S(1)}, u32[]{:S(2)}, u32[]{:S(2)}) collective-permute-start(s16[8,16,512]{2,1,0:T(8,128)(2,1)S(1)} %get-tuple-element.30), channel_id=1, source_target_pairs={{0,16},{8,24},{16,0},{24,8},{1,17},{9,25},{17,1},{25,9},{2,18},{10... | collective-permute-start | bytes 393224 | tf_op jit(solution)/shard_map/ppermute | solution.py:498
  37.7 5.4 %collective-permute-start.4 = (s16[8,16,512]{2,1,0:T(8,128)(2,1)S(1)}, s16[8,16,512]{2,1,0:T(8,128)(2,1)S(1)}, u32[]{:S(2)}, u32[]{:S(2)}) collective-permute-start(s16[8,16,512]{2,1,0:T(8,128)(2,1)S(1)} %get-tuple-element.31), channel_id=1, source_target_pairs={{0,24},{8,16},{16,8},{24,0},{1,25},{9,17},{17,9},{25,1},{2,26},{10... | collective-permute-start | bytes 393224 | tf_op jit(solution)/shard_map/ppermute | solution.py:498
  38.7 4.4 %collective-permute-start.3 = (s16[8,16,512]{2,1,0:T(8,128)(2,1)S(1)}, s16[8,16,512]{2,1,0:T(8,128)(2,1)S(1)}, u32[]{:S(2)}, u32[]{:S(2)}) collective-permute-start(s16[8,16,512]{2,1,0:T(8,128)(2,1)S(1)} %get-tuple-element.27), channel_id=1, source_target_pairs={{0,8},{8,0},{16,24},{24,16},{1,9},{9,1},{17,25},{25,17},{2,10},{10... | collective-permute-start | bytes 393224 | tf_op jit(solution)/shard_map/ppermute | solution.py:498

commit v10 on v9

--- a/solution.py
+++ b/solution.py
@@ -20,7 +20,6 @@
 WINDOW = WIDE + LANES
 GROUP = 4
 AROUND = (2, 1, 3, 0)
-LEAD = LANES
 
 PARAMS = pltpu.CompilerParams(vmem_limit_bytes=16 << 20)
 SMEM = pl.BlockSpec(memory_space=pltpu.SMEM)
@@ -120,12 +119,12 @@
 
 class Rows:
     def __init__(self, plan, priv, swapped):
-        rows, self.positions, self.columns = priv.shape
+        rows, self.positions, self.columns = swapped.shape
         self.entries = []
         for h, held in enumerate((priv, swapped)):
             for r in range(rows):
                 at = h * rows + r
-                self.entries.append((held, r, plan[at], plan[2 * rows + at]))
+                self.entries.append((held, r, plan[at], plan[2 * rows + at], h == 0))
 
 
 def begins(j, core, piece):
@@ -144,7 +143,9 @@
 def fill_strip(rows, strip, entries):
     last = rows.columns // LANES * LANES
     for e in entries:
-        held, r = rows.entries[e][:2]
+        held, r, _, _, packed = rows.entries[e]
+        if packed:
+            continue
         strip[e] = jnp.zeros(strip.shape[1:], strip.dtype)
         strip[e, :, : rows.columns - last] = held[r, :, last:]
 
@@ -164,18 +165,19 @@
 
 def add_rows(rows, pub, acc, core, piece, windows, entries, first, strip=None):
     whole = rows.columns // LANES * LANES
-    bases = [begins(j, core, piece)[0] for j, _, _ in windows]
-    at = [pl.multiple_of(place * WINDOW, LANES) for _, place, _ in windows]
+    bases = [begins(window[0], core, piece)[0] for window in windows]
+    at = [pl.multiple_of(window[1] * WINDOW, LANES) for window in windows]
+    packs = [pl.multiple_of(window[3] * WINDOW, LANES) for window in windows]
     if strip is not None:
         fill_strip(rows, strip, entries)
         ends = [base + WINDOW > rows.columns for base in bases]
         edges = [pl.multiple_of(jnp.minimum(base + WIDE, whole - LANES), LANES) for base in bases]
     for e in entries:
-        held, r, text, slot = rows.entries[e]
+        held, r, text, slot, packed = rows.entries[e]
         for g in range(len(windows)):
-            size = WINDOW if strip is None else WIDE
-            parts = [(0, held[r, :, pl.ds(bases[g], size)])]
-            if strip is not None:
+            size = WINDOW if strip is None or packed else WIDE
+            parts = [(0, held[r, :, pl.ds(packs[g] if packed else bases[g], size)])]
+            if size == WIDE:
                 parts.append((WIDE, jnp.where(ends[g], strip[e], held[r, :, pl.ds(edges[g], LANES)])))
             for offset, value in parts:
                 width = value.shape[1]
@@ -188,7 +190,7 @@
 def store_sums(rows, acc, core, piece, scale, windows, first):
     texts = acc.shape[0] - 1
     lane = lanes_of((texts * rows.positions, LANES))
-    for g, (j, _, store) in enumerate(windows):
+    for g, (j, _, store, _) in enumerate(windows):
         shift = begins(j, core, piece)[1]
         tiles = [
             jnp.concatenate(
@@ -218,9 +220,9 @@
     def kernel(
         owner_there, partner_there, counts_there, source, swapped, own,
         out, priv, plan,
-        pub, acc, strip, owner, partner, counts, left, arrived, small,
+        pub, acc, strip, tail, owner, partner, counts, left, arrived, small,
     ):
-        rows, positions, columns = priv.shape
+        rows, positions, columns = swapped.shape
         texts = pub.shape[0]
         chips, flat, _ = own.shape
         lines, beside = sizes
@@ -229,29 +231,55 @@
         lane = lanes_of((flat, LANES))
         row = lax.broadcasted_iota(jnp.int32, (flat, LANES), 0)
 
-        stride = 2 * beside * piece
-        stride = -(-stride // LANES) * LANES
-
-        def copy_of(i, start, width):
+        def piece_of(n, i):
+            return beside * i + (mine ^ AROUND[n])
+
+        def copy_of(n, i, width=WINDOW):
+            start = begins(piece_of(n, i), core, piece)[0]
+            place = n * lines + i
             return pltpu.make_async_copy(
                 source.at[:, :, pl.ds(start, width)],
-                priv.at[:, :, pl.ds(start, width)],
-                arrived.at[i],
+                priv.at[:, :, place * WINDOW : place * WINDOW + width],
+                arrived.at[place],
             )
 
-        first_chunk = (0, 0, stride + LEAD)
-        last_start = LEAD + (lines - 1) * stride
-        last_chunk = (lines - 1, last_start, columns - last_start)
+        whole = columns // LANES * LANES
+        tail_copy = pltpu.make_async_copy(source.at[:, :, whole:], tail, small.at[3])
+
+        def fill_tail(n):
+            place = (n + 1) * lines - 1
+            ends = begins(piece_of(n, lines - 1), core, piece)[0] + WINDOW > columns
+            start = place * WINDOW + WIDE
+
+            @pl.when(ends)
+            def _():
+                for r in range(rows):
+                    priv[r, :, start : start + columns - whole] = tail[r]
+
+        def each_copy(n, i, act):
+            if i < lines - 1:
+                act(copy_of(n, i))
+                return
+            ends = begins(piece_of(n, i), core, piece)[0] + WINDOW > columns
+
+            @pl.when(ends)
+            def _():
+                act(copy_of(n, i, WIDE))
+
+            @pl.when(jnp.logical_not(ends))
+            def _():
+                act(copy_of(n, i))
+
         pairs = ((owner_there, owner), (partner_there, partner), (counts_there, counts))
         little = [
             pltpu.make_async_copy(there, here, small.at[i]) for i, (there, here) in enumerate(pairs)
         ]
         for copy in little:
             copy.start()
-        copy_of(*first_chunk).start()
-        for i in range(1, lines - 1):
-            copy_of(i, LEAD + i * stride, stride).start()
-        copy_of(*last_chunk).start()
+        tail_copy.start()
+        for n in range(beside):
+            for i in range(lines):
+                each_copy(n, i, lambda copy: copy.start())
 
         def widen(i, earlier):
             for n in range(beside):
@@ -283,7 +311,7 @@
                 plan[2 * rows + at] = jnp.where(still > 0, text, texts)
         acc[texts] = jnp.zeros(acc.shape[1:], jnp.float32)
         held = Rows(plan, priv, swapped)
-        windows = [(beside * i + (mine ^ AROUND[0]), i, storing(out, i)) for i in range(lines)]
+        windows = [(piece_of(0, i), i, storing(out, i), i) for i in range(lines)]
         clear(held, acc, 0, lines)
 
         def add(entries, first):
@@ -293,12 +321,19 @@
 
         for first in range(0, lines, GROUP):
             add(range(rows, 2 * rows), first)
-        copies = {0: first_chunk, lines - 1: last_chunk}
         for first in range(0, lines, GROUP):
             for i in range(first, first + GROUP):
-                copy_of(*copies.get(i, (i, LEAD + i * stride, stride))).wait()
+                each_copy(0, i, lambda copy: copy.wait())
+            if first == 0:
+                tail_copy.wait()
+            if first + GROUP == lines:
+                fill_tail(0)
             add(range(rows), first)
             store_sums(held, acc, core, piece, scale, windows[first : first + GROUP], first)
+        for n in range(1, beside):
+            for i in range(lines):
+                each_copy(n, i, lambda copy: copy.wait())
+            fill_tail(n)
 
     return kernel
 
@@ -321,7 +356,7 @@
                     j = beside * i + (mine ^ AROUND[n])
                     place = 2 * k + n - 1
                     widen_into(pub, place, own[j].astype(jnp.float32), held.positions)
-                    windows.append((j, place, storing(out, i)))
+                    windows.append((j, place, storing(out, i), n * lines + i))
             sum_windows(held, pub, acc, core, piece, scale, windows, strip)
 
         def looped(b, carry):
@@ -349,7 +384,10 @@
             widen_into(pub, i, own[beside * i + mine].astype(jnp.float32), held.positions)
         acc[texts] = jnp.zeros(acc.shape[1:], jnp.float32)
         for first in range(0, lines, GROUP):
-            windows = [(beside * i + mine, i, storing(out, i)) for i in range(first, first + GROUP)]
+            windows = [
+                (beside * i + mine, i, storing(out, i), (beside - 1) * lines + i)
+                for i in range(first, first + GROUP)
+            ]
             last = first + GROUP == lines
             sum_windows(held, pub, acc, core, piece, scale, windows, strip if last else None)
         prepare(sizes, scale / beside, public, noise, counts, tokens, scratch, base, chosen, level, factor)
@@ -451,7 +489,7 @@
 
 def body(private_logits, public_logits, noise, owner, counts, tokens):
     texts, positions, piece = public_logits.shape
-    rows = owner.shape[0]
+    rows, _, columns = private_logits.shape
     flat = texts * positions
     sizes = (lax.axis_size("ref_0"), lax.axis_size("ref_1"))
     chips = sizes[0] * sizes[1]
@@ -501,7 +539,7 @@
         far_kernel(sizes, scale, piece),
         out_shape=(
             line_sums,
-            pltpu.VMEM(private_logits.shape, private_logits.dtype),
+            pltpu.VMEM((rows, positions, beside * windows), private_logits.dtype),
             jax.ShapeDtypeStruct((4 * rows,), jnp.int32),
         ),
         in_specs=[HBM, VMEM, HBM, HBM, VMEM, VMEM],
@@ -510,12 +548,13 @@
             pltpu.VMEM((texts, positions, windows), jnp.float32),
             pltpu.VMEM((texts + 1, positions, windows), jnp.float32),
             strip,
+            pltpu.VMEM((rows, positions, columns % LANES), private_logits.dtype),
             pltpu.SMEM((rows,), jnp.int32),
             pltpu.SMEM((rows,), jnp.int32),
             pltpu.SMEM((texts,), jnp.int32),
             pltpu.SMEM((texts,), jnp.int32),
-            pltpu.SemaphoreType.DMA((lines,)),
-            pltpu.SemaphoreType.DMA((3,)),
+            pltpu.SemaphoreType.DMA((chips,)),
+            pltpu.SemaphoreType.DMA((4,)),
         ],
         compiler_params=PARAMS,
         name="far_sums",

time: 78.4 us -> 78.5 us (level)
  no operation moved by 1% of the time
where the time goes in v10:
time: 78.5 us; the launch traced here: 78 us
  blocking collectives  59.4 us (76%)
  Pallas kernels  7.91 us (10%)
  starting transfers between devices  6.86 us (9%)
  waiting for transfers between devices  3.09 us (4%)
    all_to_all x1, blocking collectives, body(): own = lax.all_to_all(packed, CHIP, split_axis=0, concat_axis=0, tiled=True)  25.8 us
    all_to_all x1, blocking collectives, body(): lax.all_to_all(jnp.broadcast_to(stats, (devices, 1, LANES)), REF_VOC, spl...  22.1 us
    all_to_all x1, blocking collectives, body(): lax.all_to_all(joined, 'ref_0', split_axis=0, concat_axis=0, tiled=True)  11.6 us
    ppermute x1, starting transfers between devices, body(): partner = lax.ppermute(owner, CORE, swap)  3.29 us
    ppermute x3, starting transfers between devices, beyond(): return lax.ppermute(x, 'ref_1', [(k, k ^ m) for k in range(beside)])  3.23 us
    ppermute x3, waiting for transfers between devices, beyond(): return lax.ppermute(x, 'ref_1', [(k, k ^ m) for k in range(beside)])  3.02 us
    pallas_call x1, Pallas kernels, body(): pl.pallas_call(far_kernel(sizes, scale, piece), out_shape=(line_sums, plt...  2.65 us
    pallas_call x1, Pallas kernels, body(): pl.pallas_call(near_kernel(sizes, scale, piece), out_shape=(line_sums, li...  1.62 us
  transfers between devices with their start and end apart: 5, of which 2 were waited for; matrix products, arithmetic and copies ran while one was open for 0% of the time, Pallas kernels for 5%

profile of v10, /device:TPU:1, one launch (start us, length us, event | category | flops | bytes accessed | tf_op | source)
XLA Modules:
  0.0 78.0 jit_solution(672170340604071075)
XLA Ops:
  0.6 3.3 %collective-permute-start = (s32[12]{0:T(128)}, s32[12]{0:T(128)S(1)}, u32[]{:S(2)}, u32[]{:S(2)}) collective-permute-start(s32[12]{0:T(128)} %owner_there.1), channel_id=1, source_target_pairs={{0,4},{4,0},{1,5},{5,1},{2,6},{6,2},{3,7},{7,3},{8,12},{12,8},{9,1... | collective-permute-start | bytes 152 | tf_op jit(solution)/shard_map/ppermute | solution.py:505
  3.9 0.9 %turn.1 = (f32[16,512]{1,0:T(8,128)S(1)}, f32[16,128]{1,0:T(8,128)S(1)}) custom-call(bf16[4,4,501]{2,1,0:T(4,128)(2,1)} %public.3, s32[12]{0:T(128)} %owner_there.1), custom_call_target="tpu_custom_call" | custom-call | tf_op jit(solution)/shard_map/turn/pallas_call | solution.py:506
  4.8 0.1 collective-permute-done.partner_there
  4.9 0.3 collective-permute-start.1
  5.2 0.2 mark.1
  5.4 25.8 %all_to_all.15.own = bf16[32,16,512]{2,1,0:T(8,128)(2,1)S(1)} all-to-all(bf16[32,16,512]{2,1,0:T(8,128)(2,1)S(1)} %mark.1), channel_id=1, replica_groups=mesh['ref_0'=8,'ref_1'=4,'ref_2'=2,'voc'=4] {'ref_0','ref_1'}, dimensions={0} | all-to-all | bytes 1048576 | tf_op jit(solution)/shard_map/all_to_all | solution.py:525
  31.2 0.0 collective-permute-done.1.swapped
  31.2 2.6 %far_sums.1 = (s16[8,16,512]{2,1,0:T(8,128)(2,1)S(1)}, bf16[12,4,20480]{2,1,0:T(4,128)(2,1)S(1)}, s32[48]{0:T(128)S(1)}) custom-call(s32[12]{0:T(128)} %owner_there.1, s32[12]{0:T(128)S(1)} %collective-permute-done.partner_there, s32[4]{0:T(128)} %counts.1, bf16[12,4,32064]{2,1,0:T(4,128)(2,1)} %source.1, ...), custom_call_target="tpu_custom_call" | custom-call | tf_op jit(solution)/shard_map/far_sums/pallas_call | solution.py:538
  33.9 2.3 %collective-permute-start.2 = (s16[8,16,512]{2,1,0:T(8,128)(2,1)S(1)}, s16[8,16,512]{2,1,0:T(8,128)(2,1)S(1)}, u32[]{:S(2)}, u32[]{:S(2)}) collective-permute-start(s16[8,16,512]{2,1,0:T(8,128)(2,1)S(1)} %get-tuple-element.30), channel_id=1, source_target_pairs={{0,16},{8,24},{16,0},{24,8},{1,17},{9,25},{17,1},{25,9},{2,18},{10... | collective-permute-start | bytes 393224 | tf_op jit(solution)/shard_map/ppermute | solution.py:536
  36.1 1.6 %near_sums.1 = (s16[8,16,512]{2,1,0:T(8,128)(2,1)S(1)}, s16[8,16,512]{2,1,0:T(8,128)(2,1)S(1)}) custom-call(s32[48]{0:T(128)S(1)} %get-tuple-element.25.plan, bf16[12,4,20480]{2,1,0:T(4,128)(2,1)S(1)} %get-tuple-element.26.priv, bf16[12,4,32064]{2,1,0:T(4,128)(2,1)S(1)} %collective-permute-done.1.swapped, bf16[32,16,512]{2,1,0:T(8,128)(2,1)S(1)} %all_to_all.15.own), custom_call_target="tpu_custom_call" | custom-call | tf_op jit(solution)/shard_map/near_sums/pallas_call | solution.py:563
  37.8 1.0 %collective-permute-start.4 = (s16[8,16,512]{2,1,0:T(8,128)(2,1)S(1)}, s16[8,16,512]{2,1,0:T(8,128)(2,1)S(1)}, u32[]{:S(2)}, u32[]{:S(2)}) collective-permute-start(s16[8,16,512]{2,1,0:T(8,128)(2,1)S(1)} %get-tuple-element.31), channel_id=1, source_target_pairs={{0,24},{8,16},{16,8},{24,0},{1,25},{9,17},{17,9},{25,1},{2,26},{10... | collective-permute-start | bytes 393224 | tf_op jit(solution)/shard_map/ppermute | solution.py:536
  38.7 0.0 collective-permute-start.3
  38.7 1.4 %own_sums.1 = (s16[8,16,512]{2,1,0:T(8,128)(2,1)S(1)}, f32[16,512]{1,0:T(8,128)S(1)}, f32[16,512]{1,0:T(8,128)S(1)}, f32[16,128]{1,0:T(8,128)S(1)}, f32[16,128]{1,0:T(8,128)S(1)}) custom-call(bf16[4,4,501]{2,1,0:T(4,128)(2,1)} %public.3, bf16[4,4,501]{2,1,0:T(4,128)(2,1)} %noise.1, s32[4]{0:T(128)} %counts.1, s32[4,4]{1,0:T(4,128)} %tokens.1, ...), custom_call_target="tpu_custom_call" | custom-call | tf_op jit(solution)/shard_map/own_sums/pallas_call | solution.py:578
  40.2 0.0 collective-permute-done.2.b
  40.2 3.0 %collective-permute-done.4.d = s16[8,16,512]{2,1,0:T(8,128)(2,1)S(1)} collective-permute-done((s16[8,16,512]{2,1,0:T(8,128)(2,1)S(1)}, s16[8,16,512]{2,1,0:T(8,128)(2,1)S(1)}, u32[]{:S(2)}, u32[]{:S(2)}) %collective-permute-start.4) | collective-permute-done | bytes 131104 | tf_op jit(solution)/shard_map/ppermute | solution.py:536
  43.2 0.0 collective-permute-done.3.c
  43.2 0.1 join.1
  43.3 11.6 %all_to_all.16.parts = s16[8,16,512]{2,1,0:T(8,128)(2,1)S(1)} all-to-all(s16[8,16,512]{2,1,0:T(8,128)(2,1)S(1)} %join.1), channel_id=1, replica_groups=mesh['ref_0'=8,'ref_1'=4,'ref_2'=2,'voc'=4] {'ref_0'}, dimensions={0} | all-to-all | bytes 262144 | tf_op jit(solution)/shard_map/all_to_all | solution.py:600
  54.8 0.1 finish.1
  55.0 0.1 broadcast_in_dim.3
  55.0 22.1 %all_to_all.17 = f32[256,1,128]{2,1,0:T(1,128)S(1)} all-to-all(f32[256,1,128]{2,1,0:T(1,128)S(1)} %broadcast_in_dim.3), channel_id=1, replica_groups=mesh['ref_0'=8,'ref_1'=4,'ref_2'=2,'voc'=4] {'ref_0','ref_1','ref_2','voc'}, dimensions={0} | all-to-all | bytes 262144 | tf_op jit(solution)/shard_map/all_to_all | solution.py:612
  77.1 0.9 %last.1 = (f32[4,4,501]{2,1,0:T(4,128)}, f32[4,4]{1,0:T(4,128)}) custom-call(f32[256,128]{1,0:T(8,128)S(1)} %bitcast.3, f32[16,512]{1,0:T(8,128)S(1)} %get-tuple-element.37.combined), custom_call_target="tpu_custom_call" | custom-call | tf_op jit(solution)/shard_map/last/pallas_call | solution.py:615
Async XLA Ops:
  0.6 4.2 %collective-permute-start = (s32[12]{0:T(128)}, s32[12]{0:T(128)S(1)}, u32[]{:S(2)}, u32[]{:S(2)}) collective-permute-start(s32[12]{0:T(128)} %owner_there.1), channel_id=1, source_target_pairs={{0,4},{4,0},{1,5},{5,1},{2,6},{6,2},{3,7},{7,3},{8,12},{12,8},{9,1... | collective-permute-start | bytes 152 | tf_op jit(solution)/shard_map/ppermute | solution.py:505
  4.9 26.3 %collective-permute-start.1 = (bf16[12,4,32064]{2,1,0:T(4,128)(2,1)}, bf16[12,4,32064]{2,1,0:T(4,128)(2,1)S(1)}, u32[]{:S(2)}, u32[]{:S(2)}) collective-permute-start(bf16[12,4,32064]{2,1,0:T(4,128)(2,1)} %source.1), channel_id=1, source_target_pairs={{0,4},{4,0},{1,5},{5,1},{2,6},{6,2},{3,7},{7,3},{8,12},{12,8},{9,1... | collective-permute-start | bytes 9234440 | tf_op jit(solution)/shard_map/ppermute | solution.py:516
  33.9 6.3 %collective-permute-start.2 = (s16[8,16,512]{2,1,0:T(8,128)(2,1)S(1)}, s16[8,16,512]{2,1,0:T(8,128)(2,1)S(1)}, u32[]{:S(2)}, u32[]{:S(2)}) collective-permute-start(s16[8,16,512]{2,1,0:T(8,128)(2,1)S(1)} %get-tuple-element.30), channel_id=1, source_target_pairs={{0,16},{8,24},{16,0},{24,8},{1,17},{9,25},{17,1},{25,9},{2,18},{10... | collective-permute-start | bytes 393224 | tf_op jit(solution)/shard_map/ppermute | solution.py:536
  37.8 5.4 %collective-permute-start.4 = (s16[8,16,512]{2,1,0:T(8,128)(2,1)S(1)}, s16[8,16,512]{2,1,0:T(8,128)(2,1)S(1)}, u32[]{:S(2)}, u32[]{:S(2)}) collective-permute-start(s16[8,16,512]{2,1,0:T(8,128)(2,1)S(1)} %get-tuple-element.31), channel_id=1, source_target_pairs={{0,24},{8,16},{16,8},{24,0},{1,25},{9,17},{17,9},{25,1},{2,26},{10... | collective-permute-start | bytes 393224 | tf_op jit(solution)/shard_map/ppermute | solution.py:536
  38.7 4.5 %collective-permute-start.3 = (s16[8,16,512]{2,1,0:T(8,128)(2,1)S(1)}, s16[8,16,512]{2,1,0:T(8,128)(2,1)S(1)}, u32[]{:S(2)}, u32[]{:S(2)}) collective-permute-start(s16[8,16,512]{2,1,0:T(8,128)(2,1)S(1)} %get-tuple-element.27), channel_id=1, source_target_pairs={{0,8},{8,0},{16,24},{24,16},{1,9},{9,1},{17,25},{25,17},{2,10},{10... | collective-permute-start | bytes 393224 | tf_op jit(solution)/shard_map/ppermute | solution.py:536

commit v11 on v10

--- a/solution.py
+++ b/solution.py
@@ -118,13 +118,13 @@
 
 
 class Rows:
-    def __init__(self, plan, priv, swapped):
+    def __init__(self, plan, priv, swapped, packed=False):
         rows, self.positions, self.columns = swapped.shape
         self.entries = []
         for h, held in enumerate((priv, swapped)):
             for r in range(rows):
                 at = h * rows + r
-                self.entries.append((held, r, plan[at], plan[2 * rows + at], h == 0))
+                self.entries.append((held, r, plan[at], plan[2 * rows + at], packed and h == 0))
 
 
 def begins(j, core, piece):
@@ -219,8 +219,8 @@
 def far_kernel(sizes, scale, piece):
     def kernel(
         owner_there, partner_there, counts_there, source, swapped, own,
-        out, priv, plan,
-        pub, acc, strip, tail, owner, partner, counts, left, arrived, small,
+        out, plan,
+        priv, pub, acc, strip, tail, owner, partner, counts, left, arrived, small,
     ):
         rows, positions, columns = swapped.shape
         texts = pub.shape[0]
@@ -277,9 +277,8 @@
         for copy in little:
             copy.start()
         tail_copy.start()
-        for n in range(beside):
-            for i in range(lines):
-                each_copy(n, i, lambda copy: copy.start())
+        for i in range(lines):
+            each_copy(0, i, lambda copy: copy.start())
 
         def widen(i, earlier):
             for n in range(beside):
@@ -310,7 +309,7 @@
                 plan[at] = text
                 plan[2 * rows + at] = jnp.where(still > 0, text, texts)
         acc[texts] = jnp.zeros(acc.shape[1:], jnp.float32)
-        held = Rows(plan, priv, swapped)
+        held = Rows(plan, priv, swapped, packed=True)
         windows = [(piece_of(0, i), i, storing(out, i), i) for i in range(lines)]
         clear(held, acc, 0, lines)
 
@@ -330,10 +329,6 @@
                 fill_tail(0)
             add(range(rows), first)
             store_sums(held, acc, core, piece, scale, windows[first : first + GROUP], first)
-        for n in range(1, beside):
-            for i in range(lines):
-                each_copy(n, i, lambda copy: copy.wait())
-            fill_tail(n)
 
     return kernel
 
@@ -356,7 +351,7 @@
                     j = beside * i + (mine ^ AROUND[n])
                     place = 2 * k + n - 1
                     widen_into(pub, place, own[j].astype(jnp.float32), held.positions)
-                    windows.append((j, place, storing(out, i), n * lines + i))
+                    windows.append((j, place, storing(out, i), 0))
             sum_windows(held, pub, acc, core, piece, scale, windows, strip)
 
         def looped(b, carry):
@@ -385,7 +380,7 @@
         acc[texts] = jnp.zeros(acc.shape[1:], jnp.float32)
         for first in range(0, lines, GROUP):
             windows = [
-                (beside * i + mine, i, storing(out, i), (beside - 1) * lines + i)
+                (beside * i + mine, i, storing(out, i), 0)
                 for i in range(first, first + GROUP)
             ]
             last = first + GROUP == lines
@@ -535,16 +530,17 @@
     def beyond(x, m):
         return lax.ppermute(x, "ref_1", [(k, k ^ m) for k in range(beside)])
 
-    far, private_here, plan = pl.pallas_call(
+    private_here = pltpu.with_memory_space_constraint(private_logits, pltpu.VMEM)
+    far, plan = pl.pallas_call(
         far_kernel(sizes, scale, piece),
         out_shape=(
             line_sums,
-            pltpu.VMEM((rows, positions, beside * windows), private_logits.dtype),
             jax.ShapeDtypeStruct((4 * rows,), jnp.int32),
         ),
         in_specs=[HBM, VMEM, HBM, HBM, VMEM, VMEM],
-        out_specs=(VMEM, VMEM, SMEM),
+        out_specs=(VMEM, SMEM),
         scratch_shapes=[
+            pltpu.VMEM((rows, positions, windows), private_logits.dtype),
             pltpu.VMEM((texts, positions, windows), jnp.float32),
             pltpu.VMEM((texts + 1, positions, windows), jnp.float32),
             strip,
@@ -553,7 +549,7 @@
             pltpu.SMEM((rows,), jnp.int32),
             pltpu.SMEM((texts,), jnp.int32),
             pltpu.SMEM((texts,), jnp.int32),
-            pltpu.SemaphoreType.DMA((chips,)),
+            pltpu.SemaphoreType.DMA((lines,)),
             pltpu.SemaphoreType.DMA((4,)),
         ],
         compiler_params=PARAMS,

time: 78.5 us -> 78 us (level)
  no operation moved by 1% of the time
where the time goes in v11:
time: 78 us; the launch traced here: 77.6 us
  blocking collectives  59.5 us (76%)
  Pallas kernels  7.49 us (10%)
  starting transfers between devices  6.85 us (9%)
  waiting for transfers between devices  2.99 us (4%)
    all_to_all x1, blocking collectives, body(): own = lax.all_to_all(packed, CHIP, split_axis=0, concat_axis=0, tiled=True)  25.8 us
    all_to_all x1, blocking collectives, body(): lax.all_to_all(jnp.broadcast_to(stats, (devices, 1, LANES)), REF_VOC, spl...  22.2 us
    all_to_all x1, blocking collectives, body(): lax.all_to_all(joined, 'ref_0', split_axis=0, concat_axis=0, tiled=True)  11.5 us
    ppermute x1, starting transfers between devices, body(): partner = lax.ppermute(owner, CORE, swap)  3.29 us
    ppermute x3, starting transfers between devices, beyond(): return lax.ppermute(x, 'ref_1', [(k, k ^ m) for k in range(beside)])  3.22 us
    ppermute x3, waiting for transfers between devices, beyond(): return lax.ppermute(x, 'ref_1', [(k, k ^ m) for k in range(beside)])  2.92 us
    pallas_call x1, Pallas kernels, body(): pl.pallas_call(far_kernel(sizes, scale, piece), out_shape=(line_sums, jax...  2.11 us
    pallas_call x1, Pallas kernels, body(): pl.pallas_call(near_kernel(sizes, scale, piece), out_shape=(line_sums, li...  1.69 us
  transfers between devices with their start and end apart: 5, of which 2 were waited for; matrix products, arithmetic and copies ran while one was open for 0% of the time, Pallas kernels for 5%

profile of v11, /device:TPU:1, one launch (start us, length us, event | category | flops | bytes accessed | tf_op | source)
XLA Modules:
  0.0 77.6 jit_solution(755969770945164732)
XLA Ops:
  0.6 3.3 %collective-permute-start = (s32[12]{0:T(128)}, s32[12]{0:T(128)S(1)}, u32[]{:S(2)}, u32[]{:S(2)}) collective-permute-start(s32[12]{0:T(128)} %owner_there.1), channel_id=1, source_target_pairs={{0,4},{4,0},{1,5},{5,1},{2,6},{6,2},{3,7},{7,3},{8,12},{12,8},{9,1... | collective-permute-start | bytes 152 | tf_op jit(solution)/shard_map/ppermute | solution.py:500
  3.9 0.9 %turn.1 = (f32[16,512]{1,0:T(8,128)S(1)}, f32[16,128]{1,0:T(8,128)S(1)}) custom-call(bf16[4,4,501]{2,1,0:T(4,128)(2,1)} %public.3, s32[12]{0:T(128)} %owner_there.1), custom_call_target="tpu_custom_call" | custom-call | tf_op jit(solution)/shard_map/turn/pallas_call | solution.py:501
  4.8 0.1 collective-permute-done.partner_there
  4.9 0.3 collective-permute-start.1
  5.2 0.2 mark.1
  5.4 25.8 %all_to_all.15.own = bf16[32,16,512]{2,1,0:T(8,128)(2,1)S(1)} all-to-all(bf16[32,16,512]{2,1,0:T(8,128)(2,1)S(1)} %mark.1), channel_id=1, replica_groups=mesh['ref_0'=8,'ref_1'=4,'ref_2'=2,'voc'=4] {'ref_0','ref_1'}, dimensions={0} | all-to-all | bytes 1048576 | tf_op jit(solution)/shard_map/all_to_all | solution.py:520
  31.2 0.0 copy-start
  31.2 0.0 collective-permute-done.1.swapped
  31.2 2.1 %far_sums.1 = (s16[8,16,512]{2,1,0:T(8,128)(2,1)S(1)}, s32[48]{0:T(128)S(1)}) custom-call(s32[12]{0:T(128)} %owner_there.1, s32[12]{0:T(128)S(1)} %collective-permute-done.partner_there, s32[4]{0:T(128)} %counts.1, bf16[12,4,32064]{2,1,0:T(4,128)(2,1)} %priv.3, bf16[12,4,32064]{2,1,0:T(4,128)(2,1)S(1)} %collective-permute-done.1.swapped, ...), custom_call_target="tpu_custom_call" | custom-call | tf_op jit(solution)/shard_map/far_sums/pallas_call | solution.py:534
  33.3 2.3 %collective-permute-start.2 = (s16[8,16,512]{2,1,0:T(8,128)(2,1)S(1)}, s16[8,16,512]{2,1,0:T(8,128)(2,1)S(1)}, u32[]{:S(2)}, u32[]{:S(2)}) collective-permute-start(s16[8,16,512]{2,1,0:T(8,128)(2,1)S(1)} %get-tuple-element.28), channel_id=1, source_target_pairs={{0,16},{8,24},{16,0},{24,8},{1,17},{9,25},{17,1},{25,9},{2,18},{10... | collective-permute-start | bytes 393224 | tf_op jit(solution)/shard_map/ppermute | solution.py:531
  35.6 0.0 copy-done
  35.6 1.7 %near_sums.1 = (s16[8,16,512]{2,1,0:T(8,128)(2,1)S(1)}, s16[8,16,512]{2,1,0:T(8,128)(2,1)S(1)}) custom-call(s32[48]{0:T(128)S(1)} %get-tuple-element.24.plan, bf16[12,4,32064]{2,1,0:T(4,128)(2,1)S(1)} %copy-done, bf16[12,4,32064]{2,1,0:T(4,128)(2,1)S(1)} %collective-permute-done.1.swapped, bf16[32,16,512]{2,1,0:T(8,128)(2,1)S(1)} %all_to_all.15.own), custom_call_target="tpu_custom_call" | custom-call | tf_op jit(solution)/shard_map/near_sums/pallas_call | solution.py:559
  37.3 1.0 %collective-permute-start.4 = (s16[8,16,512]{2,1,0:T(8,128)(2,1)S(1)}, s16[8,16,512]{2,1,0:T(8,128)(2,1)S(1)}, u32[]{:S(2)}, u32[]{:S(2)}) collective-permute-start(s16[8,16,512]{2,1,0:T(8,128)(2,1)S(1)} %get-tuple-element.29), channel_id=1, source_target_pairs={{0,24},{8,16},{16,8},{24,0},{1,25},{9,17},{17,9},{25,1},{2,26},{10... | collective-permute-start | bytes 393224 | tf_op jit(solution)/shard_map/ppermute | solution.py:531
  38.2 0.0 collective-permute-start.3
  38.2 1.5 %own_sums.1 = (s16[8,16,512]{2,1,0:T(8,128)(2,1)S(1)}, f32[16,512]{1,0:T(8,128)S(1)}, f32[16,512]{1,0:T(8,128)S(1)}, f32[16,128]{1,0:T(8,128)S(1)}, f32[16,128]{1,0:T(8,128)S(1)}) custom-call(bf16[4,4,501]{2,1,0:T(4,128)(2,1)} %public.3, bf16[4,4,501]{2,1,0:T(4,128)(2,1)} %noise.1, s32[4]{0:T(128)} %counts.1, s32[4,4]{1,0:T(4,128)} %tokens.1, ...), custom_call_target="tpu_custom_call" | custom-call | tf_op jit(solution)/shard_map/own_sums/pallas_call | solution.py:574
  39.7 0.0 collective-permute-done.2.b
  39.7 2.9 %collective-permute-done.4.d = s16[8,16,512]{2,1,0:T(8,128)(2,1)S(1)} collective-permute-done((s16[8,16,512]{2,1,0:T(8,128)(2,1)S(1)}, s16[8,16,512]{2,1,0:T(8,128)(2,1)S(1)}, u32[]{:S(2)}, u32[]{:S(2)}) %collective-permute-start.4) | collective-permute-done | bytes 131104 | tf_op jit(solution)/shard_map/ppermute | solution.py:531
  42.7 0.0 collective-permute-done.3.c
  42.7 0.1 join.1
  42.8 11.5 %all_to_all.16.parts = s16[8,16,512]{2,1,0:T(8,128)(2,1)S(1)} all-to-all(s16[8,16,512]{2,1,0:T(8,128)(2,1)S(1)} %join.1), channel_id=1, replica_groups=mesh['ref_0'=8,'ref_1'=4,'ref_2'=2,'voc'=4] {'ref_0'}, dimensions={0} | all-to-all | bytes 262144 | tf_op jit(solution)/shard_map/all_to_all | solution.py:596
  54.3 0.1 finish.1
  54.4 0.1 broadcast_in_dim.3
  54.5 22.2 %all_to_all.17 = f32[256,1,128]{2,1,0:T(1,128)S(1)} all-to-all(f32[256,1,128]{2,1,0:T(1,128)S(1)} %broadcast_in_dim.3), channel_id=1, replica_groups=mesh['ref_0'=8,'ref_1'=4,'ref_2'=2,'voc'=4] {'ref_0','ref_1','ref_2','voc'}, dimensions={0} | all-to-all | bytes 262144 | tf_op jit(solution)/shard_map/all_to_all | solution.py:608
  76.6 0.9 %last.1 = (f32[4,4,501]{2,1,0:T(4,128)}, f32[4,4]{1,0:T(4,128)}) custom-call(f32[256,128]{1,0:T(8,128)S(1)} %bitcast.3, f32[16,512]{1,0:T(8,128)S(1)} %get-tuple-element.35.combined), custom_call_target="tpu_custom_call" | custom-call | tf_op jit(solution)/shard_map/last/pallas_call | solution.py:611
Async XLA Ops:
  0.6 4.2 %collective-permute-start = (s32[12]{0:T(128)}, s32[12]{0:T(128)S(1)}, u32[]{:S(2)}, u32[]{:S(2)}) collective-permute-start(s32[12]{0:T(128)} %owner_there.1), channel_id=1, source_target_pairs={{0,4},{4,0},{1,5},{5,1},{2,6},{6,2},{3,7},{7,3},{8,12},{12,8},{9,1... | collective-permute-start | bytes 152 | tf_op jit(solution)/shard_map/ppermute | solution.py:500
  4.9 26.3 %collective-permute-start.1 = (bf16[12,4,32064]{2,1,0:T(4,128)(2,1)}, bf16[12,4,32064]{2,1,0:T(4,128)(2,1)S(1)}, u32[]{:S(2)}, u32[]{:S(2)}) collective-permute-start(bf16[12,4,32064]{2,1,0:T(4,128)(2,1)} %priv.3), channel_id=1, source_target_pairs={{0,4},{4,0},{1,5},{5,1},{2,6},{6,2},{3,7},{7,3},{8,12},{12,8},{9,1... | collective-permute-start | bytes 9234440 | tf_op jit(solution)/shard_map/ppermute | solution.py:511
  31.2 4.4 %copy-start = (bf16[12,4,32064]{2,1,0:T(4,128)(2,1)S(1)}, bf16[12,4,32064]{2,1,0:T(4,128)(2,1)}, u32[]{:S(2)}) copy-start(bf16[12,4,32064]{2,1,0:T(4,128)(2,1)} %priv.3) | copy-start | bytes 9234436
  33.3 6.4 %collective-permute-start.2 = (s16[8,16,512]{2,1,0:T(8,128)(2,1)S(1)}, s16[8,16,512]{2,1,0:T(8,128)(2,1)S(1)}, u32[]{:S(2)}, u32[]{:S(2)}) collective-permute-start(s16[8,16,512]{2,1,0:T(8,128)(2,1)S(1)} %get-tuple-element.28), channel_id=1, source_target_pairs={{0,16},{8,24},{16,0},{24,8},{1,17},{9,25},{17,1},{25,9},{2,18},{10... | collective-permute-start | bytes 393224 | tf_op jit(solution)/shard_map/ppermute | solution.py:531
  37.3 5.4 %collective-permute-start.4 = (s16[8,16,512]{2,1,0:T(8,128)(2,1)S(1)}, s16[8,16,512]{2,1,0:T(8,128)(2,1)S(1)}, u32[]{:S(2)}, u32[]{:S(2)}) collective-permute-start(s16[8,16,512]{2,1,0:T(8,128)(2,1)S(1)} %get-tuple-element.29), channel_id=1, source_target_pairs={{0,24},{8,16},{16,8},{24,0},{1,25},{9,17},{17,9},{25,1},{2,26},{10... | collective-permute-start | bytes 393224 | tf_op jit(solution)/shard_map/ppermute | solution.py:531
  38.2 4.4 %collective-permute-start.3 = (s16[8,16,512]{2,1,0:T(8,128)(2,1)S(1)}, s16[8,16,512]{2,1,0:T(8,128)(2,1)S(1)}, u32[]{:S(2)}, u32[]{:S(2)}) collective-permute-start(s16[8,16,512]{2,1,0:T(8,128)(2,1)S(1)} %get-tuple-element.25), channel_id=1, source_target_pairs={{0,8},{8,0},{16,24},{24,16},{1,9},{9,1},{17,25},{25,17},{2,10},{10... | collective-permute-start | bytes 393224 | tf_op jit(solution)/shard_map/ppermute | solution.py:531

commit v12 on v11

--- a/solution.py
+++ b/solution.py
@@ -555,7 +555,6 @@
         compiler_params=PARAMS,
         name="far_sums",
     )(owner_there, partner, counts_there, private_there, swapped, own)
-    got = [beyond(far, AROUND[0])]
     near = pl.pallas_call(
         near_kernel(sizes, scale, piece),
         out_shape=(line_sums, line_sums),
@@ -569,7 +568,8 @@
         compiler_params=PARAMS,
         name="near_sums",
     )(plan, private_here, swapped, own)
-    got += [beyond(x, m) for x, m in zip(near, AROUND[1:])]
+    away = lax.optimization_barrier((far, *near))
+    got = [beyond(x, m) for x, m in zip(away, AROUND)]
     near_done, own_later = lax.optimization_barrier((near[0], own))
     line, base, chosen, level, factor = pl.pallas_call(
         own_kernel(sizes, scale, piece),

time: 78 us -> 78.5 us (level)
  waiting for transfers between devices: 2.99 us -> 5.09 us
  blocking collectives: 59.5 us -> 57.8 us
    ppermute x3, waiting for transfers between devices: 2.92 us -> 5.02 us  [beyond(): return lax.ppermute(x, 'ref_1', [(k, k ^ m) for k in range(beside)])]
    all_to_all x1, blocking collectives: 22.2 us -> 21.1 us  [body(): lax.all_to_all(jnp.broadcast_to(stats, (devices, 1, LANES)), REF_VOC, spl...]
  transfers between devices with their start and end apart: 5 -> 5, of which waited for: 2 -> 4; matrix products, arithmetic and copies ran while one was open for 0% -> 0% of each run, Pallas kernels for 5% -> 3%
where the time goes in v12:
time: 78.5 us; the launch traced here: 78.1 us
  blocking collectives  57.8 us (74%)
  Pallas kernels  7.48 us (10%)
  starting transfers between devices  6.97 us (9%)
  waiting for transfers between devices  5.09 us (6%)
    all_to_all x1, blocking collectives, body(): own = lax.all_to_all(packed, CHIP, split_axis=0, concat_axis=0, tiled=True)  25.8 us
    all_to_all x1, blocking collectives, body(): lax.all_to_all(jnp.broadcast_to(stats, (devices, 1, LANES)), REF_VOC, spl...  21.1 us
    all_to_all x1, blocking collectives, body(): lax.all_to_all(joined, 'ref_0', split_axis=0, concat_axis=0, tiled=True)  10.9 us
    ppermute x3, waiting for transfers between devices, beyond(): return lax.ppermute(x, 'ref_1', [(k, k ^ m) for k in range(beside)])  5.02 us
    ppermute x3, starting transfers between devices, beyond(): return lax.ppermute(x, 'ref_1', [(k, k ^ m) for k in range(beside)])  3.34 us
    ppermute x1, starting transfers between devices, body(): partner = lax.ppermute(owner, CORE, swap)  3.29 us
    pallas_call x1, Pallas kernels, body(): pl.pallas_call(far_kernel(sizes, scale, piece), out_shape=(line_sums, jax...  2.11 us
    pallas_call x1, Pallas kernels, body(): pl.pallas_call(near_kernel(sizes, scale, piece), out_shape=(line_sums, li...  1.67 us
  transfers between devices with their start and end apart: 5, of which 4 were waited for; matrix products, arithmetic and copies ran while one was open for 0% of the time, Pallas kernels for 3%

profile of v12, /device:TPU:1, one launch (start us, length us, event | category | flops | bytes accessed | tf_op | source)
XLA Modules:
  0.0 78.1 jit_solution(8978452135485243340)
XLA Ops:
  0.6 3.3 %collective-permute-start = (s32[12]{0:T(128)}, s32[12]{0:T(128)S(1)}, u32[]{:S(2)}, u32[]{:S(2)}) collective-permute-start(s32[12]{0:T(128)} %owner_there.1), channel_id=1, source_target_pairs={{0,4},{4,0},{1,5},{5,1},{2,6},{6,2},{3,7},{7,3},{8,12},{12,8},{9,1... | collective-permute-start | bytes 152 | tf_op jit(solution)/shard_map/ppermute | solution.py:500
  3.9 0.9 %turn.1 = (f32[16,512]{1,0:T(8,128)S(1)}, f32[16,128]{1,0:T(8,128)S(1)}) custom-call(bf16[4,4,501]{2,1,0:T(4,128)(2,1)} %public.3, s32[12]{0:T(128)} %owner_there.1), custom_call_target="tpu_custom_call" | custom-call | tf_op jit(solution)/shard_map/turn/pallas_call | solution.py:501
  4.8 0.1 collective-permute-done.partner_there
  4.9 0.3 collective-permute-start.1
  5.2 0.2 mark.1
  5.4 25.8 %all_to_all.15.own = bf16[32,16,512]{2,1,0:T(8,128)(2,1)S(1)} all-to-all(bf16[32,16,512]{2,1,0:T(8,128)(2,1)S(1)} %mark.1), channel_id=1, replica_groups=mesh['ref_0'=8,'ref_1'=4,'ref_2'=2,'voc'=4] {'ref_0','ref_1'}, dimensions={0} | all-to-all | bytes 1048576 | tf_op jit(solution)/shard_map/all_to_all | solution.py:520
  31.2 0.0 copy-start
  31.2 0.0 collective-permute-done.1.swapped
  31.2 2.1 %far_sums.1 = (s16[8,16,512]{2,1,0:T(8,128)(2,1)S(1)}, s32[48]{0:T(128)S(1)}) custom-call(s32[12]{0:T(128)} %owner_there.1, s32[12]{0:T(128)S(1)} %collective-permute-done.partner_there, s32[4]{0:T(128)} %counts.1, bf16[12,4,32064]{2,1,0:T(4,128)(2,1)} %priv.3, bf16[12,4,32064]{2,1,0:T(4,128)(2,1)S(1)} %collective-permute-done.1.swapped, ...), custom_call_target="tpu_custom_call" | custom-call | tf_op jit(solution)/shard_map/far_sums/pallas_call | solution.py:534
  33.3 0.0 copy-done
  33.3 1.7 %near_sums.1 = (s16[8,16,512]{2,1,0:T(8,128)(2,1)S(1)}, s16[8,16,512]{2,1,0:T(8,128)(2,1)S(1)}) custom-call(s32[48]{0:T(128)S(1)} %get-tuple-element.27.plan, bf16[12,4,32064]{2,1,0:T(4,128)(2,1)S(1)} %copy-done, bf16[12,4,32064]{2,1,0:T(4,128)(2,1)S(1)} %collective-permute-done.1.swapped, bf16[32,16,512]{2,1,0:T(8,128)(2,1)S(1)} %all_to_all.15.own), custom_call_target="tpu_custom_call" | custom-call | tf_op jit(solution)/shard_map/near_sums/pallas_call | solution.py:558
  35.0 2.3 %collective-permute-start.2 = (s16[8,16,512]{2,1,0:T(8,128)(2,1)S(1)}, s16[8,16,512]{2,1,0:T(8,128)(2,1)S(1)}, u32[]{:S(2)}, u32[]{:S(2)}) collective-permute-start(s16[8,16,512]{2,1,0:T(8,128)(2,1)S(1)} %get-tuple-element.33), channel_id=1, source_target_pairs={{0,16},{8,24},{16,0},{24,8},{1,17},{9,25},{17,1},{25,9},{2,18},{10... | collective-permute-start | bytes 393224 | tf_op jit(solution)/shard_map/ppermute | solution.py:531
  37.3 0.7 collective-permute-start.3
  38.0 0.4 collective-permute-start.4
  38.4 1.5 %own_sums.1 = (s16[8,16,512]{2,1,0:T(8,128)(2,1)S(1)}, f32[16,512]{1,0:T(8,128)S(1)}, f32[16,512]{1,0:T(8,128)S(1)}, f32[16,128]{1,0:T(8,128)S(1)}, f32[16,128]{1,0:T(8,128)S(1)}) custom-call(bf16[4,4,501]{2,1,0:T(4,128)(2,1)} %public.3, bf16[4,4,501]{2,1,0:T(4,128)(2,1)} %noise.1, s32[4]{0:T(128)} %counts.1, s32[4,4]{1,0:T(4,128)} %tokens.1, ...), custom_call_target="tpu_custom_call" | custom-call | tf_op jit(solution)/shard_map/own_sums/pallas_call | solution.py:574
  39.8 0.6 collective-permute-done.2.b
  40.4 2.4 %collective-permute-done.3.c = s16[8,16,512]{2,1,0:T(8,128)(2,1)S(1)} collective-permute-done((s16[8,16,512]{2,1,0:T(8,128)(2,1)S(1)}, s16[8,16,512]{2,1,0:T(8,128)(2,1)S(1)}, u32[]{:S(2)}, u32[]{:S(2)}) %collective-permute-start.3) | collective-permute-done | bytes 131104 | tf_op jit(solution)/shard_map/ppermute | solution.py:531
  42.8 2.1 %collective-permute-done.4.d = s16[8,16,512]{2,1,0:T(8,128)(2,1)S(1)} collective-permute-done((s16[8,16,512]{2,1,0:T(8,128)(2,1)S(1)}, s16[8,16,512]{2,1,0:T(8,128)(2,1)S(1)}, u32[]{:S(2)}, u32[]{:S(2)}) %collective-permute-start.4) | collective-permute-done | bytes 131104 | tf_op jit(solution)/shard_map/ppermute | solution.py:531
  44.9 0.1 join.1
  45.0 10.9 %all_to_all.16.parts = s16[8,16,512]{2,1,0:T(8,128)(2,1)S(1)} all-to-all(s16[8,16,512]{2,1,0:T(8,128)(2,1)S(1)} %join.1), channel_id=1, replica_groups=mesh['ref_0'=8,'ref_1'=4,'ref_2'=2,'voc'=4] {'ref_0'}, dimensions={0} | all-to-all | bytes 262144 | tf_op jit(solution)/shard_map/all_to_all | solution.py:596
  55.9 0.1 finish.1
  56.0 0.1 broadcast_in_dim.3
  56.1 21.1 %all_to_all.17 = f32[256,1,128]{2,1,0:T(1,128)S(1)} all-to-all(f32[256,1,128]{2,1,0:T(1,128)S(1)} %broadcast_in_dim.3), channel_id=1, replica_groups=mesh['ref_0'=8,'ref_1'=4,'ref_2'=2,'voc'=4] {'ref_0','ref_1','ref_2','voc'}, dimensions={0} | all-to-all | bytes 262144 | tf_op jit(solution)/shard_map/all_to_all | solution.py:608
  77.1 0.9 %last.1 = (f32[4,4,501]{2,1,0:T(4,128)}, f32[4,4]{1,0:T(4,128)}) custom-call(f32[256,128]{1,0:T(8,128)S(1)} %bitcast.3, f32[16,512]{1,0:T(8,128)S(1)} %get-tuple-element.41.combined), custom_call_target="tpu_custom_call" | custom-call | tf_op jit(solution)/shard_map/last/pallas_call | solution.py:611
Async XLA Ops:
  0.6 4.2 %collective-permute-start = (s32[12]{0:T(128)}, s32[12]{0:T(128)S(1)}, u32[]{:S(2)}, u32[]{:S(2)}) collective-permute-start(s32[12]{0:T(128)} %owner_there.1), channel_id=1, source_target_pairs={{0,4},{4,0},{1,5},{5,1},{2,6},{6,2},{3,7},{7,3},{8,12},{12,8},{9,1... | collective-permute-start | bytes 152 | tf_op jit(solution)/shard_map/ppermute | solution.py:500
  4.9 26.3 %collective-permute-start.1 = (bf16[12,4,32064]{2,1,0:T(4,128)(2,1)}, bf16[12,4,32064]{2,1,0:T(4,128)(2,1)S(1)}, u32[]{:S(2)}, u32[]{:S(2)}) collective-permute-start(bf16[12,4,32064]{2,1,0:T(4,128)(2,1)} %priv.3), channel_id=1, source_target_pairs={{0,4},{4,0},{1,5},{5,1},{2,6},{6,2},{3,7},{7,3},{8,12},{12,8},{9,1... | collective-permute-start | bytes 9234440 | tf_op jit(solution)/shard_map/ppermute | solution.py:511
  31.2 2.1 %copy-start = (bf16[12,4,32064]{2,1,0:T(4,128)(2,1)S(1)}, bf16[12,4,32064]{2,1,0:T(4,128)(2,1)}, u32[]{:S(2)}) copy-start(bf16[12,4,32064]{2,1,0:T(4,128)(2,1)} %priv.3) | copy-start | bytes 9234436
  35.0 5.4 %collective-permute-start.2 = (s16[8,16,512]{2,1,0:T(8,128)(2,1)S(1)}, s16[8,16,512]{2,1,0:T(8,128)(2,1)S(1)}, u32[]{:S(2)}, u32[]{:S(2)}) collective-permute-start(s16[8,16,512]{2,1,0:T(8,128)(2,1)S(1)} %get-tuple-element.33), channel_id=1, source_target_pairs={{0,16},{8,24},{16,0},{24,8},{1,17},{9,25},{17,1},{25,9},{2,18},{10... | collective-permute-start | bytes 393224 | tf_op jit(solution)/shard_map/ppermute | solution.py:531
  37.3 5.5 %collective-permute-start.3 = (s16[8,16,512]{2,1,0:T(8,128)(2,1)S(1)}, s16[8,16,512]{2,1,0:T(8,128)(2,1)S(1)}, u32[]{:S(2)}, u32[]{:S(2)}) collective-permute-start(s16[8,16,512]{2,1,0:T(8,128)(2,1)S(1)} %get-tuple-element.34), channel_id=1, source_target_pairs={{0,8},{8,0},{16,24},{24,16},{1,9},{9,1},{17,25},{25,17},{2,10},{10... | collective-permute-start | bytes 393224 | tf_op jit(solution)/shard_map/ppermute | solution.py:531
  38.0 6.9 %collective-permute-start.4 = (s16[8,16,512]{2,1,0:T(8,128)(2,1)S(1)}, s16[8,16,512]{2,1,0:T(8,128)(2,1)S(1)}, u32[]{:S(2)}, u32[]{:S(2)}) collective-permute-start(s16[8,16,512]{2,1,0:T(8,128)(2,1)S(1)} %get-tuple-element.35), channel_id=1, source_target_pairs={{0,24},{8,16},{16,8},{24,0},{1,25},{9,17},{17,9},{25,1},{2,26},{10... | collective-permute-start | bytes 393224 | tf_op jit(solution)/shard_map/ppermute | solution.py:531

commit v13 on v11

--- a/solution.py
+++ b/solution.py
@@ -293,7 +293,9 @@
                 earlier = earlier + jnp.where(lane == free, tile, 0.0)
             return earlier
 
-        earlier = lax.fori_loop(0, lines, widen, jnp.zeros((flat, LANES), jnp.float32))
+        earlier = lax.fori_loop(
+            0, lines, widen, jnp.zeros((flat, LANES), jnp.float32), unroll=True
+        )
         for copy in little:
             copy.wait()
         for t in range(texts):

time: 78 us -> 78 us (level)
  no operation moved by 1% of the time
where the time goes in v13:
time: 78 us; the launch traced here: 77.6 us
  blocking collectives  59.5 us (76%)
  Pallas kernels  7.51 us (10%)
  starting transfers between devices  6.84 us (9%)
  waiting for transfers between devices  3 us (4%)
    all_to_all x1, blocking collectives, body(): own = lax.all_to_all(packed, CHIP, split_axis=0, concat_axis=0, tiled=True)  25.8 us
    all_to_all x1, blocking collectives, body(): lax.all_to_all(jnp.broadcast_to(stats, (devices, 1, LANES)), REF_VOC, spl...  22.2 us
    all_to_all x1, blocking collectives, body(): lax.all_to_all(joined, 'ref_0', split_axis=0, concat_axis=0, tiled=True)  11.5 us
    ppermute x1, starting transfers between devices, body(): partner = lax.ppermute(owner, CORE, swap)  3.29 us
    ppermute x3, starting transfers between devices, beyond(): return lax.ppermute(x, 'ref_1', [(k, k ^ m) for k in range(beside)])  3.21 us
    ppermute x3, waiting for transfers between devices, beyond(): return lax.ppermute(x, 'ref_1', [(k, k ^ m) for k in range(beside)])  2.93 us
    pallas_call x1, Pallas kernels, body(): pl.pallas_call(far_kernel(sizes, scale, piece), out_shape=(line_sums, jax...  2.13 us
    pallas_call x1, Pallas kernels, body(): pl.pallas_call(near_kernel(sizes, scale, piece), out_shape=(line_sums, li...  1.69 us
  transfers between devices with their start and end apart: 5, of which 2 were waited for; matrix products, arithmetic and copies ran while one was open for 0% of the time, Pallas kernels for 5%

profile of v13, /device:TPU:1, one launch (start us, length us, event | category | flops | bytes accessed | tf_op | source)
XLA Modules:
  0.0 77.6 jit_solution(7364191420710099609)
XLA Ops:
  0.6 3.3 %collective-permute-start = (s32[12]{0:T(128)}, s32[12]{0:T(128)S(1)}, u32[]{:S(2)}, u32[]{:S(2)}) collective-permute-start(s32[12]{0:T(128)} %owner_there.1), channel_id=1, source_target_pairs={{0,4},{4,0},{1,5},{5,1},{2,6},{6,2},{3,7},{7,3},{8,12},{12,8},{9,1... | collective-permute-start | bytes 152 | tf_op jit(solution)/shard_map/ppermute | solution.py:502
  3.9 0.9 %turn.1 = (f32[16,512]{1,0:T(8,128)S(1)}, f32[16,128]{1,0:T(8,128)S(1)}) custom-call(bf16[4,4,501]{2,1,0:T(4,128)(2,1)} %public.3, s32[12]{0:T(128)} %owner_there.1), custom_call_target="tpu_custom_call" | custom-call | tf_op jit(solution)/shard_map/turn/pallas_call | solution.py:503
  4.8 0.1 collective-permute-done.partner_there
  4.9 0.3 collective-permute-start.1
  5.2 0.2 mark.1
  5.4 25.8 %all_to_all.15.own = bf16[32,16,512]{2,1,0:T(8,128)(2,1)S(1)} all-to-all(bf16[32,16,512]{2,1,0:T(8,128)(2,1)S(1)} %mark.1), channel_id=1, replica_groups=mesh['ref_0'=8,'ref_1'=4,'ref_2'=2,'voc'=4] {'ref_0','ref_1'}, dimensions={0} | all-to-all | bytes 1048576 | tf_op jit(solution)/shard_map/all_to_all | solution.py:522
  31.2 0.0 copy-start
  31.2 0.0 collective-permute-done.1.swapped
  31.2 2.1 %far_sums.1 = (s16[8,16,512]{2,1,0:T(8,128)(2,1)S(1)}, s32[48]{0:T(128)S(1)}) custom-call(s32[12]{0:T(128)} %owner_there.1, s32[12]{0:T(128)S(1)} %collective-permute-done.partner_there, s32[4]{0:T(128)} %counts.1, bf16[12,4,32064]{2,1,0:T(4,128)(2,1)} %priv.3, bf16[12,4,32064]{2,1,0:T(4,128)(2,1)S(1)} %collective-permute-done.1.swapped, ...), custom_call_target="tpu_custom_call" | custom-call | tf_op jit(solution)/shard_map/far_sums/pallas_call | solution.py:536
  33.3 2.3 %collective-permute-start.2 = (s16[8,16,512]{2,1,0:T(8,128)(2,1)S(1)}, s16[8,16,512]{2,1,0:T(8,128)(2,1)S(1)}, u32[]{:S(2)}, u32[]{:S(2)}) collective-permute-start(s16[8,16,512]{2,1,0:T(8,128)(2,1)S(1)} %get-tuple-element.28), channel_id=1, source_target_pairs={{0,16},{8,24},{16,0},{24,8},{1,17},{9,25},{17,1},{25,9},{2,18},{10... | collective-permute-start | bytes 393224 | tf_op jit(solution)/shard_map/ppermute | solution.py:533
  35.6 0.0 copy-done
  35.6 1.7 %near_sums.1 = (s16[8,16,512]{2,1,0:T(8,128)(2,1)S(1)}, s16[8,16,512]{2,1,0:T(8,128)(2,1)S(1)}) custom-call(s32[48]{0:T(128)S(1)} %get-tuple-element.24.plan, bf16[12,4,32064]{2,1,0:T(4,128)(2,1)S(1)} %copy-done, bf16[12,4,32064]{2,1,0:T(4,128)(2,1)S(1)} %collective-permute-done.1.swapped, bf16[32,16,512]{2,1,0:T(8,128)(2,1)S(1)} %all_to_all.15.own), custom_call_target="tpu_custom_call" | custom-call | tf_op jit(solution)/shard_map/near_sums/pallas_call | solution.py:561
  37.3 1.0 %collective-permute-start.4 = (s16[8,16,512]{2,1,0:T(8,128)(2,1)S(1)}, s16[8,16,512]{2,1,0:T(8,128)(2,1)S(1)}, u32[]{:S(2)}, u32[]{:S(2)}) collective-permute-start(s16[8,16,512]{2,1,0:T(8,128)(2,1)S(1)} %get-tuple-element.29), channel_id=1, source_target_pairs={{0,24},{8,16},{16,8},{24,0},{1,25},{9,17},{17,9},{25,1},{2,26},{10... | collective-permute-start | bytes 393224 | tf_op jit(solution)/shard_map/ppermute | solution.py:533
  38.3 0.0 collective-permute-start.3
  38.3 1.5 %own_sums.1 = (s16[8,16,512]{2,1,0:T(8,128)(2,1)S(1)}, f32[16,512]{1,0:T(8,128)S(1)}, f32[16,512]{1,0:T(8,128)S(1)}, f32[16,128]{1,0:T(8,128)S(1)}, f32[16,128]{1,0:T(8,128)S(1)}) custom-call(bf16[4,4,501]{2,1,0:T(4,128)(2,1)} %public.3, bf16[4,4,501]{2,1,0:T(4,128)(2,1)} %noise.1, s32[4]{0:T(128)} %counts.1, s32[4,4]{1,0:T(4,128)} %tokens.1, ...), custom_call_target="tpu_custom_call" | custom-call | tf_op jit(solution)/shard_map/own_sums/pallas_call | solution.py:576
  39.7 0.0 collective-permute-done.2.b
  39.7 2.9 %collective-permute-done.4.d = s16[8,16,512]{2,1,0:T(8,128)(2,1)S(1)} collective-permute-done((s16[8,16,512]{2,1,0:T(8,128)(2,1)S(1)}, s16[8,16,512]{2,1,0:T(8,128)(2,1)S(1)}, u32[]{:S(2)}, u32[]{:S(2)}) %collective-permute-start.4) | collective-permute-done | bytes 131104 | tf_op jit(solution)/shard_map/ppermute | solution.py:533
  42.7 0.0 collective-permute-done.3.c
  42.7 0.1 join.1
  42.8 11.5 %all_to_all.16.parts = s16[8,16,512]{2,1,0:T(8,128)(2,1)S(1)} all-to-all(s16[8,16,512]{2,1,0:T(8,128)(2,1)S(1)} %join.1), channel_id=1, replica_groups=mesh['ref_0'=8,'ref_1'=4,'ref_2'=2,'voc'=4] {'ref_0'}, dimensions={0} | all-to-all | bytes 262144 | tf_op jit(solution)/shard_map/all_to_all | solution.py:598
  54.3 0.1 finish.1
  54.4 0.1 broadcast_in_dim.3
  54.5 22.2 %all_to_all.17 = f32[256,1,128]{2,1,0:T(1,128)S(1)} all-to-all(f32[256,1,128]{2,1,0:T(1,128)S(1)} %broadcast_in_dim.3), channel_id=1, replica_groups=mesh['ref_0'=8,'ref_1'=4,'ref_2'=2,'voc'=4] {'ref_0','ref_1','ref_2','voc'}, dimensions={0} | all-to-all | bytes 262144 | tf_op jit(solution)/shard_map/all_to_all | solution.py:610
  76.7 0.9 %last.1 = (f32[4,4,501]{2,1,0:T(4,128)}, f32[4,4]{1,0:T(4,128)}) custom-call(f32[256,128]{1,0:T(8,128)S(1)} %bitcast.3, f32[16,512]{1,0:T(8,128)S(1)} %get-tuple-element.35.combined), custom_call_target="tpu_custom_call" | custom-call | tf_op jit(solution)/shard_map/last/pallas_call | solution.py:613
Async XLA Ops:
  0.6 4.2 %collective-permute-start = (s32[12]{0:T(128)}, s32[12]{0:T(128)S(1)}, u32[]{:S(2)}, u32[]{:S(2)}) collective-permute-start(s32[12]{0:T(128)} %owner_there.1), channel_id=1, source_target_pairs={{0,4},{4,0},{1,5},{5,1},{2,6},{6,2},{3,7},{7,3},{8,12},{12,8},{9,1... | collective-permute-start | bytes 152 | tf_op jit(solution)/shard_map/ppermute | solution.py:502
  4.9 26.3 %collective-permute-start.1 = (bf16[12,4,32064]{2,1,0:T(4,128)(2,1)}, bf16[12,4,32064]{2,1,0:T(4,128)(2,1)S(1)}, u32[]{:S(2)}, u32[]{:S(2)}) collective-permute-start(bf16[12,4,32064]{2,1,0:T(4,128)(2,1)} %priv.3), channel_id=1, source_target_pairs={{0,4},{4,0},{1,5},{5,1},{2,6},{6,2},{3,7},{7,3},{8,12},{12,8},{9,1... | collective-permute-start | bytes 9234440 | tf_op jit(solution)/shard_map/ppermute | solution.py:513
  31.2 4.4 %copy-start = (bf16[12,4,32064]{2,1,0:T(4,128)(2,1)S(1)}, bf16[12,4,32064]{2,1,0:T(4,128)(2,1)}, u32[]{:S(2)}) copy-start(bf16[12,4,32064]{2,1,0:T(4,128)(2,1)} %priv.3) | copy-start | bytes 9234436
  33.3 6.4 %collective-permute-start.2 = (s16[8,16,512]{2,1,0:T(8,128)(2,1)S(1)}, s16[8,16,512]{2,1,0:T(8,128)(2,1)S(1)}, u32[]{:S(2)}, u32[]{:S(2)}) collective-permute-start(s16[8,16,512]{2,1,0:T(8,128)(2,1)S(1)} %get-tuple-element.28), channel_id=1, source_target_pairs={{0,16},{8,24},{16,0},{24,8},{1,17},{9,25},{17,1},{25,9},{2,18},{10... | collective-permute-start | bytes 393224 | tf_op jit(solution)/shard_map/ppermute | solution.py:533
  37.3 5.4 %collective-permute-start.4 = (s16[8,16,512]{2,1,0:T(8,128)(2,1)S(1)}, s16[8,16,512]{2,1,0:T(8,128)(2,1)S(1)}, u32[]{:S(2)}, u32[]{:S(2)}) collective-permute-start(s16[8,16,512]{2,1,0:T(8,128)(2,1)S(1)} %get-tuple-element.29), channel_id=1, source_target_pairs={{0,24},{8,16},{16,8},{24,0},{1,25},{9,17},{17,9},{25,1},{2,26},{10... | collective-permute-start | bytes 393224 | tf_op jit(solution)/shard_map/ppermute | solution.py:533
  38.3 4.4 %collective-permute-start.3 = (s16[8,16,512]{2,1,0:T(8,128)(2,1)S(1)}, s16[8,16,512]{2,1,0:T(8,128)(2,1)S(1)}, u32[]{:S(2)}, u32[]{:S(2)}) collective-permute-start(s16[8,16,512]{2,1,0:T(8,128)(2,1)S(1)} %get-tuple-element.25), channel_id=1, source_target_pairs={{0,8},{8,0},{16,24},{24,16},{1,9},{9,1},{17,25},{25,17},{2,10},{10... | collective-permute-start | bytes 393224 | tf_op jit(solution)/shard_map/ppermute | solution.py:533

commit v14 on v13

--- a/solution.py
+++ b/solution.py
@@ -360,7 +360,7 @@
             some(b * step)
             return carry
 
-        lax.fori_loop(0, lines // step - 1, looped, 0)
+        lax.fori_loop(0, lines // step - 1, looped, 0, unroll=True)
         some(lines - step, strip)
 
     return kernel

time: 78 us -> 77.9 us (level)
  no operation moved by 1% of the time
where the time goes in v14:
time: 77.9 us; the launch traced here: 77.5 us
  blocking collectives  59.4 us (76%)
  Pallas kernels  7.41 us (10%)
  starting transfers between devices  6.85 us (9%)
  waiting for transfers between devices  3.09 us (4%)
    all_to_all x1, blocking collectives, body(): own = lax.all_to_all(packed, CHIP, split_axis=0, concat_axis=0, tiled=True)  25.8 us
    all_to_all x1, blocking collectives, body(): lax.all_to_all(jnp.broadcast_to(stats, (devices, 1, LANES)), REF_VOC, spl...  22 us
    all_to_all x1, blocking collectives, body(): lax.all_to_all(joined, 'ref_0', split_axis=0, concat_axis=0, tiled=True)  11.6 us
    ppermute x1, starting transfers between devices, body(): partner = lax.ppermute(owner, CORE, swap)  3.29 us
    ppermute x3, starting transfers between devices, beyond(): return lax.ppermute(x, 'ref_1', [(k, k ^ m) for k in range(beside)])  3.22 us
    ppermute x3, waiting for transfers between devices, beyond(): return lax.ppermute(x, 'ref_1', [(k, k ^ m) for k in range(beside)])  3.02 us
    pallas_call x1, Pallas kernels, body(): pl.pallas_call(far_kernel(sizes, scale, piece), out_shape=(line_sums, jax...  2.13 us
    pallas_call x1, Pallas kernels, body(): pl.pallas_call(near_kernel(sizes, scale, piece), out_shape=(line_sums, li...  1.58 us
  transfers between devices with their start and end apart: 5, of which 2 were waited for; matrix products, arithmetic and copies ran while one was open for 0% of the time, Pallas kernels for 5%

profile of v14, /device:TPU:1, one launch (start us, length us, event | category | flops | bytes accessed | tf_op | source)
XLA Modules:
  0.0 77.5 jit_solution(12338441745800422765)
XLA Ops:
  0.6 3.3 %collective-permute-start = (s32[12]{0:T(128)}, s32[12]{0:T(128)S(1)}, u32[]{:S(2)}, u32[]{:S(2)}) collective-permute-start(s32[12]{0:T(128)} %owner_there.1), channel_id=1, source_target_pairs={{0,4},{4,0},{1,5},{5,1},{2,6},{6,2},{3,7},{7,3},{8,12},{12,8},{9,1... | collective-permute-start | bytes 152 | tf_op jit(solution)/shard_map/ppermute | solution.py:502
  3.9 0.9 %turn.1 = (f32[16,512]{1,0:T(8,128)S(1)}, f32[16,128]{1,0:T(8,128)S(1)}) custom-call(bf16[4,4,501]{2,1,0:T(4,128)(2,1)} %public.3, s32[12]{0:T(128)} %owner_there.1), custom_call_target="tpu_custom_call" | custom-call | tf_op jit(solution)/shard_map/turn/pallas_call | solution.py:503
  4.8 0.1 collective-permute-done.partner_there
  4.9 0.3 collective-permute-start.1
  5.2 0.2 mark.1
  5.4 25.8 %all_to_all.15.own = bf16[32,16,512]{2,1,0:T(8,128)(2,1)S(1)} all-to-all(bf16[32,16,512]{2,1,0:T(8,128)(2,1)S(1)} %mark.1), channel_id=1, replica_groups=mesh['ref_0'=8,'ref_1'=4,'ref_2'=2,'voc'=4] {'ref_0','ref_1'}, dimensions={0} | all-to-all | bytes 1048576 | tf_op jit(solution)/shard_map/all_to_all | solution.py:522
  31.2 0.0 copy-start
  31.2 0.0 collective-permute-done.1.swapped
  31.2 2.1 %far_sums.1 = (s16[8,16,512]{2,1,0:T(8,128)(2,1)S(1)}, s32[48]{0:T(128)S(1)}) custom-call(s32[12]{0:T(128)} %owner_there.1, s32[12]{0:T(128)S(1)} %collective-permute-done.partner_there, s32[4]{0:T(128)} %counts.1, bf16[12,4,32064]{2,1,0:T(4,128)(2,1)} %priv.3, bf16[12,4,32064]{2,1,0:T(4,128)(2,1)S(1)} %collective-permute-done.1.swapped, ...), custom_call_target="tpu_custom_call" | custom-call | tf_op jit(solution)/shard_map/far_sums/pallas_call | solution.py:536
  33.3 2.3 %collective-permute-start.2 = (s16[8,16,512]{2,1,0:T(8,128)(2,1)S(1)}, s16[8,16,512]{2,1,0:T(8,128)(2,1)S(1)}, u32[]{:S(2)}, u32[]{:S(2)}) collective-permute-start(s16[8,16,512]{2,1,0:T(8,128)(2,1)S(1)} %get-tuple-element.28), channel_id=1, source_target_pairs={{0,16},{8,24},{16,0},{24,8},{1,17},{9,25},{17,1},{25,9},{2,18},{10... | collective-permute-start | bytes 393224 | tf_op jit(solution)/shard_map/ppermute | solution.py:533
  35.6 0.0 copy-done
  35.6 1.6 %near_sums.1 = (s16[8,16,512]{2,1,0:T(8,128)(2,1)S(1)}, s16[8,16,512]{2,1,0:T(8,128)(2,1)S(1)}) custom-call(s32[48]{0:T(128)S(1)} %get-tuple-element.24.plan, bf16[12,4,32064]{2,1,0:T(4,128)(2,1)S(1)} %copy-done, bf16[12,4,32064]{2,1,0:T(4,128)(2,1)S(1)} %collective-permute-done.1.swapped, bf16[32,16,512]{2,1,0:T(8,128)(2,1)S(1)} %all_to_all.15.own), custom_call_target="tpu_custom_call" | custom-call | tf_op jit(solution)/shard_map/near_sums/pallas_call | solution.py:561
  37.2 1.0 %collective-permute-start.4 = (s16[8,16,512]{2,1,0:T(8,128)(2,1)S(1)}, s16[8,16,512]{2,1,0:T(8,128)(2,1)S(1)}, u32[]{:S(2)}, u32[]{:S(2)}) collective-permute-start(s16[8,16,512]{2,1,0:T(8,128)(2,1)S(1)} %get-tuple-element.29), channel_id=1, source_target_pairs={{0,24},{8,16},{16,8},{24,0},{1,25},{9,17},{17,9},{25,1},{2,26},{10... | collective-permute-start | bytes 393224 | tf_op jit(solution)/shard_map/ppermute | solution.py:533
  38.2 0.0 collective-permute-start.3
  38.2 1.5 %own_sums.1 = (s16[8,16,512]{2,1,0:T(8,128)(2,1)S(1)}, f32[16,512]{1,0:T(8,128)S(1)}, f32[16,512]{1,0:T(8,128)S(1)}, f32[16,128]{1,0:T(8,128)S(1)}, f32[16,128]{1,0:T(8,128)S(1)}) custom-call(bf16[4,4,501]{2,1,0:T(4,128)(2,1)} %public.3, bf16[4,4,501]{2,1,0:T(4,128)(2,1)} %noise.1, s32[4]{0:T(128)} %counts.1, s32[4,4]{1,0:T(4,128)} %tokens.1, ...), custom_call_target="tpu_custom_call" | custom-call | tf_op jit(solution)/shard_map/own_sums/pallas_call | solution.py:576
  39.6 0.0 collective-permute-done.2.b
  39.7 3.0 %collective-permute-done.4.d = s16[8,16,512]{2,1,0:T(8,128)(2,1)S(1)} collective-permute-done((s16[8,16,512]{2,1,0:T(8,128)(2,1)S(1)}, s16[8,16,512]{2,1,0:T(8,128)(2,1)S(1)}, u32[]{:S(2)}, u32[]{:S(2)}) %collective-permute-start.4) | collective-permute-done | bytes 131104 | tf_op jit(solution)/shard_map/ppermute | solution.py:533
  42.7 0.0 collective-permute-done.3.c
  42.7 0.1 join.1
  42.8 11.6 %all_to_all.16.parts = s16[8,16,512]{2,1,0:T(8,128)(2,1)S(1)} all-to-all(s16[8,16,512]{2,1,0:T(8,128)(2,1)S(1)} %join.1), channel_id=1, replica_groups=mesh['ref_0'=8,'ref_1'=4,'ref_2'=2,'voc'=4] {'ref_0'}, dimensions={0} | all-to-all | bytes 262144 | tf_op jit(solution)/shard_map/all_to_all | solution.py:598
  54.4 0.1 finish.1
  54.5 0.1 broadcast_in_dim.3
  54.6 22.0 %all_to_all.17 = f32[256,1,128]{2,1,0:T(1,128)S(1)} all-to-all(f32[256,1,128]{2,1,0:T(1,128)S(1)} %broadcast_in_dim.3), channel_id=1, replica_groups=mesh['ref_0'=8,'ref_1'=4,'ref_2'=2,'voc'=4] {'ref_0','ref_1','ref_2','voc'}, dimensions={0} | all-to-all | bytes 262144 | tf_op jit(solution)/shard_map/all_to_all | solution.py:610
  76.6 0.9 %last.1 = (f32[4,4,501]{2,1,0:T(4,128)}, f32[4,4]{1,0:T(4,128)}) custom-call(f32[256,128]{1,0:T(8,128)S(1)} %bitcast.3, f32[16,512]{1,0:T(8,128)S(1)} %get-tuple-element.35.combined), custom_call_target="tpu_custom_call" | custom-call | tf_op jit(solution)/shard_map/last/pallas_call | solution.py:613
Async XLA Ops:
  0.6 4.2 %collective-permute-start = (s32[12]{0:T(128)}, s32[12]{0:T(128)S(1)}, u32[]{:S(2)}, u32[]{:S(2)}) collective-permute-start(s32[12]{0:T(128)} %owner_there.1), channel_id=1, source_target_pairs={{0,4},{4,0},{1,5},{5,1},{2,6},{6,2},{3,7},{7,3},{8,12},{12,8},{9,1... | collective-permute-start | bytes 152 | tf_op jit(solution)/shard_map/ppermute | solution.py:502
  4.9 26.3 %collective-permute-start.1 = (bf16[12,4,32064]{2,1,0:T(4,128)(2,1)}, bf16[12,4,32064]{2,1,0:T(4,128)(2,1)S(1)}, u32[]{:S(2)}, u32[]{:S(2)}) collective-permute-start(bf16[12,4,32064]{2,1,0:T(4,128)(2,1)} %priv.3), channel_id=1, source_target_pairs={{0,4},{4,0},{1,5},{5,1},{2,6},{6,2},{3,7},{7,3},{8,12},{12,8},{9,1... | collective-permute-start | bytes 9234440 | tf_op jit(solution)/shard_map/ppermute | solution.py:513
  31.2 4.4 %copy-start = (bf16[12,4,32064]{2,1,0:T(4,128)(2,1)S(1)}, bf16[12,4,32064]{2,1,0:T(4,128)(2,1)}, u32[]{:S(2)}) copy-start(bf16[12,4,32064]{2,1,0:T(4,128)(2,1)} %priv.3) | copy-start | bytes 9234436
  33.3 6.3 %collective-permute-start.2 = (s16[8,16,512]{2,1,0:T(8,128)(2,1)S(1)}, s16[8,16,512]{2,1,0:T(8,128)(2,1)S(1)}, u32[]{:S(2)}, u32[]{:S(2)}) collective-permute-start(s16[8,16,512]{2,1,0:T(8,128)(2,1)S(1)} %get-tuple-element.28), channel_id=1, source_target_pairs={{0,16},{8,24},{16,0},{24,8},{1,17},{9,25},{17,1},{25,9},{2,18},{10... | collective-permute-start | bytes 393224 | tf_op jit(solution)/shard_map/ppermute | solution.py:533
  37.2 5.5 %collective-permute-start.4 = (s16[8,16,512]{2,1,0:T(8,128)(2,1)S(1)}, s16[8,16,512]{2,1,0:T(8,128)(2,1)S(1)}, u32[]{:S(2)}, u32[]{:S(2)}) collective-permute-start(s16[8,16,512]{2,1,0:T(8,128)(2,1)S(1)} %get-tuple-element.29), channel_id=1, source_target_pairs={{0,24},{8,16},{16,8},{24,0},{1,25},{9,17},{17,9},{25,1},{2,26},{10... | collective-permute-start | bytes 393224 | tf_op jit(solution)/shard_map/ppermute | solution.py:533
  38.2 4.5 %collective-permute-start.3 = (s16[8,16,512]{2,1,0:T(8,128)(2,1)S(1)}, s16[8,16,512]{2,1,0:T(8,128)(2,1)S(1)}, u32[]{:S(2)}, u32[]{:S(2)}) collective-permute-start(s16[8,16,512]{2,1,0:T(8,128)(2,1)S(1)} %get-tuple-element.25), channel_id=1, source_target_pairs={{0,8},{8,0},{16,24},{24,16},{1,9},{9,1},{17,25},{25,17},{2,10},{10... | collective-permute-start | bytes 393224 | tf_op jit(solution)/shard_map/ppermute | solution.py:533
